TPU v7x, 32 devices: a whole 2x2x4 slice. The times are simulated.
32 devices in a mesh: seq: 4 (over y, core), fsdp: 8 (over z, x).
Axes of the slice: x: 2, y: 2, z: 4, core: 2. Of those that a mesh axis runs over, the one named last changes fastest.
Arguments:
- tokens: bfloat16 [16384, 1024], P(('seq', 'fsdp')), may hold values from -6 to 6
- norm_gain: float32 [1024], replicated, may hold values from 0.5 to 1.5
- w_query: bfloat16 [1024, 1024], P('fsdp'), may hold values from -0.1875 to 0.1875
- w_key: bfloat16 [1024, 1024], P('fsdp'), may hold values from -0.1875 to 0.1875
- w_value: bfloat16 [1024, 1024], P('fsdp'), may hold values from -0.1875 to 0.1875
- w_beta: bfloat16 [1024, 8], P('fsdp'), may hold values from -0.1875 to 0.1875
- conv_taps: float32 [3, 4, 1024], replicated, may hold values from -3 to 3
- head_gain: float32 [128], replicated, may hold values from 0.5 to 1.5
- w_out: bfloat16 [1024, 1024], P('fsdp'), may hold values from -0.1875 to 0.1875
- ffn_gain: float32 [1024], replicated, may hold values from 0.5 to 1.5
- w_gate: bfloat16 [1024, 2816], P('fsdp'), may hold values from -0.1875 to 0.1875
- w_up: bfloat16 [1024, 2816], P('fsdp'), may hold values from -0.1875 to 0.1875
- w_down: bfloat16 [2816, 1024], P('fsdp'), may hold values from -0.109375 to 0.109375
- cotangent: bfloat16 [16384, 1024], P(('seq', 'fsdp')), may hold values from -6 to 6
- token_order: int32 [8, 2048], P('fsdp'), may hold values from 0 to 2047, each once within a row
- seq_lengths: int32 [8, 4], P('fsdp'), may hold values from 64 to 1024, as said below
Outputs:
- result: bfloat16 [16384, 1024], P(('seq', 'fsdp'))
- grad_tokens: float32 [16384, 1024], P(('seq', 'fsdp'))
- grad_norm_gain: float32 [1024], replicated
- grad_w_query: float32 [1024, 1024], P('fsdp')
- grad_w_key: float32 [1024, 1024], P('fsdp')
- grad_w_value: float32 [1024, 1024], P('fsdp')
- grad_w_beta: float32 [1024, 8], P('fsdp')
- grad_conv_taps: float32 [3, 4, 1024], replicated
- grad_head_gain: float32 [128], replicated
- grad_w_out: float32 [1024, 1024], P('fsdp')
- grad_ffn_gain: float32 [1024], replicated
- grad_w_gate: float32 [1024, 2816], P('fsdp')
- grad_w_up: float32 [1024, 2816], P('fsdp')
- grad_w_down: float32 [2816, 1024], P('fsdp')
Inputs may be any that keep to these rules, and one draw needn't show every extreme that they name: `seq_lengths`: each row gives the lengths of a group's 4 sequences in packed order: multiples of 64 that sum to 2048, the longest exactly half of 2048. `token_order`: each row is a permutation of the arrival indices of one group.
All inputs are finite; a program needn't handle non-finite values.
Results may differ from a plain program's by a relative error of at most 0.02.
Values may be sent and summed in bfloat16 or wider, within the bound.
A program may use at most 256 MiB of HBM per device.

v0:
```python
import jax
import jax.numpy as jnp
from jax import lax
from jax.sharding import PartitionSpec as P

DK = 128
CONV = 4
CH = 64


EPS_NORM = 1e-06
PRECISION_LEVEL = lax.Precision.HIGHEST


def matmul(first_op, second_op):
    return jnp.dot(first_op, second_op, preferred_element_type=jnp.float32)


def times_transposed(first_op, second_op):
    return lax.dot_general(
        first_op, second_op, (((1,), (1,)), ((), ())), preferred_element_type=jnp.float32
    )


def contract_rows(first_op, second_op):
    return lax.dot_general(
        first_op, second_op, (((0,), (0,)), ((), ())), preferred_element_type=jnp.float32
    )


def rounded_keep(values):
    rounded = lax.optimization_barrier(values.astype(jnp.bfloat16)).astype(jnp.float32)
    return values + lax.stop_gradient(rounded - values)


def rms_forward(values, gain):
    inv_rms = lax.rsqrt(jnp.mean(values * values, axis=-1, keepdims=True) + EPS_NORM)
    unit_rows = values * inv_rms
    return (unit_rows * gain, unit_rows, inv_rms)


def rms_backward(grad_out, unit_rows, inv_rms, gain):
    grad_gain = jnp.sum(grad_out * unit_rows, axis=0)
    grad_unit = grad_out * gain
    grad_in = inv_rms * (
        grad_unit - unit_rows * jnp.mean(grad_unit * unit_rows, axis=-1, keepdims=True)
    )
    return (grad_in, grad_gain)


def layout_masks(lengths, group_rows):
    starts = jnp.cumsum(lengths) - lengths
    places = jnp.arange(group_rows, dtype=jnp.int32)
    valid_taps = [jnp.ones((group_rows,), jnp.float32)]
    for offset in range(1, CONV):
        inside = (starts[None, :] > places[:, None] - offset) & (starts[None, :] <= places[:, None])
        valid_taps.append(1.0 - jnp.any(inside, axis=1).astype(jnp.float32))
    span_first = jnp.arange(group_rows // CH, dtype=jnp.int32) * CH
    retain = 1.0 - jnp.any(starts[None, :] == span_first[:, None], axis=1).astype(jnp.float32)
    return (valid_taps, retain)


def short_conv(signal, tap_weights, valid_taps):
    summed = signal * tap_weights[0]
    for offset in range(1, CONV):
        shifted = jnp.concatenate(
            [jnp.zeros((offset, signal.shape[1]), jnp.float32), signal[:-offset]], axis=0
        )
        summed = summed + shifted * valid_taps[offset][:, None] * tap_weights[offset]
    return summed


def span_step(carried_state, inputs):
    query_block, input_keys, values, strength, retain = inputs
    carried_state = carried_state * retain
    identity = jnp.eye(CH, dtype=jnp.float32)
    lower_mask = jnp.tril(jnp.ones((CH, CH), jnp.float32), -1)
    incl_mask = jnp.tril(jnp.ones((CH, CH), jnp.float32))
    key_inner = jnp.einsum(
        "hik,hjk->hij", input_keys, input_keys, preferred_element_type=jnp.float32
    )
    strict = strength[:, :, None] * key_inner * lower_mask
    inverse_t = identity - strict
    power_a = strict
    for level_idx in range(1, CH.bit_length() - 1):
        power_a = jnp.einsum("hij,hjk->hik", power_a, power_a, precision=PRECISION_LEVEL)
        inverse_t = jnp.einsum(
            "hij,hjk->hik", inverse_t, identity + power_a, precision=PRECISION_LEVEL
        )
    weighted_keys = jnp.einsum(
        "hij,hjk->hik", inverse_t, strength[:, :, None] * input_keys, precision=PRECISION_LEVEL
    )
    weighted_values = jnp.einsum(
        "hij,hjk->hik", inverse_t, strength[:, :, None] * values, precision=PRECISION_LEVEL
    )
    fresh_update = weighted_values - jnp.einsum(
        "jto,joa->jta", weighted_keys, carried_state, precision=PRECISION_LEVEL
    )
    scores = (
        jnp.einsum("hik,hjk->hij", query_block, input_keys, preferred_element_type=jnp.float32)
        * incl_mask
    )
    block_output = jnp.einsum("jto,joa->jta", query_block, carried_state, precision=PRECISION_LEVEL)
    block_output = block_output + jnp.einsum(
        "hij,hjv->hiv", scores, fresh_update, precision=PRECISION_LEVEL
    )
    carried_state = carried_state + jnp.einsum(
        "zgb,zga->zba", input_keys, fresh_update, precision=PRECISION_LEVEL
    )
    return (carried_state, block_output)


def delta_rule(query_h, key_h, value_h, strength, retain):
    group_rows, head_count = (query_h.shape[0], query_h.shape[1])
    blocks = group_rows // CH

    def to_blocks(array):
        return array.reshape(blocks, CH, head_count, -1).transpose(0, 2, 1, 3)

    strength_b = strength.reshape(blocks, CH, head_count).transpose(0, 2, 1)
    initial = jnp.zeros((head_count, DK, DK), jnp.float32)
    last_state, block_outs = lax.scan(
        jax.checkpoint(span_step),
        initial,
        (to_blocks(query_h), to_blocks(key_h), to_blocks(value_h), strength_b, retain),
    )
    return block_outs.transpose(0, 2, 1, 3).reshape(group_rows, head_count, DK)


def mixer(query_in, key_in, value_in, beta_in, conv_in, gain_in, lengths):
    group_rows, head_count = (beta_in.shape[0], beta_in.shape[1])
    valid_taps, retain = layout_masks(lengths, group_rows)

    def activate(signal, tap_weights):
        return jax.nn.silu(short_conv(signal, tap_weights, valid_taps)).reshape(
            group_rows, head_count, DK
        )

    query_h = activate(query_in, conv_in[0])
    key_h = activate(key_in, conv_in[1])
    value_h = activate(value_in, conv_in[2])
    query_h = rounded_keep(
        query_h
        * lax.rsqrt(jnp.sum(query_h * query_h, axis=-1, keepdims=True) + EPS_NORM)
        * DK ** (-0.5)
    )
    key_h = rounded_keep(
        key_h * lax.rsqrt(jnp.sum(key_h * key_h, axis=-1, keepdims=True) + EPS_NORM)
    )
    strength = jax.nn.sigmoid(beta_in)
    block_output = delta_rule(query_h, key_h, value_h, strength, retain)
    block_output = (
        block_output
        * lax.rsqrt(jnp.mean(block_output * block_output, axis=-1, keepdims=True) + EPS_NORM)
        * gain_in
    )
    return block_output.reshape(group_rows, head_count * DK)


def split_columns(array, widths, pieces):
    row_count = array.shape[0]
    blocked = array.reshape(row_count, pieces, -1)
    outputs = []
    begin = 0
    for width in widths:
        outputs.append(blocked[:, :, begin : begin + width].reshape(row_count, pieces * width))
        begin = begin + width
    return outputs


def local(
    tokens,
    norm_gain,
    w_query,
    w_key,
    w_value,
    w_beta,
    conv_taps,
    head_gain,
    w_out,
    ffn_gain,
    w_gate,
    w_up,
    w_down,
    cotangent,
    token_order,
    seq_lengths,
):
    inputs = tokens.astype(jnp.float32)
    normed_f, unit_one, inv_one = rms_forward(inputs, norm_gain)
    normed = normed_f.astype(jnp.bfloat16)
    full_q, full_k, full_v, full_b, full_o = (
        lax.all_gather(w_query, "fsdp", axis=0, tiled=True),
        lax.all_gather(w_key, "fsdp", axis=0, tiled=True),
        lax.all_gather(w_value, "fsdp", axis=0, tiled=True),
        lax.all_gather(w_beta, "fsdp", axis=0, tiled=True),
        lax.all_gather(w_out, "fsdp", axis=0, tiled=True),
    )
    proj_q = matmul(normed, full_q).astype(jnp.bfloat16)
    proj_k = matmul(normed, full_k).astype(jnp.bfloat16)
    proj_v = matmul(normed, full_v).astype(jnp.bfloat16)
    proj_b = matmul(normed, full_b).astype(jnp.bfloat16)
    heads_q, heads_k, heads_v, heads_b = (
        lax.all_to_all(proj_q, "seq", split_axis=1, concat_axis=0, tiled=True),
        lax.all_to_all(proj_k, "seq", split_axis=1, concat_axis=0, tiled=True),
        lax.all_to_all(proj_v, "seq", split_axis=1, concat_axis=0, tiled=True),
        lax.all_to_all(proj_b, "seq", split_axis=1, concat_axis=0, tiled=True),
    )
    packing = token_order[0]
    lengths = seq_lengths[0]
    group_rows = packing.shape[0]
    inverse = (
        jnp.zeros((group_rows,), jnp.int32).at[packing].set(jnp.arange(group_rows, dtype=jnp.int32))
    )
    width_dev = heads_q.shape[1]
    first_channel = lax.axis_index("seq") * width_dev
    conv_part = lax.dynamic_slice_in_dim(conv_taps, first_channel, width_dev, 2)

    def local_mixer(query_in, key_in, value_in, beta_in, conv_in, gain_in):
        mixed_packed = mixer(
            query_in[packing],
            key_in[packing],
            value_in[packing],
            beta_in[packing],
            conv_in,
            gain_in,
            lengths,
        )
        return mixed_packed[inverse]

    mixed_out, pullback = jax.vjp(
        local_mixer,
        heads_q.astype(jnp.float32),
        heads_k.astype(jnp.float32),
        heads_v.astype(jnp.float32),
        heads_b.astype(jnp.float32),
        conv_part,
        head_gain,
    )
    mixed_tok = lax.all_to_all(
        mixed_out.astype(jnp.bfloat16), "seq", split_axis=0, concat_axis=1, tiled=True
    )
    hidden = inputs + matmul(mixed_tok, full_o)
    second_f, unit_two, inv_two = rms_forward(hidden, ffn_gain)
    second = second_f.astype(jnp.bfloat16)
    full_gate, full_up, full_down = (
        lax.all_gather(w_gate, "fsdp", axis=0, tiled=True),
        lax.all_gather(w_up, "fsdp", axis=0, tiled=True),
        lax.all_gather(w_down, "fsdp", axis=0, tiled=True),
    )
    gate_lin = matmul(second, full_gate)
    upward = matmul(second, full_up)
    sigmoid_gate = jax.nn.sigmoid(gate_lin)
    active = (gate_lin * sigmoid_gate * upward).astype(jnp.bfloat16)
    result = (hidden + matmul(active, full_down)).astype(jnp.bfloat16)
    back_q, back_k, back_v, back_b, back_o, back_gate, back_up, back_down = (
        lax.all_gather(w_query, "fsdp", axis=0, tiled=True),
        lax.all_gather(w_key, "fsdp", axis=0, tiled=True),
        lax.all_gather(w_value, "fsdp", axis=0, tiled=True),
        lax.all_gather(w_beta, "fsdp", axis=0, tiled=True),
        lax.all_gather(w_out, "fsdp", axis=0, tiled=True),
        lax.all_gather(w_gate, "fsdp", axis=0, tiled=True),
        lax.all_gather(w_up, "fsdp", axis=0, tiled=True),
        lax.all_gather(w_down, "fsdp", axis=0, tiled=True),
    )
    grad_active = times_transposed(cotangent, back_down)
    grad_gate = (
        grad_active * upward * sigmoid_gate * (1.0 + gate_lin * (1.0 - sigmoid_gate))
    ).astype(jnp.bfloat16)
    grad_upward = (grad_active * gate_lin * sigmoid_gate).astype(jnp.bfloat16)
    grad_second = times_transposed(grad_gate, back_gate) + times_transposed(grad_upward, back_up)
    grad_hidden, grad_ffn_gain = rms_backward(grad_second, unit_two, inv_two, ffn_gain)
    grad_hidden = grad_hidden + cotangent.astype(jnp.float32)
    grad_attn = grad_hidden.astype(jnp.bfloat16)
    grad_mixed = times_transposed(grad_attn, back_o).astype(jnp.bfloat16)
    grad_heads = lax.all_to_all(grad_mixed, "seq", split_axis=1, concat_axis=0, tiled=True)
    grad_hq, grad_hk, grad_hv, grad_hb, grad_conv, grad_head_gain = pullback(
        grad_heads.astype(jnp.float32)
    )
    low_hq = grad_hq.astype(jnp.bfloat16)
    low_hk = grad_hk.astype(jnp.bfloat16)
    low_hv = grad_hv.astype(jnp.bfloat16)
    low_hb = grad_hb.astype(jnp.bfloat16)
    tok_q, tok_k, tok_v, tok_b = (
        lax.all_to_all(low_hq, "seq", split_axis=0, concat_axis=1, tiled=True),
        lax.all_to_all(low_hk, "seq", split_axis=0, concat_axis=1, tiled=True),
        lax.all_to_all(low_hv, "seq", split_axis=0, concat_axis=1, tiled=True),
        lax.all_to_all(low_hb, "seq", split_axis=0, concat_axis=1, tiled=True),
    )
    grad_normed = (
        times_transposed(tok_q, back_q)
        + times_transposed(tok_k, back_k)
        + times_transposed(tok_v, back_v)
        + times_transposed(tok_b, back_b)
    )
    pieces = 1
    rows_norm, rows_mixed, rows_second, rows_active = (normed, mixed_tok, second, active)
    proj_wide = jnp.concatenate([tok_q, tok_k, tok_v, tok_b], axis=1)
    gate_up_wide = jnp.concatenate([grad_gate, grad_upward], axis=1)
    wide_part = lax.psum_scatter(
        jnp.concatenate(
            [
                contract_rows(rows_norm, proj_wide),
                contract_rows(rows_mixed, grad_attn),
                contract_rows(rows_second, gate_up_wide),
            ],
            axis=1,
        ).astype(jnp.bfloat16),
        "fsdp",
        scatter_dimension=0,
        tiled=True,
    )
    down_part = lax.psum_scatter(
        contract_rows(rows_active, cotangent).astype(jnp.bfloat16),
        "fsdp",
        scatter_dimension=0,
        tiled=True,
    )
    grad_inputs, grad_norm_gain = rms_backward(grad_normed, unit_one, inv_one, norm_gain)
    grad_inputs = grad_inputs + grad_hidden
    conv_full = lax.dynamic_update_slice_in_dim(
        jnp.zeros_like(conv_taps), grad_conv, first_channel, 2
    )
    wide_sum, down_sum = (
        lax.psum(wide_part, "seq").astype(jnp.float32),
        lax.psum(down_part, "seq").astype(jnp.float32),
    )
    norm_total, ffn_total, head_total, conv_total = lax.psum(
        (grad_norm_gain, grad_ffn_gain, grad_head_gain, conv_full), ("seq", "fsdp")
    )
    model_width = w_query.shape[1]
    hidden_units = w_gate.shape[1]
    head_count = w_beta.shape[1]
    widths = [
        model_width // pieces,
        model_width // pieces,
        model_width // pieces,
        head_count // pieces,
        model_width // pieces,
        hidden_units // pieces,
        hidden_units // pieces,
    ]
    sum_q, sum_k, sum_v, sum_b, sum_o, sum_gate, sum_up = split_columns(wide_sum, widths, pieces)
    return (
        result,
        grad_inputs,
        norm_total,
        sum_q,
        sum_k,
        sum_v,
        sum_b,
        conv_total,
        head_total,
        sum_o,
        ffn_total,
        sum_gate,
        sum_up,
        down_sum,
    )


def solution(mesh):
    in_specs = (
        P(("seq", "fsdp"), None),
        P(),
        P("fsdp", None),
        P("fsdp", None),
        P("fsdp", None),
        P("fsdp", None),
        P(),
        P(),
        P("fsdp", None),
        P(),
        P("fsdp", None),
        P("fsdp", None),
        P("fsdp", None),
        P(("seq", "fsdp"), None),
        P("fsdp", None),
        P("fsdp", None),
    )
    out_specs = (
        P(("seq", "fsdp"), None),
        P(("seq", "fsdp"), None),
        P(),
        P("fsdp", None),
        P("fsdp", None),
        P("fsdp", None),
        P("fsdp", None),
        P(),
        P(),
        P("fsdp", None),
        P(),
        P("fsdp", None),
        P("fsdp", None),
        P("fsdp", None),
    )
    return jax.shard_map(local, mesh=mesh, in_specs=in_specs, out_specs=out_specs, check_vma=False)
```

profile of v0, /device:TPU:0, one launch (start us, length us, event | category | flops | bytes accessed | tf_op | source)
XLA Modules:
  0.0 2473.3 jit_solution(7532236400136616017)
XLA Ops:
  11.2 28.1 %all_gather.33 = bf16[1024,8]{0,1:T(8,128)(2,1)S(1)} all-gather(bf16[128,8]{0,1:T(8,128)(2,1)S(1)} %copy-done.96), channel_id=1, replica_groups=mesh['seq'=4,'fsdp'=8] {'fsdp'}, dimensions={0}, use_global_device_ids=true | all-gather | bytes 18432 | tf_op jit(solution)/shard_map/all_gather | solution.py:196
  45.3 8.0 scatter_custom_fusion
  69.9 42.3 %all-gather.12.cloned.1.call-done = bf16[1024,1024]{1,0:T(8,128)(2,1)} async-done(((bf16[128,1024]{1,0:T(8,128)(2,1)}), bf16[1024,1024]{1,0:T(8,128)(2,1)}) %all-gather.12.cloned.1.call-update) | async-done | bytes 2097168 | tf_op jit(solution)/shard_map/all_gather | solution.py:193
  116.2 46.0 %all-gather.10.cloned.1.call-done = bf16[1024,1024]{1,0:T(8,128)(2,1)} async-done(((bf16[128,1024]{1,0:T(8,128)(2,1)}), bf16[1024,1024]{1,0:T(8,128)(2,1)}) %all-gather.10.cloned.1.call-update) | async-done | bytes 2097168 | tf_op jit(solution)/shard_map/all_gather | solution.py:195
  171.1 8.2 gather_fusion
  204.2 10.2 gather_fusion.3
  217.1 10.1 gather_fusion.2
  227.3 12.1 fusion.193
  260.4 417.4 %while.41 = (s32[]{:T(128)}, f32[2,128,128]{2,1,0:T(8,128)S(1)}, f32[32,2,64,128]{3,2,1,0:T(8,128)}, f32[32,2,128,128]{3,2,1,0:T(8,128)}, f32[32]{0:T(128)S(1)},...) while((s32[]{:T(128)}, f32[2,128,128]{2,1,0:T(8,128)S(1)}, ...), condition=%wide.region_9.10_spmd.clone.clone, body=%wide.region_8.9_spmd.clone.clone.sunk | while | flops 180781056 | bytes 2954170 | solution.py:122
  689.7 9.0 gather_fusion.4
  701.1 12.8 all-to-all-start.4
  714.0 14.4 all-to-all-done.4
  733.3 8.0 fusion.252
  741.2 7.6 fusion.253
  748.8 11.5 multiply_convert_fusion
  760.3 7.3 fusion.254
  783.0 7.9 convolution_convert_fusion.2
  795.1 13.4 scatter_custom_fusion.1
  822.9 1013.7 %while.40 = (s32[]{:T(128)}, f32[2,128,128]{2,1,0:T(8,128)}, f32[32,2,64,128]{3,2,1,0:T(8,128)}, f32[32,2,64,128]{3,2,1,0:T(8,128)}, f32[32,2,64,128]{3,2,1,0:T(...) while((s32[]{:T(128)}, f32[2,128,128]{2,1,0:T(8,128)}, ...), condition=%wide.region_20.21_spmd.clone, body=%wide.region_16.20_spmd.clone.sunk | while | flops 479051712 | bytes 10532303 | solution.py:122
  1839.5 12.2 scatter_custom_fusion.5
  1897.3 10.7 multiply_reduce_fusion.8
  1918.4 13.3 scatter_custom_fusion.4
  1939.0 13.3 scatter_custom_fusion.2
  1967.2 13.3 scatter_custom_fusion.3
  1988.8 11.7 convolution_convert_fusion
  2003.3 7.8 convolution_convert_fusion.1
  2011.0 9.3 copy.536
  2020.3 34.6 %concatenate.48 = bf16[1024,9736]{1,0:T(8,128)(2,1)} concatenate(bf16[1024,3080]{1,0:T(8,128)(2,1)} %copy.536, bf16[1024,1024]{1,0:T(8,128)(2,1)S(1)} %copy-done.32, bf16[1024,5632]{1,0:T(8,128)(2,1)} %convolution_convert_fusion), dimensions={1} | concatenate | bytes 39878656 | tf_op jit(solution)/shard_map/concatenate | solution.py:301
  2055.2 8.4 add_convert_fusion
  2069.0 316.5 %reduce-scatter.3.cloned.1.call-done = bf16[128,9736]{1,0:T(8,128)(2,1)} async-done(((bf16[1024,9736]{1,0:T(8,128)(2,1)}), bf16[128,9736]{1,0:T(8,128)(2,1)}) %reduce-scatter.3.cloned.1.call-update) | async-done | bytes 2492432 | tf_op jit(solution)/shard_map/reduce_scatter | solution.py:300
  2393.6 41.1 %all-reduce.33 = (f32[1024]{0:T(1024)}, f32[3,4,1024]{2,1,0:T(4,128)}, f32[128]{0:T(128)}, f32[1024]{0:T(1024)}) all-reduce(f32[1024]{0:T(1024)S(1)} %get-tuple-element.766, f32[3,4,1024]{2,1,0:T(4,128)S(1)} %add_dynamic-update-slice_fusion, f32[128]{0:T(128)S(1)} %bitcast_reduce_fusion, ...), channel_id=1, replica_groups=mesh['seq'=4,'fsdp'=8] {'seq','fsdp'}, use_global_device_ids=true, to_apply=%region_29.30 | all-reduce | flops 14464 | bytes 115712 | tf_op jit(solution)/shard_map/psum | solution.py:328
  2438.3 20.1 all-reduce.37.cloned.1.call-done
  (3836 shorter events, 1668.2 us)
Async XLA Ops:
  7.2 55.1 %all-gather.8.cloned.1.call-start = ((), (), s32[]{:S(2)}) async-start(), calls=%async_computation.12 | async-start | bytes 2359296 | tf_op jit(solution)/shard_map/all_gather | solution.py:194
  7.9 104.3 %all-gather.12.cloned.1.call-start = ((), (), s32[]{:S(2)}) async-start(), calls=%async_computation.14 | async-start | bytes 2359296 | tf_op jit(solution)/shard_map/all_gather | solution.py:193
  8.7 153.5 %all-gather.10.cloned.1.call-start = ((), (), s32[]{:S(2)}) async-start(), calls=%async_computation.13 | async-start | bytes 2359296 | tf_op jit(solution)/shard_map/all_gather | solution.py:195
  9.4 704.5 %all-gather.14.cloned.1.call-start = ((), (), s32[]{:S(2)}) async-start(), calls=%async_computation.15 | async-start | bytes 2359296 | tf_op jit(solution)/shard_map/all_gather | solution.py:197
  10.0 723.3 %all-gather.16.cloned.1.call-start = ((), (), s32[]{:S(2)}) async-start(), calls=%async_computation.16 | async-start | bytes 6488064 | tf_op jit(solution)/shard_map/all_gather | solution.py:247
  10.6 730.6 %all-gather.18.cloned.1.call-start = ((), (), s32[]{:S(2)}) async-start(), calls=%async_computation.17 | async-start | bytes 6488064 | tf_op jit(solution)/shard_map/all_gather | solution.py:248
  40.7 13.8 all-to-all-start.1
  44.0 704.8 %all-gather.20.cloned.1.call-start = ((), (), s32[]{:S(2)}) async-start(), calls=%async_computation.18 | async-start | bytes 6488064 | tf_op jit(solution)/shard_map/all_gather | solution.py:249
  53.4 726.9 %copy-start.51 = (f32[2048]{0:T(1024)}, f32[2048]{0:T(1024)S(1)}, u32[]{:S(2)}) copy-start(f32[2048]{0:T(1024)S(1)} %get-tuple-element.903) | copy-start | bytes 24580
  53.4 727.6 %copy-start.49 = (f32[2048]{0:T(1024)}, f32[2048]{0:T(1024)S(1)}, u32[]{:S(2)}) copy-start(f32[2048]{0:T(1024)S(1)} %get-tuple-element.902) | copy-start | bytes 24580
  54.4 124.9 %copy-start.71 = (f32[1,1,256]{2,1,0:T(1,128)}, f32[1,1,256]{2,1,0:T(1,128)S(1)}, u32[]{:S(2)}) copy-start(f32[1,1,256]{2,1,0:T(1,128)S(1)} %get-tuple-element.881) | copy-start | bytes 3076
  54.4 124.9 %copy-start.77 = (f32[1,1,256]{2,1,0:T(1,128)}, f32[1,1,256]{2,1,0:T(1,128)S(1)}, u32[]{:S(2)}) copy-start(f32[1,1,256]{2,1,0:T(1,128)S(1)} %get-tuple-element.878) | copy-start | bytes 3076
  54.5 172.8 %copy-start.73 = (f32[1,1,256]{2,1,0:T(1,128)}, f32[1,1,256]{2,1,0:T(1,128)S(1)}, u32[]{:S(2)}) copy-start(f32[1,1,256]{2,1,0:T(1,128)S(1)} %get-tuple-element.871) | copy-start | bytes 3076
  54.5 172.8 %copy-start.75 = (f32[1,1,256]{2,1,0:T(1,128)}, f32[1,1,256]{2,1,0:T(1,128)S(1)}, u32[]{:S(2)}) copy-start(f32[1,1,256]{2,1,0:T(1,128)S(1)} %get-tuple-element.874) | copy-start | bytes 3076
  54.5 172.8 %copy-start.79 = (f32[1,1,256]{2,1,0:T(1,128)}, f32[1,1,256]{2,1,0:T(1,128)S(1)}, u32[]{:S(2)}) copy-start(f32[1,1,256]{2,1,0:T(1,128)S(1)} %get-tuple-element.882) | copy-start | bytes 3076
  54.5 172.8 %copy-start.81 = (f32[1,1,256]{2,1,0:T(1,128)}, f32[1,1,256]{2,1,0:T(1,128)S(1)}, u32[]{:S(2)}) copy-start(f32[1,1,256]{2,1,0:T(1,128)S(1)} %get-tuple-element.872) | copy-start | bytes 3076
  54.5 172.8 %copy-start.83 = (f32[1,1,256]{2,1,0:T(1,128)}, f32[1,1,256]{2,1,0:T(1,128)S(1)}, u32[]{:S(2)}) copy-start(f32[1,1,256]{2,1,0:T(1,128)S(1)} %get-tuple-element.875) | copy-start | bytes 3076
  54.5 172.8 %copy-start.87 = (f32[1,1,256]{2,1,0:T(1,128)}, f32[1,1,256]{2,1,0:T(1,128)S(1)}, u32[]{:S(2)}) copy-start(f32[1,1,256]{2,1,0:T(1,128)S(1)} %get-tuple-element.873) | copy-start | bytes 3076
  54.5 172.8 %copy-start.89 = (f32[1,1,256]{2,1,0:T(1,128)}, f32[1,1,256]{2,1,0:T(1,128)S(1)}, u32[]{:S(2)}) copy-start(f32[1,1,256]{2,1,0:T(1,128)S(1)} %get-tuple-element.876) | copy-start | bytes 3076
  66.2 99.9 %all-to-all-start = ((bf16[512,4,256]{2,0,1:T(8,128)(2,1)}), bf16[512,4,256]{2,0,1:T(8,128)(2,1)S(1)}, u32[]{:S(2)}, u32[]{:S(2)}) async-start(bf16[512,4,256]{2,0,1:T(8,128)(2,1)} %bitcast.427), calls=%async_computation | async-start | bytes 2097152 | tf_op jit(solution)/shard_map/all_to_all | solution.py:205
  166.1 27.6 %all-to-all-start.3 = ((bf16[512,4,256]{2,0,1:T(8,128)(2,1)}), bf16[512,4,256]{2,0,1:T(8,128)(2,1)S(1)}, u32[]{:S(2)}, u32[]{:S(2)}) async-start(bf16[512,4,256]{2,0,1:T(8,128)(2,1)} %bitcast.425), calls=%async_computation.3 | async-start | bytes 2097152 | tf_op jit(solution)/shard_map/all_to_all | solution.py:204
  193.7 20.7 all-to-all-start.2
  701.1 27.2 %all-to-all-start.4 = ((bf16[4,512,256]{1,2,0:T(8,128)(2,1)}), bf16[4,512,256]{1,2,0:T(8,128)(2,1)}, u32[]{:S(2)}, u32[]{:S(2)}) async-start(bf16[4,512,256]{1,2,0:T(8,128)(2,1)} %copy.510), calls=%async_computation.4 | async-start | bytes 2097152 | tf_op jit(solution)/shard_map/all_to_all | solution.py:240
  775.6 18.0 all-to-all-start.5
  779.2 1289.8 %reduce-scatter.5.cloned.1.call-start = ((), (), s32[]{:S(2)}) async-start(), calls=%async_computation.20 | async-start | bytes 6488064 | tf_op jit(solution)/shard_map/reduce_scatter | solution.py:313
  1854.5 80.2 %all-to-all-start.9 = ((bf16[4,512,2]{1,2,0:T(2,128)(2,1)}), bf16[4,512,2]{1,2,0:T(2,128)(2,1)S(1)}, u32[]{:S(2)}, u32[]{:S(2)}) async-start(bf16[4,512,2]{1,2,0:T(2,128)(2,1)} %bitcast.57), calls=%async_computation.9 | async-start | bytes 16384 | tf_op jit(solution)/shard_map/all_to_all | solution.py:288
  1934.7 20.6 all-to-all-start.8
  1955.3 28.2 %all-to-all-start.6 = ((bf16[4,512,256]{1,2,0:T(8,128)(2,1)}), bf16[4,512,256]{1,2,0:T(8,128)(2,1)S(1)}, u32[]{:S(2)}, u32[]{:S(2)}) async-start(bf16[4,512,256]{1,2,0:T(8,128)(2,1)} %copy.523), calls=%async_computation.6 | async-start | bytes 2097152 | tf_op jit(solution)/shard_map/all_to_all | solution.py:285
  1984.4 18.8 all-to-all-start.7
  1988.8 396.7 %reduce-scatter.3.cloned.1.call-start = ((), (), s32[]{:S(2)}) async-start(), calls=%async_computation.19 | async-start | bytes 22708224 | tf_op jit(solution)/shard_map/reduce_scatter | solution.py:300
  2054.9 403.5 %all-reduce.37.cloned.1.call-start = ((), (), s32[]{:S(2)}) async-start(), calls=%async_computation.21 | async-start | bytes 6488064 | tf_op jit(solution)/shard_map/psum | solution.py:325
  2069.0 316.5 %copy-start.46 = (bf16[4,512,256]{1,2,0:T(8,128)(2,1)S(1)}, bf16[4,512,256]{1,2,0:T(8,128)(2,1)}, u32[]{:S(2)}) copy-start(bf16[4,512,256]{1,2,0:T(8,128)(2,1)} %copy-done.44) | copy-start | bytes 3145732
  (341 other events, 2324.9 us)
Sparse Core Ops, SparseCore 0:
  10.2 52.0 all-gather.7
  64.4 47.7 all-gather.11
  114.4 47.7 all-gather.9
  164.1 47.7 all-gather.13
  214.0 91.1 all-gather.15
  307.2 91.0 all-gather.17
  400.5 91.1 all-gather.19
  791.0 109.6 reduce-scatter.4
  2055.0 330.3 reduce-scatter.2
  2387.8 70.5 all-reduce.36
where the time goes:
time: 2510 us; the launch traced here: 2470 us
  matrix products  1240 us (49%)
  waiting for transfers between devices  451 us (18%)
  local copies, waits for them, and re-layouts  386 us (15%)
  other arithmetic  245 us (10%)
  blocking collectives  69.3 us (3%)
  starting transfers between devices  47.8 us (2%)
    reduce_scatter x1, waiting for transfers between devices, local(): lax.psum_scatter(jnp.concatenate([contract_rows(rows_norm, proj_wide), co...  317 us
    dot_general x128, matrix products, span_step(): jnp.einsum('jto,joa->jta', weighted_keys, carried_state, precision=PRECIS...  192 us
    dot_general x640, matrix products, span_step(): jnp.einsum('hij,hjk->hik', power_a, power_a, precision=PRECISION_LEVEL)  154 us
    dot_general x640, matrix products, span_step(): jnp.einsum('hij,hjk->hik', inverse_t, identity + power_a, precision=PRECI...  147 us
    dot_general x96, matrix products, span_step(): jnp.einsum('jto,joa->jta', query_block, carried_state, precision=PRECISIO...  118 us
    dot_general x96, matrix products, span_step(): jnp.einsum('zgb,zga->zba', input_keys, fresh_update, precision=PRECISION_...  99 us
    dot_general x96, matrix products, span_step(): jnp.einsum('hij,hjv->hiv', scores, fresh_update, precision=PRECISION_LEVEL)  94.6 us
    dot_general x128, matrix products, span_step(): jnp.einsum('hik,hjk->hij', query_block, input_keys, preferred_element_typ...  91.7 us
  transfers between devices with their start and end apart: 20, of which 8 were waited for; matrix products, arithmetic and copies ran while one was open for 74% of the time, Pallas kernels for 0%

commit v1 on v0

v1 whole, which is shorter than its diff:
```python
import functools

import jax
import jax.numpy as jnp
from jax import lax
from jax.experimental import pallas as pl
from jax.experimental.pallas import tpu as pltpu
from jax.sharding import PartitionSpec as P

DK = 128
CONV = 4
CH = 64
BT = 128
HALO = 16
PB = 256
EPS_NORM = 1e-06

NN = (((1,), (0,)), ((), ()))
NT = (((1,), (1,)), ((), ()))
TN = (((0,), (0,)), ((), ()))


def bdot(first, second, dims=NN):
    return lax.dot_general(
        first.astype(jnp.bfloat16),
        second.astype(jnp.bfloat16),
        dims,
        preferred_element_type=jnp.float32,
    )


def iota(shape, axis):
    return lax.broadcasted_iota(jnp.int32, shape, axis)


def sigmoid(values):
    return 1.0 / (1.0 + jnp.exp(-values))


def fill_masks(mask_ref):
    rows, cols = iota((BT, BT), 0), iota((BT, BT), 1)
    size, level = 1, 0
    while size < BT:
        inside = (rows // (2 * size) == cols // (2 * size)) & (rows // size > cols // size)
        mask_ref[level] = jnp.where(inside, 1.0, 0.0)
        size, level = 2 * size, level + 1


def unit_lower_inverses(stricts, mask_ref):
    rows, cols = iota((BT, BT), 0), iota((BT, BT), 1)
    eye = jnp.where(rows == cols, 1.0, 0.0)
    inverses = [eye - strict * mask_ref[0] for strict in stricts]
    for level in range(1, 7):
        lows = [inverse.astype(jnp.bfloat16) for inverse in inverses]
        inner = [bdot(strict * mask_ref[level], low) for strict, low in zip(stricts, lows)]
        inverses = [
            inverse - bdot(low, mid) for inverse, low, mid in zip(inverses, lows, inner)
        ]
    return inverses


def tap_masks(first, second, third, count):
    rows = iota((count, 1), 0)
    flag = jnp.where(rows < CH, first, jnp.where(rows < BT, second, third))
    return [None] + [jnp.where(rows % CH < back, flag, 1.0) for back in range(1, CONV)]


def conv_of(halo_rows, taps, masks):
    total = halo_rows[HALO:] * taps[0]
    for back in range(1, CONV):
        total = total + pltpu.roll(halo_rows, back, 0)[HALO:] * (taps[back] * masks[back])
    return total


def block_flags(first, second):
    upper = iota((BT, 1), 0) < CH
    seen = jnp.where(upper, first, first * second)
    kept = jnp.where(upper, second, 1.0)
    return seen, kept


def pair_mask(second):
    rows, cols = iota((BT, BT), 0), iota((BT, BT), 1)
    cross = (rows >= CH) & (cols < CH)
    return rows, cols, jnp.where(cross, second, 1.0)


def permute_rows(column, source, width):
    hot = jnp.where(column == iota((column.shape[0], width), 1), 1.0, 0.0).astype(jnp.bfloat16)
    return lax.dot_general(hot, source, NN, preferred_element_type=jnp.float32)


def unpermute_rows(row, base, source, width):
    hot = jnp.where(row == iota((PB, width), 0) + base, 1.0, 0.0).astype(jnp.bfloat16)
    return lax.dot_general(hot, source, NN, preferred_element_type=jnp.float32)


def mixer_forward_kernel(
    heads,
    retain_ref,
    column_ref,
    row_ref,
    proj_ref,
    taps_ref,
    gain_ref,
    mixed_ref,
    packed_ref,
    delta_ref,
    inverse_ref,
    big_ref,
    update_ref,
    state_ref,
    mask_ref,
    fresh_ref,
    own_ref,
    add_ref,
    normed_ref,
):
    tokens = proj_ref.shape[0]
    blocks = tokens // BT
    fill_masks(mask_ref)
    packed_ref[0:HALO, :] = jnp.zeros((HALO, packed_ref.shape[1]), jnp.bfloat16)

    def permute(step, carry):
        base = pl.multiple_of(step * PB, PB)
        picked = permute_rows(column_ref[pl.ds(base, PB), :], proj_ref[...], tokens)
        packed_ref[pl.ds(HALO + base, PB), :] = picked.astype(jnp.bfloat16)
        return carry

    lax.fori_loop(0, tokens // PB, permute, 0)

    unroll = 2

    def prepare(step, carry):
        places, stricts, kept_values = [], [], []
        for sub in range(unroll):
            block = step * unroll + sub
            first, second = retain_ref[2 * block], retain_ref[2 * block + 1]
            base = pl.multiple_of(block * BT, BT)
            masks = tap_masks(first, second, 1.0, BT)
            seen, kept = block_flags(first, second)
            rows, cols, cross = pair_mask(second)
            strengths = sigmoid(
                packed_ref[pl.ds(HALO + base, BT), 3 * heads * DK : 3 * heads * DK + BT].astype(
                    jnp.float32
                )
            )
            for head in range(heads):
                parts = []
                for kind in range(3):
                    at = (kind * heads + head) * DK
                    window = packed_ref[pl.ds(base, HALO + BT), at : at + DK].astype(jnp.float32)
                    taps = [
                        taps_ref[kind * CONV + back : kind * CONV + back + 1, head * DK : head * DK + DK]
                        for back in range(CONV)
                    ]
                    conv = conv_of(window, taps, masks)
                    parts.append(conv * sigmoid(conv))
                query, key, value = parts
                query = query * lax.rsqrt(
                    jnp.sum(query * query, axis=1, keepdims=True) + EPS_NORM
                ) * DK ** (-0.5)
                key = key * lax.rsqrt(jnp.sum(key * key, axis=1, keepdims=True) + EPS_NORM)
                query_low, key_low = query.astype(jnp.bfloat16), key.astype(jnp.bfloat16)
                query, key = query_low.astype(jnp.float32), key_low.astype(jnp.float32)
                beta = strengths[:, head : head + 1]
                inner = bdot(jnp.concatenate([key_low, query_low], axis=0), key_low, NT)
                stricts.append(jnp.where(rows > cols, inner[:BT] * cross * beta, 0.0))
                scores = jnp.where(rows >= cols, inner[BT:] * cross, 0.0)
                sides = jnp.concatenate([key * (beta * seen), value * beta], axis=1)
                kept_values.append((scores, sides, key * kept, query * seen))
                places.append(head * blocks + block)
        inverses = unit_lower_inverses(stricts, mask_ref)
        solved = [
            bdot(inverse, values[1]) for inverse, values in zip(inverses, kept_values)
        ]
        through = [bdot(values[0], both) for values, both in zip(kept_values, solved)]
        onward = [bdot(values[2], both, TN) for values, both in zip(kept_values, solved)]
        for index, place in enumerate(places):
            inverse_ref[place] = inverses[index].astype(jnp.bfloat16)
            big_ref[place, 0:BT, :] = onward[index][:, :DK].astype(jnp.bfloat16)
            big_ref[place, BT : 2 * BT, :] = solved[index][:, :DK].astype(jnp.bfloat16)
            big_ref[place, 2 * BT : 3 * BT, :] = (
                kept_values[index][3] - through[index][:, :DK]
            ).astype(jnp.bfloat16)
            add_ref[place] = onward[index][:, DK:]
            fresh_ref[place] = solved[index][:, DK:]
            own_ref[place] = through[index][:, DK:]
        return carry

    lax.fori_loop(0, blocks // unroll, prepare, 0)

    def advance(block, states):
        through = retain_ref[2 * block] * retain_ref[2 * block + 1]
        base = pl.multiple_of(block * BT, BT)
        lows = [state.astype(jnp.bfloat16) for state in states]
        products = [bdot(big_ref[head * blocks + block], lows[head]) for head in range(heads)]
        following = []
        for head in range(heads):
            place = head * blocks + block
            product = products[head]
            state_ref[place] = lows[head]
            following.append(states[head] * through - product[:BT] + add_ref[place])
            update_ref[place] = (fresh_ref[place] - product[BT : 2 * BT]).astype(jnp.bfloat16)
            delta = own_ref[place] + product[2 * BT :]
            delta_ref[pl.ds(base, BT), head * DK : head * DK + DK] = delta
            inv = lax.rsqrt(jnp.mean(delta * delta, axis=1, keepdims=True) + EPS_NORM)
            normed_ref[pl.ds(base, BT), head * DK : head * DK + DK] = (
                delta * inv * gain_ref[...]
            ).astype(jnp.bfloat16)
        return tuple(following)

    zero = jnp.zeros((DK, DK), jnp.float32)
    lax.fori_loop(0, blocks, advance, (zero,) * heads)

    def unpermute(step, carry):
        base = pl.multiple_of(step * PB, PB)
        mixed_ref[pl.ds(base, PB), :] = unpermute_rows(
            row_ref[...], base, normed_ref[...], tokens
        ).astype(jnp.bfloat16)
        return carry

    lax.fori_loop(0, tokens // PB, unpermute, 0)


VMEM = pltpu.MemorySpace.VMEM
SMEM = pltpu.MemorySpace.SMEM


def spec(space=VMEM):
    return pl.BlockSpec(memory_space=space)


def mixer_forward(retain, column, row, proj, taps, gain):
    tokens, width = proj.shape
    heads = taps.shape[1] // DK
    blocks = tokens // BT
    count = heads * blocks
    low, full = jnp.bfloat16, jnp.float32
    return pl.pallas_call(
        functools.partial(mixer_forward_kernel, heads),
        out_shape=(
            jax.ShapeDtypeStruct((tokens, heads * DK), low),
            jax.ShapeDtypeStruct((HALO + tokens, width), low),
            jax.ShapeDtypeStruct((tokens, heads * DK), full),
            jax.ShapeDtypeStruct((count, BT, BT), low),
            jax.ShapeDtypeStruct((count, 3 * BT, BT), low),
            jax.ShapeDtypeStruct((count, BT, BT), low),
            jax.ShapeDtypeStruct((count, BT, BT), low),
        ),
        in_specs=[spec(SMEM)] + [spec()] * 5,
        out_specs=(spec(),) * 7,
        scratch_shapes=[
            pltpu.VMEM((7, BT, BT), full),
            pltpu.VMEM((count, BT, BT), full),
            pltpu.VMEM((count, BT, BT), full),
            pltpu.VMEM((count, BT, BT), full),
            pltpu.VMEM((tokens, heads * DK), low),
        ],
        compiler_params=pltpu.CompilerParams(vmem_limit_bytes=56 << 20),
        name="mixer_forward",
    )(retain, column, row, proj, taps, gain)


def mixer_backward_kernel(
    heads,
    retain_ref,
    column_ref,
    row_ref,
    grad_ref,
    packed_ref,
    taps_ref,
    gain_ref,
    delta_ref,
    inverse_ref,
    big_ref,
    update_ref,
    state_ref,
    out_ref,
    taps_out_ref,
    gain_out_ref,
    grad_delta_ref,
    add_ref,
    after_ref,
    conv_ref,
    grad_proj_ref,
):
    tokens = grad_ref.shape[0]
    blocks = tokens // BT
    width = 3 * heads * DK

    def head_norm(step, total):
        base = pl.multiple_of(step * PB, PB)
        picked = permute_rows(column_ref[pl.ds(base, PB), :], grad_ref[...], tokens)
        for head in range(heads):
            at = slice(head * DK, head * DK + DK)
            grad = picked[:, at]
            delta = delta_ref[pl.ds(base, PB), at]
            inv = lax.rsqrt(jnp.mean(delta * delta, axis=1, keepdims=True) + EPS_NORM)
            unit = delta * inv
            total = total + jnp.sum(grad * unit, axis=0, keepdims=True)
            grad_unit = grad * gain_ref[...]
            low = (
                inv * (grad_unit - unit * jnp.mean(grad_unit * unit, axis=1, keepdims=True))
            ).astype(jnp.bfloat16)
            grad_delta_ref[pl.ds(base, PB), at] = low
            for sub in range(PB // BT):
                place = head * blocks + step * (PB // BT) + sub
                add_ref[place] = bdot(
                    big_ref[place, 2 * BT : 3 * BT, :], low[sub * BT : sub * BT + BT], TN
                )
        return total

    gain_out_ref[...] = lax.fori_loop(
        0, tokens // PB, head_norm, jnp.zeros((1, DK), jnp.float32)
    )

    def retreat(step, grads):
        block = blocks - 1 - step
        through = retain_ref[2 * block] * retain_ref[2 * block + 1]
        lows = [grad.astype(jnp.bfloat16) for grad in grads]
        following = []
        for head in range(heads):
            place = head * blocks + block
            after_ref[place] = lows[head]
            following.append(
                grads[head] * through
                - bdot(big_ref[place, 0:BT, :], lows[head], TN)
                + add_ref[place]
            )
        return tuple(following)

    zero = jnp.zeros((DK, DK), jnp.float32)
    lax.fori_loop(0, blocks, retreat, (zero,) * heads)

    conv_ref[tokens : tokens + HALO, :] = jnp.zeros((HALO, width), jnp.float32)

    def gradients(block, carry):
        first, second = retain_ref[2 * block], retain_ref[2 * block + 1]
        base = pl.multiple_of(block * BT, BT)
        masks = tap_masks(first, second, 1.0, BT)
        seen, kept = block_flags(first, second)
        rows, cols, cross = pair_mask(second)
        _, _, _ = rows, cols, cross
        turned = jnp.where((rows < CH) & (cols >= CH), second, 1.0)
        lanes = iota((BT, BT), 1)
        strengths = sigmoid(
            packed_ref[pl.ds(HALO + base, BT), width : width + BT].astype(jnp.float32)
        )
        grad_strengths = jnp.zeros((BT, BT), jnp.float32)
        for head in range(heads):
            place = head * blocks + block
            convs, gates, acts = [], [], []
            for kind in range(3):
                at = (kind * heads + head) * DK
                window = packed_ref[pl.ds(base, HALO + BT), at : at + DK].astype(jnp.float32)
                taps = [
                    taps_ref[kind * CONV + back : kind * CONV + back + 1, head * DK : head * DK + DK]
                    for back in range(CONV)
                ]
                conv = conv_of(window, taps, masks)
                gate = sigmoid(conv)
                convs.append(conv)
                gates.append(gate)
                acts.append(conv * gate)
            inv_q = lax.rsqrt(jnp.sum(acts[0] * acts[0], axis=1, keepdims=True) + EPS_NORM)
            inv_k = lax.rsqrt(jnp.sum(acts[1] * acts[1], axis=1, keepdims=True) + EPS_NORM)
            query_low = (acts[0] * inv_q * DK ** (-0.5)).astype(jnp.bfloat16)
            key_low = (acts[1] * inv_k).astype(jnp.bfloat16)
            key = key_low.astype(jnp.float32)
            value = acts[2]
            beta = strengths[:, head : head + 1]
            grad_low = grad_delta_ref[pl.ds(base, BT), head * DK : head * DK + DK]
            after = after_ref[place]
            state = state_ref[place]
            update = update_ref[place]
            inner = bdot(key_low, jnp.concatenate([key_low, query_low], axis=0), NT)
            scores_t = jnp.where(rows <= cols, inner[:, BT:] * turned, 0.0)
            grad_update = bdot(scores_t, grad_low) + bdot(key * kept, after)
            solved = bdot(inverse_ref[place], grad_update, TN)
            solved_beta = solved * beta
            both = jnp.concatenate([grad_low, solved.astype(jnp.bfloat16)], axis=0)
            on_state = bdot(both, state, NT)
            on_update = bdot(both, update, NT)
            grad_scores = jnp.where(rows >= cols, on_update[:BT] * cross, 0.0)
            grad_strict = jnp.where(rows > cols, on_update[BT:] * cross, 0.0)
            grad_weighted = on_state[BT:] * seen
            turned_both = bdot(
                update,
                jnp.concatenate(
                    [grad_low, solved_beta.astype(jnp.bfloat16)], axis=0
                ),
                NT,
            )
            grad_scores_t = jnp.where(rows <= cols, turned_both[:, :BT] * turned, 0.0)
            strict_t = jnp.where(rows < cols, turned_both[:, BT:] * turned, 0.0)
            grad_query = on_state[:BT] * seen + bdot(grad_scores, key_low)
            grad_key = (
                bdot(grad_scores_t, query_low)
                + bdot(update, after, NT) * kept
                - beta * grad_weighted
                - bdot(grad_strict * beta + strict_t, key_low)
            )
            grad_value = solved_beta
            grad_beta = jnp.sum(
                solved * value - grad_strict * inner[:, :BT] - grad_weighted * key,
                axis=1,
                keepdims=True,
            )
            grad_strengths = jnp.where(lanes == head, grad_beta, grad_strengths)
            scaled = (
                inv_q
                * DK ** (-0.5)
                * (
                    grad_query
                    - acts[0]
                    * (inv_q * inv_q)
                    * jnp.sum(grad_query * acts[0], axis=1, keepdims=True)
                ),
                inv_k
                * (
                    grad_key
                    - acts[1] * (inv_k * inv_k) * jnp.sum(grad_key * acts[1], axis=1, keepdims=True)
                ),
                grad_value,
            )
            for kind in range(3):
                at = (kind * heads + head) * DK
                conv_ref[pl.ds(base, BT), at : at + DK] = (
                    scaled[kind] * gates[kind] * (1.0 + convs[kind] * (1.0 - gates[kind]))
                )
        grad_proj_ref[pl.ds(base, BT), width : width + BT] = (
            grad_strengths * strengths * (1.0 - strengths)
        ).astype(jnp.bfloat16)
        return carry

    lax.fori_loop(0, blocks, gradients, 0)

    taps_out_ref[...] = jnp.zeros(taps_out_ref.shape, jnp.float32)

    def conv_back(block, carry):
        first, second, third = (
            retain_ref[2 * block],
            retain_ref[2 * block + 1],
            retain_ref[2 * block + 2],
        )
        base = pl.multiple_of(block * BT, BT)
        masks = tap_masks(first, second, third, BT + HALO)
        for kind in range(3):
            for head in range(heads):
                at = (kind * heads + head) * DK
                grads = conv_ref[pl.ds(base, BT + HALO), at : at + DK]
                window = packed_ref[pl.ds(base, HALO + BT), at : at + DK].astype(jnp.float32)
                total = None
                for back in range(CONV):
                    row = kind * CONV + back
                    tap = taps_ref[row : row + 1, head * DK : head * DK + DK]
                    masked = grads if back == 0 else grads * masks[back]
                    shifted = (
                        masked if back == 0 else pltpu.roll(masked, BT + HALO - back, 0)
                    )[:BT]
                    total = shifted * tap if total is None else total + shifted * tap
                    past = (window if back == 0 else pltpu.roll(window, back, 0))[HALO:]
                    taps_out_ref[row : row + 1, head * DK : head * DK + DK] += jnp.sum(
                        masked[:BT] * past, axis=0, keepdims=True
                    )
                grad_proj_ref[pl.ds(base, BT), at : at + DK] = total.astype(jnp.bfloat16)
        return carry

    lax.fori_loop(0, blocks, conv_back, 0)

    def unpermute(step, carry):
        base = pl.multiple_of(step * PB, PB)
        out_ref[pl.ds(base, PB), :] = unpermute_rows(
            row_ref[...], base, grad_proj_ref[...], tokens
        ).astype(jnp.bfloat16)
        return carry

    lax.fori_loop(0, tokens // PB, unpermute, 0)


def mixer_backward(retain, column, row, grad_mixed, taps, gain, saved):
    packed, delta, inverse, big, update, state = saved
    tokens = grad_mixed.shape[0]
    width = packed.shape[1]
    heads = taps.shape[1] // DK
    count = heads * (tokens // BT)
    low, full = jnp.bfloat16, jnp.float32
    return pl.pallas_call(
        functools.partial(mixer_backward_kernel, heads),
        out_shape=(
            jax.ShapeDtypeStruct((tokens, width), low),
            jax.ShapeDtypeStruct(taps.shape, full),
            jax.ShapeDtypeStruct((1, DK), full),
        ),
        in_specs=[spec(SMEM)] + [spec()] * 11,
        out_specs=(spec(),) * 3,
        scratch_shapes=[
            pltpu.VMEM((tokens, heads * DK), low),
            pltpu.VMEM((count, BT, BT), full),
            pltpu.VMEM((count, BT, BT), low),
            pltpu.VMEM((tokens + HALO, 3 * heads * DK), full),
            pltpu.VMEM((tokens, width), low),
        ],
        compiler_params=pltpu.CompilerParams(vmem_limit_bytes=56 << 20),
        name="mixer_backward",
    )(retain, column, row, grad_mixed, packed, taps, gain, delta, inverse, big, update, state)


def matmul(first, second):
    return lax.dot_general(first, second, NN, preferred_element_type=jnp.float32)


def times_transposed(first, second):
    return lax.dot_general(first, second, NT, preferred_element_type=jnp.float32)


def contract_rows(first, second):
    return lax.dot_general(first, second, TN, preferred_element_type=jnp.float32)


def rms_forward(values, gain):
    inv_rms = lax.rsqrt(jnp.mean(values * values, axis=-1, keepdims=True) + EPS_NORM)
    unit_rows = values * inv_rms
    return (unit_rows * gain, unit_rows, inv_rms)


def rms_backward(grad_out, unit_rows, inv_rms, gain):
    grad_gain = jnp.sum(grad_out * unit_rows, axis=0)
    grad_unit = grad_out * gain
    grad_in = inv_rms * (
        grad_unit - unit_rows * jnp.mean(grad_unit * unit_rows, axis=-1, keepdims=True)
    )
    return (grad_in, grad_gain)


def retains(lengths, tokens):
    index = jnp.arange(lengths.shape[0])
    starts = jnp.sum(jnp.where(index[:, None] > index[None, :], lengths[None, :], 0), axis=1)
    spans = jnp.arange(tokens // CH, dtype=jnp.int32) * CH
    keep = 1.0 - jnp.any(starts[None, :] == spans[:, None], axis=1).astype(jnp.float32)
    return jnp.pad(keep, (0, 2))


def own_slice(array, place, size, axis):
    return lax.dynamic_slice_in_dim(array, place * size, size, axis)


def local(
    n_seq,
    n_fsdp,
    tokens,
    norm_gain,
    w_query,
    w_key,
    w_value,
    w_beta,
    conv_taps,
    head_gain,
    w_out,
    ffn_gain,
    w_gate,
    w_up,
    w_down,
    cotangent,
    token_order,
    seq_lengths,
):
    place = lax.axis_index("seq")
    model = tokens.shape[1]
    head_count = w_beta.shape[1]
    heads = head_count // n_seq
    width = heads * DK
    hidden_units = w_gate.shape[1]
    slab = hidden_units // (n_fsdp * n_seq)
    units = slab * n_fsdp
    own_rows = w_query.shape[0]

    def gather(array, axis_name, axis=0):
        return lax.all_gather(array, axis_name, axis=axis, tiled=True)

    def pick_units(array):
        split = array.reshape(array.shape[0], n_fsdp, n_seq, slab)
        return lax.dynamic_index_in_dim(split, place, 2, keepdims=False).reshape(-1, units)

    inputs = tokens.astype(jnp.float32)
    normed_f, unit_one, inv_one = rms_forward(inputs, norm_gain)
    normed = gather(normed_f.astype(jnp.bfloat16), "seq")
    cot_all = gather(cotangent, "seq")
    group_tokens = normed.shape[0]
    w_mixer = gather(
        jnp.concatenate(
            [own_slice(array, place, width, 1) for array in (w_query, w_key, w_value)]
            + [jnp.pad(own_slice(w_beta, place, heads, 1), ((0, 0), (0, DK - heads)))],
            axis=1,
        ),
        "fsdp",
    )
    full_o = gather(w_out, "fsdp")
    full_gate = gather(pick_units(w_gate), "fsdp")
    full_up = gather(pick_units(w_up), "fsdp")
    full_down = gather(own_slice(w_down, place, slab, 0), "fsdp")

    proj = matmul(normed, w_mixer).astype(jnp.bfloat16)
    retain = retains(seq_lengths[0], group_tokens)
    column, row = token_order.reshape(-1, 1), token_order.reshape(1, -1)
    taps = own_slice(conv_taps, place, width, 2).reshape(3 * CONV, width)
    gain = head_gain.reshape(1, DK)
    mixed, *saved = mixer_forward(retain, column, row, proj, taps, gain)
    mixed_tok = lax.all_to_all(mixed, "seq", split_axis=0, concat_axis=1, tiled=True)
    hidden = inputs + matmul(mixed_tok, full_o)
    second_f, unit_two, inv_two = rms_forward(hidden, ffn_gain)
    second = gather(second_f.astype(jnp.bfloat16), "seq")
    gate_lin = matmul(second, full_gate)
    upward = matmul(second, full_up)
    sigmoid_gate = jax.nn.sigmoid(gate_lin)
    active = (gate_lin * sigmoid_gate * upward).astype(jnp.bfloat16)
    grad_active = times_transposed(cot_all, full_down)
    grad_gate = (
        grad_active * upward * sigmoid_gate * (1.0 + gate_lin * (1.0 - sigmoid_gate))
    ).astype(jnp.bfloat16)
    grad_upward = (grad_active * gate_lin * sigmoid_gate).astype(jnp.bfloat16)

    def spread(partial):
        pieces = lax.all_to_all(
            partial.astype(jnp.bfloat16).reshape(n_seq, -1, model),
            "seq",
            split_axis=0,
            concat_axis=0,
            tiled=True,
        )
        return jnp.sum(pieces.astype(jnp.float32), axis=0)

    grad_second = spread(
        times_transposed(grad_gate, full_gate) + times_transposed(grad_upward, full_up)
    )
    grad_hidden, grad_ffn_gain = rms_backward(grad_second, unit_two, inv_two, ffn_gain)
    grad_hidden = grad_hidden + cotangent.astype(jnp.float32)
    grad_attn = grad_hidden.astype(jnp.bfloat16)
    grad_mixed = times_transposed(grad_attn, full_o).astype(jnp.bfloat16)
    grad_heads = lax.all_to_all(grad_mixed, "seq", split_axis=1, concat_axis=0, tiled=True)
    result = (hidden + spread(matmul(active, full_down))).astype(jnp.bfloat16)

    def scatter(array):
        return lax.psum_scatter(
            array.astype(jnp.bfloat16), "fsdp", scatter_dimension=0, tiled=True
        )

    part_gate = scatter(contract_rows(second, grad_gate))
    part_up = scatter(contract_rows(second, grad_upward))
    part_down = scatter(contract_rows(active, cot_all))
    part_out = scatter(contract_rows(mixed_tok, grad_attn))

    grad_proj, grad_taps, grad_gain = mixer_backward(
        retain, column, row, grad_heads, taps, gain, saved
    )
    grad_normed = spread(times_transposed(grad_proj, w_mixer))
    part_mixer = scatter(contract_rows(normed, grad_proj))
    grad_inputs, grad_norm_gain = rms_backward(grad_normed, unit_one, inv_one, norm_gain)
    grad_inputs = grad_inputs + grad_hidden

    all_mixer = gather(part_mixer[None], "seq").astype(jnp.float32)

    def mixer_columns(start, size):
        return (
            all_mixer[:, :, start : start + size].transpose(1, 0, 2).reshape(own_rows, n_seq * size)
        )

    sum_q, sum_k, sum_v = (mixer_columns(kind * width, width) for kind in range(3))
    sum_b = mixer_columns(3 * width, heads)

    def all_units(part):
        pieces = gather(part[None], "seq").astype(jnp.float32)
        return (
            pieces.reshape(n_seq, own_rows, n_fsdp, slab)
            .transpose(1, 2, 0, 3)
            .reshape(own_rows, hidden_units)
        )

    sum_gate, sum_up = all_units(part_gate), all_units(part_up)
    sum_down = gather(part_down, "seq").astype(jnp.float32)
    sum_out = lax.psum(part_out, "seq").astype(jnp.float32)
    conv_full = lax.dynamic_update_slice_in_dim(
        jnp.zeros_like(conv_taps), grad_taps.reshape(3, CONV, width), place * width, 2
    )
    norm_total, ffn_total, head_total, conv_total = lax.psum(
        (grad_norm_gain, grad_ffn_gain, grad_gain[0], conv_full), ("seq", "fsdp")
    )
    return (
        result,
        grad_inputs,
        norm_total,
        sum_q,
        sum_k,
        sum_v,
        sum_b,
        conv_total,
        head_total,
        sum_out,
        ffn_total,
        sum_gate,
        sum_up,
        sum_down,
    )


def solution(mesh):
    tokens = P(("seq", "fsdp"), None)
    rows = P("fsdp", None)
    in_specs = (
        (tokens, P()) + (rows,) * 4 + (P(), P(), rows, P()) + (rows,) * 3 + (tokens, rows, rows)
    )
    out_specs = (
        (tokens, tokens, P()) + (rows,) * 4 + (P(), P(), rows, P()) + (rows,) * 3
    )
    return jax.shard_map(
        functools.partial(local, mesh.shape["seq"], mesh.shape["fsdp"]),
        mesh=mesh,
        in_specs=in_specs,
        out_specs=out_specs,
        check_vma=False,
    )
```

time: 2510 us -> 890 us (0.35); the launches traced: 2470 us -> 881 us
  matrix products: 1240 us -> 102 us
  local copies, waits for them, and re-layouts: 386 us -> 35.9 us
  other arithmetic: 245 us -> 25.7 us
  Pallas kernels: 0 us -> 109 us
  blocking collectives: 69.3 us -> 121 us
  starting transfers between devices: 47.8 us -> 19.8 us
    dot_general x2228 -> x15, matrix products: 1240 us -> 102 us  [the longest x5 40.5 us: matmul(): lax.dot_general(first, second, NN, preferred_element_type=jnp.float32)]
    reduce_scatter x2 -> x3, waiting for transfers between devices: 317 us -> 95.5 us  [scatter(): lax.psum_scatter(array.astype(jnp.bfloat16), 'fsdp', scatter_dimension=0,...]
    all_gather x7 -> x8, waiting for transfers between devices: 89.9 us -> 228 us  [gather(): return lax.all_gather(array, axis_name, axis=axis, tiled=True)]
    pallas_call x0 -> x2, Pallas kernels: none -> 109 us  [the longest x1 59.8 us: mixer_backward(): pl.pallas_call(functools.partial(mixer_backward_kernel, heads), out_shape...]
    squeeze x128 -> x0, local copies, waits for them, and re-layouts: 87 us -> none  [delta_rule(): lax.scan(jax.checkpoint(span_step), initial, (to_blocks(query_h), to_bloc...]
    all_to_all x10 -> x4, waiting for transfers between devices: 19.8 us -> 98.2 us  [the longest x3 83.8 us: spread(): lax.all_to_all(partial.astype(jnp.bfloat16).reshape(n_seq, -1, model), 's...]
    scatter-add x5 -> x0, other arithmetic: 65.4 us -> none  [the longest x1 13.4 us: local_mixer(): return mixed_packed[inverse]]
    select_n x32 -> x0, local copies, waits for them, and re-layouts: 46 us -> none  [span_step(): incl_mask = jnp.tril(jnp.ones((CH, CH), jnp.float32))]
  transfers between devices with their start and end apart: 20 -> 18, of which waited for: 8 -> 14; matrix products, arithmetic and copies ran while one was open for 74% -> 14% of each run, Pallas kernels for 0% -> 12%
where the time goes in v1:
time: 890 us; the launch traced here: 881 us
  waiting for transfers between devices  453 us (51%)
  blocking collectives  121 us (14%)
  Pallas kernels  109 us (12%)
  matrix products  102 us (11%)
  local copies, waits for them, and re-layouts  35.9 us (4%)
  other arithmetic  25.7 us (3%)
  starting transfers between devices  19.8 us (2%)
  between operations  14.8 us (2%)
    all_gather x8, waiting for transfers between devices, gather(): return lax.all_gather(array, axis_name, axis=axis, tiled=True)  228 us
    reduce_scatter x3, waiting for transfers between devices, scatter(): lax.psum_scatter(array.astype(jnp.bfloat16), 'fsdp', scatter_dimension=0,...  95.5 us
    all_to_all x3, waiting for transfers between devices, spread(): lax.all_to_all(partial.astype(jnp.bfloat16).reshape(n_seq, -1, model), 's...  83.8 us
    all_gather x4, blocking collectives, gather(): return lax.all_gather(array, axis_name, axis=axis, tiled=True)  63.5 us
    pallas_call x1, Pallas kernels, mixer_backward(): pl.pallas_call(functools.partial(mixer_backward_kernel, heads), out_shape...  59.8 us
    pallas_call x1, Pallas kernels, mixer_forward(): pl.pallas_call(functools.partial(mixer_forward_kernel, heads), out_shape=...  48.8 us
    dot_general x5, matrix products, matmul(): lax.dot_general(first, second, NN, preferred_element_type=jnp.float32)  40.5 us
    psum x1, blocking collectives, local(): lax.psum((grad_norm_gain, grad_ffn_gain, grad_gain[0], conv_full), ('seq'...  40.3 us
  transfers between devices with their start and end apart: 18, of which 14 were waited for; matrix products, arithmetic and copies ran while one was open for 14% of the time, Pallas kernels for 12%

profile of v1, /device:TPU:0, one launch (start us, length us, event | category | flops | bytes accessed | tf_op | source)
XLA Modules:
  0.0 880.8 jit_solution(16408047792453236235)
XLA Ops:
  20.3 39.6 %all-gather.14.cloned.1.call-done = bf16[1024,896]{1,0:T(8,128)(2,1)} async-done(((bf16[128,896]{1,0:T(8,128)(2,1)}), bf16[1024,896]{1,0:T(8,128)(2,1)}) %all-gather.14.cloned.1.call-update) | async-done | bytes 1835024 | tf_op jit(solution)/shard_map/all_gather | solution.py:580
  59.8 35.7 %all-gather.12.cloned.1.call-done = bf16[2048,1024]{1,0:T(8,128)(2,1)} async-done(((bf16[512,1024]{1,0:T(8,128)(2,1)}), bf16[2048,1024]{1,0:T(8,128)(2,1)}) %all-gather.12.cloned.1.call-update) | async-done | bytes 4194320 | tf_op jit(solution)/shard_map/all_gather | solution.py:580
  95.5 9.1 %convolution_convert_fusion.2.proj_ref = bf16[2048,896]{1,0:T(8,128)(2,1)} fusion(bf16[2048,1024]{1,0:T(8,128)(2,1)} %all-gather.12.cloned.1.call-done, bf16[1024,896]{1,0:T(8,128)(2,1)} %all-gather.14.cloned.1.call-done), kind=kOutput, calls=%fused_computation.15 | convolution fusion | flops 3759931392 | bytes 9699328 | tf_op jit(solution)/shard_map/dot_general | solution.py:511
  104.7 48.8 %mixer_forward.1 = (bf16[2048,256]{1,0:T(8,128)(2,1)}, bf16[2064,896]{1,0:T(8,128)(2,1)}, f32[2048,256]{1,0:T(8,128)}, bf16[32,128,128]{2,1,0:T(8,128)(2,1)}, bf...) custom-call(f32[34]{0:T(128)} %pad.8.retain_ref, ...), custom_call_target="tpu_custom_call" | custom-call | tf_op jit(solution)/shard_map/mixer_forward/pallas_call | solution.py:240
  159.3 14.4 %all-to-all-done = bf16[4,512,256]{1,2,0:T(8,128)(2,1)S(1)} async-done(((bf16[4,512,256]{1,2,0:T(8,128)(2,1)}), bf16[4,512,256]{1,2,0:T(8,128)(2,1)S(1)}, u32[]{:S(2)}, u32[]{:S(2)}) %all-to-all-start) | async-done | bytes 1048608 | tf_op jit(solution)/shard_map/all_to_all | solution.py:610
  183.5 7.7 all-gather.24.cloned.1.call-done
  191.2 34.3 %all-gather.26.cloned.1.call-done = bf16[2048,1024]{1,0:T(8,128)(2,1)} async-done(((bf16[512,1024]{1,0:T(8,128)(2,1)}), bf16[2048,1024]{1,0:T(8,128)(2,1)}) %all-gather.26.cloned.1.call-update) | async-done | bytes 4194320 | tf_op jit(solution)/shard_map/all_gather | solution.py:580
  225.4 8.3 fusion.21
  233.7 38.0 %all-gather.22.cloned.1.call-done = bf16[1024,704]{0,1:T(8,128)(2,1)} async-done(((bf16[128,704]{0,1:T(8,128)(2,1)}), bf16[1024,704]{0,1:T(8,128)(2,1)}) %all-gather.22.cloned.1.call-update) | async-done | bytes 1441808 | tf_op jit(solution)/shard_map/all_gather | solution.py:580
  271.7 35.0 %all-gather.18.cloned.1.call-done = bf16[2048,1024]{1,0:T(8,128)(2,1)} async-done(((bf16[512,1024]{1,0:T(8,128)(2,1)}), bf16[2048,1024]{1,0:T(8,128)(2,1)}) %all-gather.18.cloned.1.call-update) | async-done | bytes 4194320 | tf_op jit(solution)/shard_map/all_gather | solution.py:580
  306.8 8.3 fusion.20
  315.1 38.2 %all-gather.20.cloned.1.call-done = bf16[1024,704]{0,1:T(8,128)(2,1)} async-done(((bf16[128,704]{0,1:T(8,128)(2,1)}), bf16[1024,704]{0,1:T(8,128)(2,1)}) %all-gather.20.cloned.1.call-update) | async-done | bytes 1441808 | tf_op jit(solution)/shard_map/all_gather | solution.py:580
  353.3 12.1 %fusion.4 = (bf16[2048,704]{0,1:T(8,128)(2,1)S(1)}, bf16[2048,704]{0,1:T(8,128)(2,1)S(1)}, bf16[2048,704]{0,1:T(8,128)(2,1)}) fusion(f32[704,2048]{1,0:T(8,128)} %fusion.21, f32[2048,704]{0,1:T(8,128)} %fusion.20, bf16[2048,1024]{1,0:T(8,128)(2,1)} %all-gather.18.cloned.1.call-done, bf16[1024,704]{0,1:T(8,128)(2,1)} %all-gather.20.cloned.1.call-done), kind=kOutput, calls=%fused_computation.10 | convolution fusion | flops 2975858688 | bytes 25821184 | tf_op jit(solution)/shard_map/dot_general | solution.py:511
  368.9 5.0 add_convert_fusion
  378.8 7.7 convolution_convert_fusion
  386.4 40.6 %all-to-all-done.2 = bf16[4,512,1024]{2,1,0:T(8,128)(2,1)} async-done(((bf16[4,512,1024]{2,1,0:T(8,128)(2,1)}), bf16[4,512,1024]{2,1,0:T(8,128)(2,1)}, u32[]{:S(2)}, u32[]{:S(2)}) %all-to-all-start.2) | async-done | bytes 4194336 | tf_op jit(solution)/shard_map/all_to_all | solution.py:625
  437.0 43.2 %all-to-all-done.1 = bf16[4,512,1024]{2,1,0:T(8,128)(2,1)} async-done(((bf16[4,512,1024]{2,1,0:T(8,128)(2,1)}), bf16[4,512,1024]{2,1,0:T(8,128)(2,1)}, u32[]{:S(2)}, u32[]{:S(2)}) %all-to-all-start.1) | async-done | bytes 4194336 | tf_op jit(solution)/shard_map/all_to_all | solution.py:625
  490.5 6.2 convolution_convert_fusion.6
  498.4 6.2 convolution_convert_fusion.5
  506.5 7.6 convolution_convert_fusion.7
  517.1 17.6 %all_to_all.53 = bf16[512,4,256]{2,0,1:T(8,128)(2,1)} all-to-all(bf16[512,4,256]{2,0,1:T(8,128)(2,1)S(1)} %bitcast.98), channel_id=1, replica_groups=mesh['seq'=4,'fsdp'=8] {'seq'}, dimensions={1} | all-to-all | bytes 2097152 | tf_op jit(solution)/shard_map/all_to_all | solution.py:641
  534.7 59.8 %mixer_backward.1 = (bf16[2048,896]{1,0:T(8,128)(2,1)}, f32[12,256]{1,0:T(8,128)}, f32[1,128]{1,0:T(1,128)}) custom-call(f32[34]{0:T(128)} %pad.8.retain_ref, s32[2048,1]{1,0:T(8,128)} %copy.82.column_ref, s32[1,2048]{1,0:T(1,128)} %row_ref.3, bf16[2048,256]{1,0:T(8,128)(2,1)} %bitcast.94, bf16[2064,896]{1,0:T(8,128)(2,1)} %get-tuple-element.25.packed_ref, ...), custom_call_target="tpu_custom_call" | custom-call | tf_op jit(solution)/shard_map/mixer_backward/pallas_call | solution.py:489
  594.5 8.3 convolution_convert_fusion.1
  608.8 9.3 %convolution_convert_fusion.4 = bf16[1024,896]{1,0:T(8,128)(2,1)} fusion(bf16[2048,1024]{1,0:T(8,128)(2,1)} %all-gather.12.cloned.1.call-done, bf16[2048,896]{1,0:T(8,128)(2,1)} %get-tuple-element.31), kind=kOutput, calls=%fused_computation.37 | convolution fusion | flops 3759013888 | bytes 9699328 | tf_op jit(solution)/shard_map/dot_general | solution.py:519
  624.1 37.0 %all-gather.1 = bf16[512,704]{0,1:T(8,128)(2,1)} all-gather(bf16[128,704]{0,1:T(8,128)(2,1)S(1)} %copy.97), channel_id=3, replica_groups=mesh['seq'=4,'fsdp'=8] {'seq'}, dimensions={0}, use_global_device_ids=true | all-gather | bytes 901120 | tf_op jit(solution)/shard_map/all_gather | solution.py:580
  666.9 23.7 %reduce-scatter.18.cloned.1.call-done = bf16[128,704]{1,0:T(8,128)(2,1)} async-done(((bf16[1024,704]{1,0:T(8,128)(2,1)}), bf16[128,704]{1,0:T(8,128)(2,1)}) %reduce-scatter.18.cloned.1.call-update) | async-done | bytes 180240
  691.6 8.7 all-gather.2
  706.1 51.6 %reduce-scatter.14.cloned.1.call-done = bf16[88,1024]{1,0:T(8,128)(2,1)} async-done(((bf16[704,1024]{1,0:T(8,128)(2,1)}), bf16[88,1024]{1,0:T(8,128)(2,1)}) %reduce-scatter.14.cloned.1.call-update) | async-done | bytes 180240 | tf_op jit(solution)/shard_map/reduce_scatter | solution.py:645
  757.7 8.3 all_gather.47
  771.3 40.3 %all-reduce.2 = (f32[1024]{0:T(1024)}, f32[3,4,1024]{2,1,0:T(4,128)}, f32[128]{0:T(128)}, f32[1024]{0:T(1024)}) all-reduce(f32[1024]{0:T(1024)S(1)} %get-tuple-element.92, f32[3,4,1024]{2,1,0:T(4,128)S(1)} %constant_dynamic-update-slice_fusion, f32[128]{0:T(128)S(1)} %bitcast.115, ...), channel_id=1, replica_groups=mesh['seq'=4,'fsdp'=8] {'seq','fsdp'}, use_global_device_ids=true, to_apply=%region_10.11 | all-reduce | flops 14464 | bytes 115712 | tf_op jit(solution)/shard_map/psum | solution.py:686
  816.9 43.9 %reduce-scatter.10.cloned.1.call-done = bf16[128,896]{1,0:T(8,128)(2,1)} async-done(((bf16[1024,896]{1,0:T(8,128)(2,1)}), bf16[128,896]{1,0:T(8,128)(2,1)}) %reduce-scatter.10.cloned.1.call-update) | async-done | bytes 229392 | tf_op jit(solution)/shard_map/reduce_scatter | solution.py:645
  860.8 9.5 %all-gather = bf16[512,896]{1,0:T(8,128)(2,1)S(1)} all-gather(bf16[128,896]{1,0:T(8,128)(2,1)} %reduce-scatter.10.cloned.1.call-done), channel_id=2, replica_groups=mesh['seq'=4,'fsdp'=8] {'seq'}, dimensions={0}, use_global_device_ids=true | all-gather | bytes 1146880 | tf_op jit(solution)/shard_map/all_gather | solution.py:580
  (139 shorter events, 102.1 us)
Async XLA Ops:
  7.2 7.2 copy-start
  7.2 5.0 copy-start.2
  7.2 5.0 copy-start.12
  7.2 52.6 %all-gather.14.cloned.1.call-start = ((), (), s32[]{:S(2)}) async-start(), calls=%async_computation.11 | async-start | bytes 2064384 | tf_op jit(solution)/shard_map/all_gather | solution.py:580
  10.7 84.8 %all-gather.12.cloned.1.call-start = ((), (), s32[]{:S(2)}) async-start(), calls=%async_computation.10 | async-start | bytes 5242880 | tf_op jit(solution)/shard_map/all_gather | solution.py:580
  13.6 4.6 copy-start.10
  13.6 145.7 %all-gather.16.cloned.1.call-start = ((), (), s32[]{:S(2)}) async-start(), calls=%async_computation.12 | async-start | bytes 2359296 | tf_op jit(solution)/shard_map/all_gather | solution.py:580
  14.3 176.8 %all-gather.24.cloned.1.call-start = ((), (), s32[]{:S(2)}) async-start(), calls=%async_computation.16 | async-start | bytes 1622016 | tf_op jit(solution)/shard_map/all_gather | solution.py:580
  15.1 4.4 copy-start.18
  15.1 210.3 %all-gather.26.cloned.1.call-start = ((), (), s32[]{:S(2)}) async-start(), calls=%async_computation.17 | async-start | bytes 5242880 | tf_op jit(solution)/shard_map/all_gather | solution.py:580
  15.7 256.0 %all-gather.22.cloned.1.call-start = ((), (), s32[]{:S(2)}) async-start(), calls=%async_computation.15 | async-start | bytes 1622016 | tf_op jit(solution)/shard_map/all_gather | solution.py:580
  155.7 18.0 %all-to-all-start = ((bf16[4,512,256]{1,2,0:T(8,128)(2,1)}), bf16[4,512,256]{1,2,0:T(8,128)(2,1)S(1)}, u32[]{:S(2)}, u32[]{:S(2)}) async-start(bf16[4,512,256]{1,2,0:T(8,128)(2,1)} %copy.83), calls=%async_computation | async-start | bytes 2097152 | tf_op jit(solution)/shard_map/all_to_all | solution.py:610
  159.3 147.5 %all-gather.18.cloned.1.call-start = ((), (), s32[]{:S(2)}) async-start(), calls=%async_computation.13 | async-start | bytes 5242880 | tf_op jit(solution)/shard_map/all_gather | solution.py:580
  179.2 174.0 %all-gather.20.cloned.1.call-start = ((), (), s32[]{:S(2)}) async-start(), calls=%async_computation.14 | async-start | bytes 1622016 | tf_op jit(solution)/shard_map/all_gather | solution.py:580
  353.3 12.1 %copy-start.17 = (bf16[1024,704]{0,1:T(8,128)(2,1)S(1)}, bf16[1024,704]{0,1:T(8,128)(2,1)}, u32[]{:S(2)}) copy-start(bf16[1024,704]{0,1:T(8,128)(2,1)} %all-gather.20.cloned.1.call-done) | copy-start | bytes 4325380
  365.3 3.5 copy-start.19
  365.3 3.5 copy-start.20
  365.3 3.5 copy-start.16
  373.9 53.1 %all-to-all-start.2 = ((bf16[4,512,1024]{2,1,0:T(8,128)(2,1)}), bf16[4,512,1024]{2,1,0:T(8,128)(2,1)}, u32[]{:S(2)}, u32[]{:S(2)}) async-start(bf16[4,512,1024]{2,1,0:T(8,128)(2,1)} %bitcast.97), calls=%async_computation.2 | async-start | bytes 8388608 | tf_op jit(solution)/shard_map/all_to_all | solution.py:625
  427.0 53.2 %all-to-all-start.1 = ((bf16[4,512,1024]{2,1,0:T(8,128)(2,1)}), bf16[4,512,1024]{2,1,0:T(8,128)(2,1)}, u32[]{:S(2)}, u32[]{:S(2)}) async-start(bf16[4,512,1024]{2,1,0:T(8,128)(2,1)} %bitcast.96), calls=%async_computation.1 | async-start | bytes 8388608 | tf_op jit(solution)/shard_map/all_to_all | solution.py:625
  432.0 175.8 %reduce-scatter.12.cloned.1.call-start = ((), (), s32[]{:S(2)}) async-start(), calls=%async_computation.19 | async-start | bytes 2359296 | tf_op jit(solution)/shard_map/reduce_scatter | solution.py:645
  480.2 3.6 copy-start.4
  480.2 3.6 copy-start.5
  490.5 132.5 %reduce-scatter.16.cloned.1.call-start = ((), (), s32[]{:S(2)}) async-start(), calls=%async_computation.22 | async-start | bytes 1769472
  498.3 192.2 %reduce-scatter.18.cloned.1.call-start = ((), (), s32[]{:S(2)}) async-start(), calls=%async_computation.23 | async-start | bytes 1769472
  506.2 7.9 copy-start.8
  506.2 251.5 %reduce-scatter.14.cloned.1.call-start = ((), (), s32[]{:S(2)}) async-start(), calls=%async_computation.21 | async-start | bytes 1622016 | tf_op jit(solution)/shard_map/reduce_scatter | solution.py:645
  534.7 59.8 %copy-start.15 = (bf16[1024,896]{1,0:T(8,128)(2,1)S(1)}, bf16[1024,896]{1,0:T(8,128)(2,1)}, u32[]{:S(2)}) copy-start(bf16[1024,896]{1,0:T(8,128)(2,1)} %all-gather.14.cloned.1.call-done) | copy-start | bytes 5505028
  602.8 164.5 %all-to-all-start.4 = ((bf16[4,512,1024]{2,1,0:T(8,128)(2,1)}), bf16[4,512,1024]{2,1,0:T(8,128)(2,1)}, u32[]{:S(2)}, u32[]{:S(2)}) async-start(bf16[4,512,1024]{2,1,0:T(8,128)(2,1)} %bitcast.95), calls=%async_computation.4 | async-start | bytes 8388608 | tf_op jit(solution)/shard_map/all_to_all | solution.py:625
  607.7 207.4 %all-reduce.5.cloned.1.call-start = ((), (), s32[]{:S(2)}) async-start(), calls=%async_computation.20 | async-start | bytes 524288 | tf_op jit(solution)/shard_map/psum | solution.py:682
  608.5 252.3 %reduce-scatter.10.cloned.1.call-start = ((), (), s32[]{:S(2)}) async-start(), calls=%async_computation.18 | async-start | bytes 2064384 | tf_op jit(solution)/shard_map/reduce_scatter | solution.py:645
  706.1 61.2 %copy-start.13 = (f32[12,256]{1,0:T(8,128)S(1)}, f32[12,256]{1,0:T(8,128)}, u32[]{:S(2)}) copy-start(f32[12,256]{1,0:T(8,128)} %get-tuple-element.32) | copy-start | bytes 36868
  (7 other events, 15.7 us)
Sparse Core Ops, SparseCore 0:
  10.8 48.9 all-gather.13
  62.0 33.5 all-gather.11
  97.7 49.2 all-gather.15
  149.6 41.5 all-gather.23
  192.6 32.8 all-gather.25
  227.9 43.8 all-gather.21
  273.9 32.8 all-gather.17
  309.4 43.8 all-gather.19
  490.6 65.2 reduce-scatter.11
  559.1 63.7 reduce-scatter.15
  626.8 63.6 reduce-scatter.17
  693.8 63.8 reduce-scatter.13
  760.0 30.9 all-reduce.4
  794.7 66.0 reduce-scatter.9

commit v2 on v1

--- a/solution.py
+++ b/solution.py
@@ -95,15 +95,184 @@
     return lax.dot_general(hot, source, NN, preferred_element_type=jnp.float32)
 
 
+MESH = pl.DeviceIdType.MESH
+ANY = pl.ANY
+
+
+class Gather:
+    outer = 4
+
+    @classmethod
+    def copies(cls, n_fsdp):
+        inner = n_fsdp // cls.outer
+        return (cls.outer - 1) + cls.outer * (inner - 1)
+
+    def __init__(self, n_fsdp, source, slot, sems, base, local_sem):
+        self.inner = n_fsdp // self.outer
+        self.me = lax.axis_index("fsdp")
+        self.seq = lax.axis_index("seq")
+        self.high, self.low = self.me // self.inner, self.me % self.inner
+        self.source, self.slot = source, slot
+        self.send, self.recv = sems
+        self.base, self.local_sem = base, local_sem
+
+    def at(self, high, low):
+        return (high % self.outer) * self.inner + (low % self.inner)
+
+    def copy(self, source, owner, target, index):
+        return pltpu.make_async_remote_copy(
+            src_ref=source,
+            dst_ref=self.slot(owner),
+            send_sem=self.send.at[self.base + index],
+            recv_sem=self.recv.at[self.base + index],
+            device_id=(self.seq, target),
+            device_id_type=MESH,
+        )
+
+    def along_outer(self, step):
+        return self.copy(self.source, self.me, self.at(self.high + step, self.low), step - 1)
+
+    def along_inner(self, hop):
+        return self.copy(
+            self.source, self.me, self.at(self.high, self.low + hop), self.outer - 2 + hop
+        )
+
+    def passed_on(self, step, hop):
+        owner = self.at(self.high - step, self.low)
+        index = self.outer - 1 + (self.inner - 1) * step + hop - 1
+        return self.copy(self.slot(owner), owner, self.at(self.high, self.low + hop), index)
+
+    def own(self):
+        return pltpu.make_async_copy(self.source, self.slot(self.me), self.local_sem)
+
+    def start(self):
+        for step in range(1, self.outer):
+            self.along_outer(step).start()
+        for hop in range(1, self.inner):
+            self.along_inner(hop).start()
+        self.own().start()
+
+    def relay(self):
+        for step in range(1, self.outer):
+            self.along_outer(step).wait_recv()
+            for hop in range(1, self.inner):
+                self.passed_on(step, hop).start()
+
+    def finish(self):
+        self.own().wait()
+        for hop in range(1, self.inner):
+            self.along_inner(hop).wait_recv()
+            for step in range(1, self.outer):
+                self.passed_on(step, hop).wait_recv()
+        for step in range(1, self.outer):
+            self.along_outer(step).wait_send()
+        for hop in range(1, self.inner):
+            self.along_inner(hop).wait_send()
+            for step in range(1, self.outer):
+                self.passed_on(step, hop).wait_send()
+
+
+class Share:
+    @staticmethod
+    def copies(n_seq):
+        return 1 + 2 * (n_seq // 2 - 1)
+
+    def __init__(self, n_seq, source, slot, sems, base, local_sem):
+        self.n_seq, self.chips = n_seq, n_seq // 2
+        self.me = lax.axis_index("seq")
+        self.fsdp = lax.axis_index("fsdp")
+        self.mate = self.me + 1 - 2 * (self.me % 2)
+        self.source, self.slot = source, slot
+        self.send, self.recv = sems
+        self.base, self.local_sem = base, local_sem
+
+    def copy(self, source, owner, target, index):
+        return pltpu.make_async_remote_copy(
+            src_ref=source,
+            dst_ref=self.slot(owner),
+            send_sem=self.send.at[self.base + index],
+            recv_sem=self.recv.at[self.base + index],
+            device_id=(target, self.fsdp),
+            device_id_type=MESH,
+        )
+
+    def to_mate(self):
+        return self.copy(self.source, self.me, self.mate, 0)
+
+    def across(self, step):
+        return self.copy(self.source, self.me, (self.me + 2 * step) % self.n_seq, step)
+
+    def passed_on(self, step):
+        owner = (self.me + self.n_seq - 2 * step) % self.n_seq
+        return self.copy(self.slot(owner), owner, self.mate, self.chips - 1 + step)
+
+    def own(self):
+        return pltpu.make_async_copy(self.source, self.slot(self.me), self.local_sem)
+
+    def start(self):
+        for step in range(1, self.chips):
+            self.across(step).start()
+        self.to_mate().start()
+        self.own().start()
+
+    def relay(self):
+        for step in range(1, self.chips):
+            self.across(step).wait_recv()
+            self.passed_on(step).start()
+
+    def finish(self):
+        self.own().wait()
+        self.to_mate().wait_recv()
+        for step in range(1, self.chips):
+            self.passed_on(step).wait_recv()
+        self.to_mate().wait_send()
+        for step in range(1, self.chips):
+            self.across(step).wait_send()
+            self.passed_on(step).wait_send()
+
+
+def greet(n_seq, n_fsdp):
+    seq, fsdp = lax.axis_index("seq"), lax.axis_index("fsdp")
+    barrier = pltpu.get_barrier_semaphore()
+    for step in range(1, n_seq):
+        pl.semaphore_signal(
+            barrier, inc=1, device_id=((seq + step) % n_seq, fsdp), device_id_type=MESH
+        )
+    for step in range(1, n_fsdp):
+        pl.semaphore_signal(
+            barrier, inc=1, device_id=(seq, (fsdp + step) % n_fsdp), device_id_type=MESH
+        )
+    pl.semaphore_wait(barrier, n_seq + n_fsdp - 2)
+
+
+def aligned(value, unit):
+    return pl.multiple_of(value, unit)
+
+
 def mixer_forward_kernel(
     heads,
+    n_seq,
+    n_fsdp,
     retain_ref,
     column_ref,
     row_ref,
-    proj_ref,
     taps_ref,
     gain_ref,
-    mixed_ref,
+    normed_in,
+    mixer_in,
+    gate_in,
+    up_in,
+    down_in,
+    out_in,
+    cot_in,
+    tokens_mixed,
+    normed_all,
+    mixer_all,
+    gate_all,
+    up_all,
+    down_all,
+    out_all,
+    cot_all,
     packed_ref,
     delta_ref,
     inverse_ref,
@@ -114,12 +283,110 @@
     fresh_ref,
     own_ref,
     add_ref,
+    mixed_ref,
+    ready_ref,
+    proj_ref,
     normed_ref,
+    weight_ref,
+    gather_send,
+    gather_recv,
+    share_send,
+    share_recv,
+    local_sems,
 ):
-    tokens = proj_ref.shape[0]
+    tokens, width = proj_ref.shape
     blocks = tokens // BT
+    own_tokens = tokens // n_seq
+    seq = lax.axis_index("seq")
+    own_rows = mixer_in.shape[0]
+    half_rows = own_rows // 2
+    out_rows, out_width = out_in.shape
+    half_width = out_width // 2
+    core = seq % 2
+
+    greet(n_seq, n_fsdp)
+
+    gather_sems = (gather_send, gather_recv)
+    share_sems = (share_send, share_recv)
+    per_gather = Gather.copies(n_fsdp)
+    per_share = Share.copies(n_seq)
+
+    def rows_slot(ref, size, start=0, count=None):
+        count = size if count is None else count
+        return lambda owner: ref.at[pl.ds(aligned(owner * size + start, count), count)]
+
+    def gather_piece(index, source, slot):
+        return Gather(
+            n_fsdp, source, slot, gather_sems, index * per_gather, local_sems.at[index]
+        )
+
+    mixers = [
+        gather_piece(
+            part,
+            mixer_in.at[pl.ds(part * half_rows, half_rows)],
+            rows_slot(weight_ref, own_rows, part * half_rows, half_rows),
+        )
+        for part in range(2)
+    ]
+    half_at = aligned(core * half_width, half_width)
+    pieces = [
+        gather_piece(
+            2,
+            out_in.at[:, pl.ds(half_at, half_width)],
+            lambda owner: out_all.at[
+                pl.ds(aligned(owner * out_rows, out_rows), out_rows), pl.ds(half_at, half_width)
+            ],
+        ),
+        gather_piece(3, gate_in, rows_slot(gate_all, own_rows)),
+        gather_piece(4, up_in, rows_slot(up_all, own_rows)),
+        gather_piece(5, down_in, lambda owner: down_all.at[owner]),
+    ]
+    share_normed = Share(
+        n_seq, normed_in, rows_slot(normed_ref, own_tokens), share_sems, 0, local_sems.at[6]
+    )
+    share_cot = Share(
+        n_seq, cot_in, rows_slot(cot_all, own_tokens), share_sems, per_share, local_sems.at[7]
+    )
+    swap = pltpu.make_async_remote_copy(
+        src_ref=out_all.at[:, pl.ds(half_at, half_width)],
+        dst_ref=out_all.at[:, pl.ds(half_at, half_width)],
+        send_sem=share_send.at[2 * per_share],
+        recv_sem=share_recv.at[2 * per_share],
+        device_id=(share_normed.mate, lax.axis_index("fsdp")),
+        device_id_type=MESH,
+    )
+
+    mixers[0].start()
+    share_normed.start()
     fill_masks(mask_ref)
     packed_ref[0:HALO, :] = jnp.zeros((HALO, packed_ref.shape[1]), jnp.bfloat16)
+    mixers[0].relay()
+    mixers[1].start()
+    share_normed.relay()
+    mixers[1].relay()
+    pieces[0].start()
+    share_cot.start()
+    mixers[0].finish()
+    mixers[1].finish()
+    share_normed.finish()
+    keep_normed = pltpu.make_async_copy(normed_ref, normed_all, local_sems.at[8])
+    keep_mixer = pltpu.make_async_copy(weight_ref, mixer_all, local_sems.at[9])
+    keep_normed.start()
+    keep_mixer.start()
+
+    def project(step, carry):
+        base = aligned(step * PB, PB)
+        proj_ref[pl.ds(base, PB), :] = lax.dot_general(
+            normed_ref[pl.ds(base, PB), :],
+            weight_ref[...],
+            NN,
+            preferred_element_type=jnp.float32,
+        ).astype(jnp.bfloat16)
+        return carry
+
+    lax.fori_loop(0, tokens // PB, project, 0)
+    pieces[0].relay()
+    pieces[1].start()
 
     def permute(step, carry):
         base = pl.multiple_of(step * PB, PB)
@@ -128,10 +395,20 @@
         return carry
 
     lax.fori_loop(0, tokens // PB, permute, 0)
+    pieces[0].finish()
+    swap.start()
+    share_cot.relay()
 
     unroll = 2
 
     def prepare(step, carry):
+        for number in (1, 2):
+
+            @pl.when(step == (0, 1, 5)[number])
+            def _():
+                pieces[number].relay()
+                pieces[number + 1].start()
+
         places, stricts, kept_values = [], [], []
         for sub in range(unroll):
             block = step * unroll + sub
@@ -205,7 +482,7 @@
             delta = own_ref[place] + product[2 * BT :]
             delta_ref[pl.ds(base, BT), head * DK : head * DK + DK] = delta
             inv = lax.rsqrt(jnp.mean(delta * delta, axis=1, keepdims=True) + EPS_NORM)
-            normed_ref[pl.ds(base, BT), head * DK : head * DK + DK] = (
+            ready_ref[pl.ds(base, BT), head * DK : head * DK + DK] = (
                 delta * inv * gain_ref[...]
             ).astype(jnp.bfloat16)
         return tuple(following)
@@ -213,14 +490,46 @@
     zero = jnp.zeros((DK, DK), jnp.float32)
     lax.fori_loop(0, blocks, advance, (zero,) * heads)
 
-    def unpermute(step, carry):
-        base = pl.multiple_of(step * PB, PB)
-        mixed_ref[pl.ds(base, PB), :] = unpermute_rows(
-            row_ref[...], base, normed_ref[...], tokens
-        ).astype(jnp.bfloat16)
-        return carry
-
-    lax.fori_loop(0, tokens // PB, unpermute, 0)
+    pieces[3].relay()
+
+    def hand_over(shift):
+        target = (seq + shift) % n_seq
+        base = aligned(target * own_tokens, own_tokens)
+        for part in range(max(own_tokens // PB, 1)):
+            size = min(own_tokens, PB)
+            first = aligned(base + part * size, size)
+            hot = jnp.where(
+                row_ref[...] == iota((size, tokens), 0) + first, 1.0, 0.0
+            ).astype(jnp.bfloat16)
+            mixed_ref[pl.ds(first, size), :] = lax.dot_general(
+                hot, ready_ref[...], NN, preferred_element_type=jnp.float32
+            ).astype(jnp.bfloat16)
+        source = mixed_ref.at[pl.ds(base, own_tokens)]
+        slot = tokens_mixed.at[:, pl.ds(aligned(seq * heads * DK, heads * DK), heads * DK)]
+        if shift == 0:
+            return pltpu.make_async_copy(source, slot, local_sems.at[10])
+        return pltpu.make_async_remote_copy(
+            src_ref=source,
+            dst_ref=slot,
+            send_sem=share_send.at[2 * per_share + shift],
+            recv_sem=share_recv.at[2 * per_share + shift],
+            device_id=(target, lax.axis_index("fsdp")),
+            device_id_type=MESH,
+        )
+
+    handed = []
+    for shift in list(range(1, n_seq)) + [0]:
+        copy = hand_over(shift)
+        copy.start()
+        handed.append(copy)
+    for copy in handed:
+        copy.wait()
+    swap.wait()
+    keep_normed.wait()
+    keep_mixer.wait()
+    share_cot.finish()
+    for piece in pieces[1:]:
+        piece.finish()
 
 
 VMEM = pltpu.MemorySpace.VMEM
@@ -231,16 +540,33 @@
     return pl.BlockSpec(memory_space=space)
 
 
-def mixer_forward(retain, column, row, proj, taps, gain):
-    tokens, width = proj.shape
+def mixer_forward(n_seq, n_fsdp, retain, column, row, taps, gain, shards):
+    normed, mixer, gate, up, down, out, cot = shards
+    own_tokens, model = normed.shape
+    tokens = own_tokens * n_seq
+    width = mixer.shape[1]
     heads = taps.shape[1] // DK
     blocks = tokens // BT
     count = heads * blocks
     low, full = jnp.bfloat16, jnp.float32
+    per_gather, per_share = Gather.copies(n_fsdp), Share.copies(n_seq)
+    gathers = 6 * per_gather
+    shares = 2 * per_share + n_seq
+
+    def whole(array):
+        return jax.ShapeDtypeStruct((array.shape[0] * n_fsdp, array.shape[1]), low)
+
     return pl.pallas_call(
-        functools.partial(mixer_forward_kernel, heads),
+        functools.partial(mixer_forward_kernel, heads, n_seq, n_fsdp),
         out_shape=(
-            jax.ShapeDtypeStruct((tokens, heads * DK), low),
+            jax.ShapeDtypeStruct((own_tokens, n_seq * heads * DK), low),
+            jax.ShapeDtypeStruct((tokens, model), low),
+            whole(mixer),
+            whole(gate),
+            whole(up),
+            jax.ShapeDtypeStruct((n_fsdp,) + down.shape, low),
+            whole(out),
+            jax.ShapeDtypeStruct((tokens, model), low),
             jax.ShapeDtypeStruct((HALO + tokens, width), low),
             jax.ShapeDtypeStruct((tokens, heads * DK), full),
             jax.ShapeDtypeStruct((count, BT, BT), low),
@@ -248,18 +574,29 @@
             jax.ShapeDtypeStruct((count, BT, BT), low),
             jax.ShapeDtypeStruct((count, BT, BT), low),
         ),
-        in_specs=[spec(SMEM)] + [spec()] * 5,
-        out_specs=(spec(),) * 7,
+        in_specs=[spec(SMEM)] + [spec()] * 4 + [spec(ANY)] * 7,
+        out_specs=(spec(ANY),) * 8 + (spec(),) * 6,
         scratch_shapes=[
             pltpu.VMEM((7, BT, BT), full),
             pltpu.VMEM((count, BT, BT), full),
             pltpu.VMEM((count, BT, BT), full),
             pltpu.VMEM((count, BT, BT), full),
             pltpu.VMEM((tokens, heads * DK), low),
+            pltpu.VMEM((tokens, heads * DK), low),
+            pltpu.VMEM((tokens, width), low),
+            pltpu.VMEM((tokens, model), low),
+            pltpu.VMEM((mixer.shape[0] * n_fsdp, width), low),
+            pltpu.SemaphoreType.DMA((gathers,)),
+            pltpu.SemaphoreType.DMA((gathers,)),
+            pltpu.SemaphoreType.DMA((shares,)),
+            pltpu.SemaphoreType.DMA((shares,)),
+            pltpu.SemaphoreType.DMA((11,)),
         ],
-        compiler_params=pltpu.CompilerParams(vmem_limit_bytes=56 << 20),
+        compiler_params=pltpu.CompilerParams(
+            vmem_limit_bytes=60 << 20, collective_id=1, has_side_effects=True
+        ),
         name="mixer_forward",
-    )(retain, column, row, proj, taps, gain)
+    )(retain, column, row, taps, gain, normed, mixer, gate, up, down, out, cot)
 
 
 def mixer_backward_kernel(
@@ -585,29 +922,37 @@
 
     inputs = tokens.astype(jnp.float32)
     normed_f, unit_one, inv_one = rms_forward(inputs, norm_gain)
-    normed = gather(normed_f.astype(jnp.bfloat16), "seq")
-    cot_all = gather(cotangent, "seq")
-    group_tokens = normed.shape[0]
-    w_mixer = gather(
-        jnp.concatenate(
-            [own_slice(array, place, width, 1) for array in (w_query, w_key, w_value)]
-            + [jnp.pad(own_slice(w_beta, place, heads, 1), ((0, 0), (0, DK - heads)))],
-            axis=1,
-        ),
-        "fsdp",
-    )
-    full_o = gather(w_out, "fsdp")
-    full_gate = gather(pick_units(w_gate), "fsdp")
-    full_up = gather(pick_units(w_up), "fsdp")
-    full_down = gather(own_slice(w_down, place, slab, 0), "fsdp")
-
-    proj = matmul(normed, w_mixer).astype(jnp.bfloat16)
+    group_tokens = tokens.shape[0] * n_seq
+    mixer_shard = jnp.concatenate(
+        [own_slice(array, place, width, 1) for array in (w_query, w_key, w_value)]
+        + [jnp.pad(own_slice(w_beta, place, heads, 1), ((0, 0), (0, DK - heads)))],
+        axis=1,
+    )
     retain = retains(seq_lengths[0], group_tokens)
     column, row = token_order.reshape(-1, 1), token_order.reshape(1, -1)
     taps = own_slice(conv_taps, place, width, 2).reshape(3 * CONV, width)
     gain = head_gain.reshape(1, DK)
-    mixed, *saved = mixer_forward(retain, column, row, proj, taps, gain)
-    mixed_tok = lax.all_to_all(mixed, "seq", split_axis=0, concat_axis=1, tiled=True)
+    mixed_tok, normed, w_mixer, full_gate, full_up, full_down, full_o, cot_all, *saved = (
+        mixer_forward(
+            n_seq,
+            n_fsdp,
+            retain,
+            column,
+            row,
+            taps,
+            gain,
+            (
+                normed_f.astype(jnp.bfloat16),
+                mixer_shard,
+                pick_units(w_gate),
+                pick_units(w_up),
+                own_slice(w_down, place, slab, 0),
+                w_out,
+                cotangent,
+            ),
+        )
+    )
+    full_down = full_down.reshape(units, model)
     hidden = inputs + matmul(mixed_tok, full_o)
     second_f, unit_two, inv_two = rms_forward(hidden, ffn_gain)
     second = gather(second_f.astype(jnp.bfloat16), "seq")

time: 890 us -> 725 us (0.81)
  waiting for transfers between devices: 453 us -> 256 us
  Pallas kernels: 109 us -> 170 us
  matrix products: 102 us -> 79.4 us
    all_gather x8 -> x1, waiting for transfers between devices: 228 us -> 40.1 us  [gather(): return lax.all_gather(array, axis_name, axis=axis, tiled=True)]
    pallas_call x1, Pallas kernels: 48.8 us -> 110 us  [mixer_forward(): pl.pallas_call(functools.partial(mixer_forward_kernel, heads, n_seq, n_fs...]
    dot_general x5 -> x4, matrix products: 40.5 us -> 19.3 us  [matmul(): lax.dot_general(first, second, NN, preferred_element_type=jnp.float32)]
    all_to_all x1 -> x0, waiting for transfers between devices: 14.4 us -> none  [local(): lax.all_to_all(mixed, 'seq', split_axis=0, concat_axis=1, tiled=True)]
    unnamed x16 -> x9, waiting for transfers between devices: 30.6 us -> 35.6 us
  transfers between devices with their start and end apart: 18 -> 10, of which waited for: 14 -> 7; matrix products, arithmetic and copies ran while one was open for 14% -> 11% of each run, Pallas kernels for 12% -> 8%
where the time goes in v2:
time: 725 us; the launch traced here: 716 us
  waiting for transfers between devices  256 us (35%)
  Pallas kernels  170 us (23%)
  blocking collectives  118 us (16%)
  matrix products  79.4 us (11%)
  local copies, waits for them, and re-layouts  35.3 us (5%)
  other arithmetic  26.3 us (4%)
  starting transfers between devices  15.7 us (2%)
  between operations  15 us (2%)
    pallas_call x1, Pallas kernels, mixer_forward(): pl.pallas_call(functools.partial(mixer_forward_kernel, heads, n_seq, n_fs...  110 us
    reduce_scatter x3, waiting for transfers between devices, scatter(): lax.psum_scatter(array.astype(jnp.bfloat16), 'fsdp', scatter_dimension=0,...  95.4 us
    all_to_all x3, waiting for transfers between devices, spread(): lax.all_to_all(partial.astype(jnp.bfloat16).reshape(n_seq, -1, model), 's...  85.3 us
    all_gather x4, blocking collectives, gather(): return lax.all_gather(array, axis_name, axis=axis, tiled=True)  60.7 us
    pallas_call x1, Pallas kernels, mixer_backward(): pl.pallas_call(functools.partial(mixer_backward_kernel, heads), out_shape...  59.8 us
    psum x1, blocking collectives, local(): lax.psum((grad_norm_gain, grad_ffn_gain, grad_gain[0], conv_full), ('seq'...  40.2 us
    all_gather x1, waiting for transfers between devices, gather(): return lax.all_gather(array, axis_name, axis=axis, tiled=True)  40.1 us
    unnamed x9, waiting for transfers between devices  35.6 us
  transfers between devices with their start and end apart: 10, of which 7 were waited for; matrix products, arithmetic and copies ran while one was open for 11% of the time, Pallas kernels for 8%

profile of v2, /device:TPU:0, one launch (start us, length us, event | category | flops | bytes accessed | tf_op | source)
XLA Modules:
  0.0 716.5 jit_solution(11714015361459871124)
XLA Ops:
  25.2 110.1 %mixer_forward.1 = (bf16[512,1024]{1,0:T(8,128)(2,1)}, bf16[2048,1024]{1,0:T(8,128)(2,1)}, bf16[1024,896]{1,0:T(8,128)(2,1)}, bf16[1024,704]{1,0:T(8,128)(2,1)},...) custom-call(f32[34]{0:T(128)} %pad.8.retain_ref, ...), custom_call_target="tpu_custom_call" | custom-call | tf_op jit(solution)/shard_map/mixer_forward/pallas_call | solution.py:559
  141.2 40.1 %all-gather.5.cloned.1.call-done = bf16[2048,1024]{1,0:T(8,128)(2,1)} async-done(((bf16[512,1024]{1,0:T(8,128)(2,1)}), bf16[2048,1024]{1,0:T(8,128)(2,1)}) %all-gather.5.cloned.1.call-update) | async-done | bytes 4194320 | tf_op jit(solution)/shard_map/all_gather | solution.py:917
  181.3 5.8 fusion.15
  190.4 7.1 multiply_convert_fusion
  197.5 3.5 fusion.17
  201.1 5.1 add_convert_fusion
  206.2 5.2 all-to-all-start.1
  211.4 6.9 convolution_convert_fusion
  218.4 41.3 %all-to-all-done.1 = bf16[4,512,1024]{2,1,0:T(8,128)(2,1)} async-done(((bf16[4,512,1024]{2,1,0:T(8,128)(2,1)}), bf16[4,512,1024]{2,1,0:T(8,128)(2,1)}, u32[]{:S(2)}, u32[]{:S(2)}) %all-to-all-start.1) | async-done | bytes 4194336 | tf_op jit(solution)/shard_map/all_to_all | solution.py:970
  259.7 4.8 all-to-all-start
  264.6 3.4 convert_reduce_fusion.1
  268.7 44.0 %all-to-all-done = bf16[4,512,1024]{2,1,0:T(8,128)(2,1)} async-done(((bf16[4,512,1024]{2,1,0:T(8,128)(2,1)}), bf16[4,512,1024]{2,1,0:T(8,128)(2,1)}, u32[]{:S(2)}, u32[]{:S(2)}) %all-to-all-start) | async-done | bytes 4194336 | tf_op jit(solution)/shard_map/all_to_all | solution.py:970
  312.7 3.6 convert_reduce_fusion.2
  318.7 4.2 convolution_convert_fusion.2
  323.0 6.2 convolution_convert_fusion.5
  330.9 6.2 convolution_convert_fusion.4
  339.0 7.5 %convolution_convert_fusion.6 = bf16[704,1024]{1,0:T(8,128)(2,1)} fusion(bf16[2048,704]{0,1:T(8,128)(2,1)} %get-tuple-element.114, bf16[2048,1024]{1,0:T(8,128)(2,1)} %get-tuple-element.36), kind=kOutput, calls=%fused_computation.34 | convolution fusion | flops 2953510912 | bytes 8519680 | tf_op jit(solution)/shard_map/dot_general | solution.py:856
  349.5 17.6 %all_to_all.34 = bf16[512,4,256]{2,0,1:T(8,128)(2,1)} all-to-all(bf16[512,4,256]{2,0,1:T(8,128)(2,1)S(1)} %bitcast.80), channel_id=1, replica_groups=mesh['seq'=4,'fsdp'=8] {'seq'}, dimensions={1} | all-to-all | bytes 2097152 | tf_op jit(solution)/shard_map/all_to_all | solution.py:986
  367.1 59.8 %mixer_backward.1 = (bf16[2048,896]{1,0:T(8,128)(2,1)}, f32[12,256]{1,0:T(8,128)}, f32[1,128]{1,0:T(1,128)}) custom-call(f32[34]{0:T(128)} %pad.8.retain_ref, s32[2048,1]{1,0:T(8,128)} %copy.89.column_ref, s32[1,2048]{1,0:T(1,128)} %row_ref.3, bf16[2048,256]{1,0:T(8,128)(2,1)} %bitcast.76, bf16[2064,896]{1,0:T(8,128)(2,1)} %get-tuple-element.37.packed_ref, ...), custom_call_target="tpu_custom_call" | custom-call | tf_op jit(solution)/shard_map/mixer_backward/pallas_call | solution.py:826
  426.9 8.2 %convolution_convert_fusion.1 = bf16[2048,1024]{1,0:T(8,128)(2,1)} fusion(bf16[2048,896]{1,0:T(8,128)(2,1)} %get-tuple-element.43, bf16[1024,896]{1,0:T(8,128)(2,1)S(1)} %copy-done.14), kind=kOutput, calls=%fused_computation.9 | convolution fusion | flops 3760193536 | bytes 9699328 | tf_op jit(solution)/shard_map/dot_general | solution.py:852
  435.1 4.8 all-to-all-start.3
  440.9 9.1 %convolution_convert_fusion.3 = bf16[1024,896]{1,0:T(8,128)(2,1)} fusion(bf16[2048,1024]{1,0:T(8,128)(2,1)} %get-tuple-element.45, bf16[2048,896]{1,0:T(8,128)(2,1)} %get-tuple-element.43), kind=kOutput, calls=%fused_computation.31 | convolution fusion | flops 3759013888 | bytes 9699328 | tf_op jit(solution)/shard_map/dot_general | solution.py:856
  450.0 8.3 %reduce-scatter.16.cloned.1.call-done = bf16[128,704]{1,0:T(8,128)(2,1)} async-done(((bf16[1024,704]{1,0:T(8,128)(2,1)}), bf16[128,704]{1,0:T(8,128)(2,1)}) %reduce-scatter.16.cloned.1.call-update) | async-done | bytes 180240
  459.4 33.9 %all-gather.1 = bf16[512,704]{0,1:T(8,128)(2,1)} all-gather(bf16[128,704]{0,1:T(8,128)(2,1)S(1)} %copy.103), channel_id=3, replica_groups=mesh['seq'=4,'fsdp'=8] {'seq'}, dimensions={0}, use_global_device_ids=true | all-gather | bytes 901120 | tf_op jit(solution)/shard_map/all_gather | solution.py:917
  499.1 26.7 %reduce-scatter.18.cloned.1.call-done = bf16[128,704]{1,0:T(8,128)(2,1)} async-done(((bf16[1024,704]{1,0:T(8,128)(2,1)}), bf16[128,704]{1,0:T(8,128)(2,1)}) %reduce-scatter.18.cloned.1.call-update) | async-done | bytes 180240
  526.9 8.7 %all-gather.2 = bf16[512,704]{0,1:T(8,128)(2,1)} all-gather(bf16[128,704]{0,1:T(8,128)(2,1)S(1)} %copy.105), channel_id=4, replica_groups=mesh['seq'=4,'fsdp'=8] {'seq'}, dimensions={0}, use_global_device_ids=true | all-gather | bytes 901120 | tf_op jit(solution)/shard_map/all_gather | solution.py:917
  541.4 51.5 %reduce-scatter.14.cloned.1.call-done = bf16[88,1024]{1,0:T(8,128)(2,1)} async-done(((bf16[704,1024]{1,0:T(8,128)(2,1)}), bf16[88,1024]{1,0:T(8,128)(2,1)}) %reduce-scatter.14.cloned.1.call-update) | async-done | bytes 180240 | tf_op jit(solution)/shard_map/reduce_scatter | solution.py:990
  592.9 8.5 %all_gather.19 = bf16[352,1024]{1,0:T(8,128)(2,1)S(1)} all-gather(bf16[88,1024]{1,0:T(8,128)(2,1)} %reduce-scatter.14.cloned.1.call-done), channel_id=1, replica_groups=mesh['seq'=4,'fsdp'=8] {'seq'}, dimensions={0}, use_global_device_ids=true | all-gather | bytes 901120 | tf_op jit(solution)/shard_map/all_gather | solution.py:917
  606.8 40.2 %all-reduce.2 = (f32[1024]{0:T(1024)}, f32[3,4,1024]{2,1,0:T(4,128)}, f32[128]{0:T(128)}, f32[1024]{0:T(1024)}) all-reduce(f32[1024]{0:T(1024)S(1)} %get-tuple-element.106, f32[3,4,1024]{2,1,0:T(4,128)S(1)} %constant_dynamic-update-slice_fusion, f32[128]{0:T(128)S(1)} %bitcast.94, ...), channel_id=1, replica_groups=mesh['seq'=4,'fsdp'=8] {'seq','fsdp'}, use_global_device_ids=true, to_apply=%region_10.11 | all-reduce | flops 14464 | bytes 115712 | tf_op jit(solution)/shard_map/psum | solution.py:1031
  646.9 3.4 fusion.8
  652.2 43.9 %reduce-scatter.10.cloned.1.call-done = bf16[128,896]{1,0:T(8,128)(2,1)} async-done(((bf16[1024,896]{1,0:T(8,128)(2,1)}), bf16[128,896]{1,0:T(8,128)(2,1)}) %reduce-scatter.10.cloned.1.call-update) | async-done | bytes 229392 | tf_op jit(solution)/shard_map/reduce_scatter | solution.py:990
  696.1 9.5 %all-gather = bf16[512,896]{1,0:T(8,128)(2,1)S(1)} all-gather(bf16[128,896]{1,0:T(8,128)(2,1)} %reduce-scatter.10.cloned.1.call-done), channel_id=2, replica_groups=mesh['seq'=4,'fsdp'=8] {'seq'}, dimensions={0}, use_global_device_ids=true | all-gather | bytes 1146880 | tf_op jit(solution)/shard_map/all_gather | solution.py:917
  (117 shorter events, 62.1 us)
Async XLA Ops:
  7.2 16.6 %copy-start = (bf16[352,1024]{1,0:T(8,128)(2,1)S(1)}, bf16[352,1024]{1,0:T(8,128)(2,1)}, u32[]{:S(2)}) copy-start(bf16[352,1024]{1,0:T(8,128)(2,1)} %param.28) | copy-start | bytes 2162692
  7.2 174.1 %all-gather.5.cloned.1.call-start = ((), (), s32[]{:S(2)}) async-start(), calls=%async_computation.9 | async-start | bytes 5242880 | tf_op jit(solution)/shard_map/all_gather | solution.py:917
  14.7 6.9 copy-start.5
  14.7 6.9 copy-start.8
  135.4 4.6 copy-start.7
  138.6 1.3 copy-start.2
  140.0 41.3 %copy-start.16 = (bf16[1024,704]{1,0:T(8,128)(2,1)S(1)}, bf16[1024,704]{1,0:T(8,128)(2,1)}, u32[]{:S(2)}) copy-start(bf16[1024,704]{1,0:T(8,128)(2,1)} %get-tuple-element.33) | copy-start | bytes 4325380
  181.3 5.8 copy-start.12
  181.3 5.8 copy-start.15
  187.1 3.3 copy-start.11
  187.1 3.3 copy-start.17
  197.5 3.5 copy-start.20
  197.5 3.5 copy-start.21
  206.2 5.2 copy-start.18
  206.2 53.4 %all-to-all-start.1 = ((bf16[4,512,1024]{2,1,0:T(8,128)(2,1)}), bf16[4,512,1024]{2,1,0:T(8,128)(2,1)}, u32[]{:S(2)}, u32[]{:S(2)}) async-start(bf16[4,512,1024]{2,1,0:T(8,128)(2,1)} %bitcast.79), calls=%async_computation.1 | async-start | bytes 8388608 | tf_op jit(solution)/shard_map/all_to_all | solution.py:970
  259.7 53.1 %all-to-all-start = ((bf16[4,512,1024]{2,1,0:T(8,128)(2,1)}), bf16[4,512,1024]{2,1,0:T(8,128)(2,1)}, u32[]{:S(2)}, u32[]{:S(2)}) async-start(bf16[4,512,1024]{2,1,0:T(8,128)(2,1)} %bitcast.78), calls=%async_computation | async-start | bytes 8388608 | tf_op jit(solution)/shard_map/all_to_all | solution.py:970
  264.5 175.5 %reduce-scatter.12.cloned.1.call-start = ((), (), s32[]{:S(2)}) async-start(), calls=%async_computation.11 | async-start | bytes 2359296 | tf_op jit(solution)/shard_map/reduce_scatter | solution.py:990
  264.6 3.5 copy-start.3
  312.7 3.6 copy-start.4
  312.7 3.6 copy-start.6
  316.3 2.4 copy-start.19
  323.0 135.3 %reduce-scatter.16.cloned.1.call-start = ((), (), s32[]{:S(2)}) async-start(), calls=%async_computation.14 | async-start | bytes 1769472
  330.8 195.0 %reduce-scatter.18.cloned.1.call-start = ((), (), s32[]{:S(2)}) async-start(), calls=%async_computation.15 | async-start | bytes 1769472
  338.7 7.8 %copy-start.13 = (bf16[1024,1024]{1,0:T(8,128)(2,1)S(1)}, bf16[1024,1024]{1,0:T(8,128)(2,1)}, u32[]{:S(2)}) copy-start(bf16[1024,1024]{1,0:T(8,128)(2,1)} %get-tuple-element.32) | copy-start | bytes 6291460
  338.7 254.2 %reduce-scatter.14.cloned.1.call-start = ((), (), s32[]{:S(2)}) async-start(), calls=%async_computation.13 | async-start | bytes 1622016 | tf_op jit(solution)/shard_map/reduce_scatter | solution.py:990
  367.1 59.8 %copy-start.14 = (bf16[1024,896]{1,0:T(8,128)(2,1)S(1)}, bf16[1024,896]{1,0:T(8,128)(2,1)}, u32[]{:S(2)}) copy-start(bf16[1024,896]{1,0:T(8,128)(2,1)} %get-tuple-element.44) | copy-start | bytes 5505028
  435.1 167.6 %all-to-all-start.3 = ((bf16[4,512,1024]{2,1,0:T(8,128)(2,1)}), bf16[4,512,1024]{2,1,0:T(8,128)(2,1)}, u32[]{:S(2)}, u32[]{:S(2)}) async-start(bf16[4,512,1024]{2,1,0:T(8,128)(2,1)} %bitcast.77), calls=%async_computation.3 | async-start | bytes 8388608 | tf_op jit(solution)/shard_map/all_to_all | solution.py:970
  440.0 210.4 %all-reduce.5.cloned.1.call-start = ((), (), s32[]{:S(2)}) async-start(), calls=%async_computation.12 | async-start | bytes 524288 | tf_op jit(solution)/shard_map/psum | solution.py:1027
  440.6 255.5 %reduce-scatter.10.cloned.1.call-start = ((), (), s32[]{:S(2)}) async-start(), calls=%async_computation.10 | async-start | bytes 2064384 | tf_op jit(solution)/shard_map/reduce_scatter | solution.py:990
  541.4 61.3 %copy-start.9 = (f32[12,256]{1,0:T(8,128)S(1)}, f32[12,256]{1,0:T(8,128)}, u32[]{:S(2)}) copy-start(f32[12,256]{1,0:T(8,128)} %get-tuple-element.46) | copy-start | bytes 36868
  606.1 0.7 copy-start.10
  705.7 3.4 copy-start.1
Sparse Core Ops, SparseCore 0:
  141.3 39.9 all-gather.4
  323.1 67.6 reduce-scatter.11
  394.3 63.9 reduce-scatter.15
  462.0 63.8 reduce-scatter.17
  529.1 63.7 reduce-scatter.13
  595.1 31.0 all-reduce.4
  630.0 65.9 reduce-scatter.9

commit v3 on v2

--- a/solution.py
+++ b/solution.py
@@ -844,6 +844,357 @@
     )(retain, column, row, grad_mixed, packed, taps, gain, delta, inverse, big, update, state)
 
 
+class Wire:
+    def __init__(self, send, recv):
+        self.send, self.recv, self.used = send, recv, 0
+
+    def copy(self, source, target, seq, fsdp):
+        index = self.used
+        self.used += 1
+        return pltpu.make_async_remote_copy(
+            src_ref=source,
+            dst_ref=target,
+            send_sem=self.send.at[index],
+            recv_sem=self.recv.at[index],
+            device_id=(seq, fsdp),
+            device_id_type=MESH,
+        )
+
+
+def ffn_copies(n_seq, parts):
+    chips = n_seq // 2
+    return parts * (2 + 4 * (chips - 1)) + parts * (n_seq - 1)
+
+
+def ffn_kernel(
+    n_seq,
+    n_fsdp,
+    tokens_ref,
+    mixed_ref,
+    out_ref,
+    gain_ref,
+    gate_in,
+    up_in,
+    down_in,
+    cot_in,
+    hidden_ref,
+    grad_hidden_ref,
+    heads_ref,
+    result_ref,
+    grad_gate_ref,
+    grad_up_ref,
+    grad_down_ref,
+    grad_out_ref,
+    grad_gain_ref,
+    gate_ref,
+    up_ref,
+    down_ref,
+    cot_ref,
+    second_ref,
+    second_t_ref,
+    active_t_ref,
+    lin_gate_ref,
+    lin_up_ref,
+    keep_ref,
+    give_ref,
+    from_mate_ref,
+    reduce_ref,
+    from_far_ref,
+    attn_ref,
+    mixed_grad_ref,
+    stage_ref,
+    send_sems,
+    recv_sems,
+    local_sems,
+):
+    own, model = tokens_ref.shape
+    group = own * n_seq
+    part = min(PB, own)
+    parts = own // part
+    chips = n_seq // 2
+    seq, fsdp = lax.axis_index("seq"), lax.axis_index("fsdp")
+    mate = seq + 1 - 2 * (seq % 2)
+    units = gate_ref.shape[1]
+    low = jnp.bfloat16
+
+    loads = [
+        pltpu.make_async_copy(source, target, local_sems.at[index])
+        for index, (source, target) in enumerate(
+            ((gate_in, gate_ref), (up_in, up_ref), (down_in, down_ref), (cot_in, cot_ref))
+        )
+    ]
+    for load in loads:
+        load.start()
+
+    wire = Wire(send_sems, recv_sems)
+
+    def far(step):
+        return (seq + n_seq - 2 * step) % n_seq
+
+    def rows(ref, shard, index):
+        return ref.at[pl.ds(aligned(shard * own + index * part, part), part)]
+
+    def local_rows(ref, index):
+        return ref.at[pl.ds(index * part, part)]
+
+    to_mate, across, passed, give_mate, give_far, reduced = {}, {}, {}, {}, {}, {}
+    for index in range(parts):
+        mine = rows(second_ref, seq, index)
+        to_mate[index] = wire.copy(mine, mine, mate, fsdp)
+        give_mate[index] = wire.copy(
+            local_rows(give_ref.at[0], index), local_rows(from_mate_ref.at[0], index), mate, fsdp
+        )
+        for step in range(1, chips):
+            across[step, index] = wire.copy(mine, mine, (seq + 2 * step) % n_seq, fsdp)
+            there = rows(second_ref, far(step), index)
+            passed[step, index] = wire.copy(there, there, mate, fsdp)
+            give_far[step, index] = wire.copy(
+                local_rows(give_ref.at[step], index),
+                local_rows(from_mate_ref.at[step], index),
+                mate,
+                fsdp,
+            )
+            reduced[step, index] = wire.copy(
+                local_rows(reduce_ref.at[step - 1], index),
+                local_rows(from_far_ref.at[step - 1], index),
+                far(step),
+                fsdp,
+            )
+
+    greet_near(n_seq)
+
+    for index in range(parts):
+        at = slice(index * part, index * part + part)
+        hidden = tokens_ref[at, :].astype(jnp.float32) + bdot(mixed_ref[at, :], out_ref[...])
+        hidden_ref[at, :] = hidden
+        inv = lax.rsqrt(jnp.mean(hidden * hidden, axis=1, keepdims=True) + EPS_NORM)
+        second_ref[pl.ds(aligned(seq * own + index * part, part), part), :] = (
+            hidden * inv * gain_ref[...]
+        ).astype(low)
+        for step in range(1, chips):
+            across[step, index].start()
+        to_mate[index].start()
+    for load in loads:
+        load.wait()
+
+    count = n_seq * parts
+
+    def block(number, carry):
+        near = number < 2 * parts
+        late = number - 2 * parts
+        step_at = late // (2 * parts) + 1
+        rest = late % (2 * parts)
+        far_at = (seq + 2 * n_seq - 2 * step_at) % n_seq
+        far_mate = far_at + 1 - 2 * (far_at % 2)
+        shard = jnp.where(
+            near,
+            jnp.where(number < parts, seq, mate),
+            jnp.where(rest % 2 == 0, far_mate, far_at),
+        )
+        index_at = jnp.where(near, number % parts, rest // 2)
+        base = aligned(shard * own + index_at * part, part)
+
+        for index in range(parts):
+
+            @pl.when(number == parts + index)
+            def _():
+                to_mate[index].wait_recv()
+
+            for step in range(1, chips):
+
+                @pl.when(number == 2 * parts * step + 2 * index)
+                def _():
+                    across[step, index].wait_recv()
+                    passed[step, index].start()
+                    passed[step, index].wait_recv()
+
+        second = second_ref[pl.ds(base, part), :]
+        second_t_ref[:, pl.ds(base, part)] = second.T
+        gate_lin = bdot(second, gate_ref[...])
+        up_lin = bdot(second, up_ref[...])
+        cot = cot_ref[pl.ds(base, part), :]
+        grad_active = bdot(cot, down_ref[...], NT)
+        gate_sig = sigmoid(gate_lin)
+        silu = gate_lin * gate_sig
+        active = (silu * up_lin).astype(low)
+        active_t_ref[:, pl.ds(base, part)] = active.T
+        grad_gate = (grad_active * up_lin * (gate_sig + silu * (1.0 - gate_sig))).astype(low)
+        grad_up = (grad_active * silu).astype(low)
+        lin_gate_ref[pl.ds(base, part), :] = grad_gate
+        lin_up_ref[pl.ds(base, part), :] = grad_up
+        grad_second = bdot(grad_gate, gate_ref[...], NT) + bdot(grad_up, up_ref[...], NT)
+        stage_ref[...] = grad_second
+        result_ref[pl.ds(base, part), :] = bdot(active, down_ref[...]).astype(low)
+
+        for index in range(parts):
+            at = slice(index * part, index * part + part)
+
+            @pl.when(number == index)
+            def _():
+                keep_ref[at, :] = stage_ref[...]
+
+            @pl.when(number == parts + index)
+            def _():
+                give_ref[0, at, :] = stage_ref[...].astype(low)
+                give_mate[index].start()
+
+            for step in range(1, chips):
+
+                @pl.when(number == 2 * parts * step + 2 * index)
+                def _():
+                    give_ref[step, at, :] = stage_ref[...].astype(low)
+                    give_far[step, index].start()
+
+                @pl.when(number == 2 * parts * step + 2 * index + 1)
+                def _():
+                    give_far[step, index].wait_recv()
+                    reduce_ref[step - 1, at, :] = (
+                        stage_ref[...] + from_mate_ref[step, at, :].astype(jnp.float32)
+                    ).astype(low)
+                    reduced[step, index].start()
+
+        return carry
+
+    lax.fori_loop(0, count, block, 0)
+
+    tile = 256
+
+    def down_tile(number, carry):
+        base = aligned(number * tile, tile)
+        grad_down_ref[:, pl.ds(base, tile)] = bdot(
+            active_t_ref[...], cot_ref[:, pl.ds(base, tile)]
+        ).astype(low)
+        return carry
+
+    lax.fori_loop(0, model // tile, down_tile, 0)
+
+    grad_gain_ref[...] = jnp.zeros(grad_gain_ref.shape, jnp.float32)
+    width = model // n_seq
+    handed = []
+    for index in range(parts):
+        at = slice(index * part, index * part + part)
+        give_mate[index].wait_recv()
+        total = keep_ref[at, :] + from_mate_ref[0, at, :].astype(jnp.float32)
+        for step in range(1, chips):
+            reduced[step, index].wait_recv()
+            total = total + from_far_ref[step - 1, at, :].astype(jnp.float32)
+        hidden = hidden_ref[at, :]
+        inv = lax.rsqrt(jnp.mean(hidden * hidden, axis=1, keepdims=True) + EPS_NORM)
+        unit = hidden * inv
+        grad_gain_ref[...] += jnp.sum(total * unit, axis=0, keepdims=True)
+        grad_unit = total * gain_ref[...]
+        grad_hidden = inv * (
+            grad_unit - unit * jnp.mean(grad_unit * unit, axis=1, keepdims=True)
+        ) + cot_ref[pl.ds(aligned(seq * own + index * part, part), part), :].astype(jnp.float32)
+        grad_hidden_ref[at, :] = grad_hidden
+        attn = grad_hidden.astype(low)
+        attn_ref[at, :] = attn
+        mixed_grad_ref[at, :] = bdot(attn, out_ref[...], NT).astype(low)
+        for shift in range(1, n_seq):
+            target = (seq + shift) % n_seq
+            copy = wire.copy(
+                mixed_grad_ref.at[at, pl.ds(aligned(target * width, width), width)],
+                rows(heads_ref, seq, index),
+                target,
+                fsdp,
+            )
+            copy.start()
+            handed.append(copy)
+        heads_ref[pl.ds(aligned(seq * own + index * part, part), part), :] = mixed_grad_ref[
+            at, pl.ds(aligned(seq * width, width), width)
+        ]
+
+    def wide_tile(number, carry):
+        base = aligned(number * tile, tile)
+        turned = second_t_ref[pl.ds(base, tile), :]
+        grad_gate_ref[pl.ds(base, tile), :] = bdot(turned, lin_gate_ref[...]).astype(low)
+        grad_up_ref[pl.ds(base, tile), :] = bdot(turned, lin_up_ref[...]).astype(low)
+        return carry
+
+    lax.fori_loop(0, model // tile, wide_tile, 0)
+    for base in range(0, model, tile):
+        grad_out_ref[base : base + tile, :] = bdot(
+            mixed_ref[:, base : base + tile], attn_ref[...], TN
+        ).astype(low)
+
+    for index in range(parts):
+        to_mate[index].wait_send()
+        give_mate[index].wait_send()
+        for step in range(1, chips):
+            across[step, index].wait_send()
+            passed[step, index].wait_send()
+            give_far[step, index].wait_send()
+            reduced[step, index].wait_send()
+    for copy in handed:
+        copy.wait()
+
+
+def greet_near(n_seq):
+    seq, fsdp = lax.axis_index("seq"), lax.axis_index("fsdp")
+    barrier = pltpu.get_barrier_semaphore()
+    for step in range(1, n_seq):
+        pl.semaphore_signal(
+            barrier, inc=1, device_id=((seq + step) % n_seq, fsdp), device_id_type=MESH
+        )
+    pl.semaphore_wait(barrier, n_seq - 1)
+
+
+def ffn_block(n_seq, n_fsdp, tokens, mixed, out, gain, gate, up, down, cot):
+    own, model = tokens.shape
+    group = own * n_seq
+    units = gate.shape[1]
+    chips = n_seq // 2
+    low, full = jnp.bfloat16, jnp.float32
+    part = min(PB, own)
+    copies = ffn_copies(n_seq, own // part)
+
+    def shape(dims, kind=low):
+        return jax.ShapeDtypeStruct(dims, kind)
+
+    return pl.pallas_call(
+        functools.partial(ffn_kernel, n_seq, n_fsdp),
+        out_shape=(
+            shape((own, model), full),
+            shape((own, model), full),
+            shape((group, model // n_seq)),
+            shape((group, model)),
+            shape((model, units)),
+            shape((model, units)),
+            shape((units, model)),
+            shape((model, model)),
+            shape((1, model), full),
+        ),
+        in_specs=[spec()] * 4 + [spec(ANY)] * 4,
+        out_specs=(spec(),) * 9,
+        scratch_shapes=[
+            pltpu.VMEM((model, units), low),
+            pltpu.VMEM((model, units), low),
+            pltpu.VMEM((units, model), low),
+            pltpu.VMEM((group, model), low),
+            pltpu.VMEM((group, model), low),
+            pltpu.VMEM((model, group), low),
+            pltpu.VMEM((units, group), low),
+            pltpu.VMEM((group, units), low),
+            pltpu.VMEM((group, units), low),
+            pltpu.VMEM((own, model), full),
+            pltpu.VMEM((chips, own, model), low),
+            pltpu.VMEM((chips, own, model), low),
+            pltpu.VMEM((chips - 1, own, model), low),
+            pltpu.VMEM((chips - 1, own, model), low),
+            pltpu.VMEM((own, model), low),
+            pltpu.VMEM((own, model), low),
+            pltpu.VMEM((part, model), full),
+            pltpu.SemaphoreType.DMA((copies,)),
+            pltpu.SemaphoreType.DMA((copies,)),
+            pltpu.SemaphoreType.DMA((4,)),
+        ],
+        compiler_params=pltpu.CompilerParams(
+            vmem_limit_bytes=63 << 20, collective_id=2, has_side_effects=True
+        ),
+        name="ffn",
+    )(tokens, mixed, out, gain, gate, up, down, cot)
+
+
 def matmul(first, second):
     return lax.dot_general(first, second, NN, preferred_element_type=jnp.float32)
 
@@ -953,18 +1304,29 @@
         )
     )
     full_down = full_down.reshape(units, model)
-    hidden = inputs + matmul(mixed_tok, full_o)
-    second_f, unit_two, inv_two = rms_forward(hidden, ffn_gain)
-    second = gather(second_f.astype(jnp.bfloat16), "seq")
-    gate_lin = matmul(second, full_gate)
-    upward = matmul(second, full_up)
-    sigmoid_gate = jax.nn.sigmoid(gate_lin)
-    active = (gate_lin * sigmoid_gate * upward).astype(jnp.bfloat16)
-    grad_active = times_transposed(cot_all, full_down)
-    grad_gate = (
-        grad_active * upward * sigmoid_gate * (1.0 + gate_lin * (1.0 - sigmoid_gate))
-    ).astype(jnp.bfloat16)
-    grad_upward = (grad_active * gate_lin * sigmoid_gate).astype(jnp.bfloat16)
+    (
+        hidden,
+        grad_hidden,
+        grad_heads,
+        result_part,
+        wide_gate,
+        wide_up,
+        wide_down,
+        wide_out,
+        grad_ffn_gain,
+    ) = ffn_block(
+        n_seq,
+        n_fsdp,
+        tokens,
+        mixed_tok,
+        full_o,
+        ffn_gain.reshape(1, model),
+        full_gate,
+        full_up,
+        full_down,
+        cot_all,
+    )
+    grad_ffn_gain = grad_ffn_gain[0]
 
     def spread(partial):
         pieces = lax.all_to_all(
@@ -976,26 +1338,16 @@
         )
         return jnp.sum(pieces.astype(jnp.float32), axis=0)
 
-    grad_second = spread(
-        times_transposed(grad_gate, full_gate) + times_transposed(grad_upward, full_up)
-    )
-    grad_hidden, grad_ffn_gain = rms_backward(grad_second, unit_two, inv_two, ffn_gain)
-    grad_hidden = grad_hidden + cotangent.astype(jnp.float32)
-    grad_attn = grad_hidden.astype(jnp.bfloat16)
-    grad_mixed = times_transposed(grad_attn, full_o).astype(jnp.bfloat16)
-    grad_heads = lax.all_to_all(grad_mixed, "seq", split_axis=1, concat_axis=0, tiled=True)
-    result = (hidden + spread(matmul(active, full_down))).astype(jnp.bfloat16)
+    result = (hidden + spread(result_part)).astype(jnp.bfloat16)
 
     def scatter(array):
         return lax.psum_scatter(
             array.astype(jnp.bfloat16), "fsdp", scatter_dimension=0, tiled=True
         )
 
-    part_gate = scatter(contract_rows(second, grad_gate))
-    part_up = scatter(contract_rows(second, grad_upward))
-    part_down = scatter(contract_rows(active, cot_all))
-    part_out = scatter(contract_rows(mixed_tok, grad_attn))
-
+    part_gate, part_up, part_down, part_out = (
+        scatter(array) for array in (wide_gate, wide_up, wide_down, wide_out)
+    )
     grad_proj, grad_taps, grad_gain = mixer_backward(
         retain, column, row, grad_heads, taps, gain, saved
     )

time: 725 us -> 591 us (0.82)
  waiting for transfers between devices: 256 us -> 150 us
  Pallas kernels: 170 us -> 238 us
  matrix products: 79.4 us -> 17.3 us
  local copies, waits for them, and re-layouts: 35.3 us -> 21.8 us
  other arithmetic: 26.3 us -> 16.5 us
    pallas_call x0 -> x1, Pallas kernels: none -> 67.1 us  [ffn_block(): pl.pallas_call(functools.partial(ffn_kernel, n_seq, n_fsdp), out_shape=(s...]
    all_to_all x3 -> x2, waiting for transfers between devices: 85.3 us -> 39 us  [spread(): lax.all_to_all(partial.astype(jnp.bfloat16).reshape(n_seq, -1, model), 's...]
    all_gather x1 -> x0, waiting for transfers between devices: 40.1 us -> none  [gather(): return lax.all_gather(array, axis_name, axis=axis, tiled=True)]
    unnamed x9 -> x6, waiting for transfers between devices: 35.6 us -> 1.96 us
    psum x1, waiting for transfers between devices: 0.01 us -> 32.5 us  [local(): sum_out = lax.psum(part_out, 'seq').astype(jnp.float32)]
    dot_general x5 -> x1, matrix products: 33.3 us -> 9.14 us  [contract_rows(): lax.dot_general(first, second, TN, preferred_element_type=jnp.float32)]
    dot_general x4 -> x0, matrix products: 19.3 us -> none  [matmul(): lax.dot_general(first, second, NN, preferred_element_type=jnp.float32)]
    dot_general x5 -> x1, matrix products: 26.8 us -> 8.19 us  [times_transposed(): lax.dot_general(first, second, NT, preferred_element_type=jnp.float32)]
  transfers between devices with their start and end apart: 10 -> 8, of which waited for: 7 -> 5; matrix products, arithmetic and copies ran while one was open for 11% -> 6% of each run, Pallas kernels for 8% -> 10%
where the time goes in v3:
time: 591 us; the launch traced here: 589 us
  Pallas kernels  238 us (40%)
  waiting for transfers between devices  150 us (25%)
  blocking collectives  120 us (20%)
  local copies, waits for them, and re-layouts  21.8 us (4%)
  matrix products  17.3 us (3%)
  other arithmetic  16.5 us (3%)
  between operations  14.7 us (2%)
  starting transfers between devices  10.3 us (2%)
    pallas_call x1, Pallas kernels, mixer_forward(): pl.pallas_call(functools.partial(mixer_forward_kernel, heads, n_seq, n_fs...  111 us
    all_gather x4, blocking collectives, gather(): return lax.all_gather(array, axis_name, axis=axis, tiled=True)  79.3 us
    reduce_scatter x5, waiting for transfers between devices, scatter(): lax.psum_scatter(array.astype(jnp.bfloat16), 'fsdp', scatter_dimension=0,...  76.8 us
    pallas_call x1, Pallas kernels, ffn_block(): pl.pallas_call(functools.partial(ffn_kernel, n_seq, n_fsdp), out_shape=(s...  67.1 us
    pallas_call x1, Pallas kernels, mixer_backward(): pl.pallas_call(functools.partial(mixer_backward_kernel, heads), out_shape...  59.9 us
    psum x1, blocking collectives, local(): lax.psum((grad_norm_gain, grad_ffn_gain, grad_gain[0], conv_full), ('seq'...  40.7 us
    all_to_all x2, waiting for transfers between devices, spread(): lax.all_to_all(partial.astype(jnp.bfloat16).reshape(n_seq, -1, model), 's...  39 us
    psum x1, waiting for transfers between devices, local(): sum_out = lax.psum(part_out, 'seq').astype(jnp.float32)  32.5 us
  transfers between devices with their start and end apart: 8, of which 5 were waited for; matrix products, arithmetic and copies ran while one was open for 6% of the time, Pallas kernels for 10%

profile of v3, /device:TPU:0, one launch (start us, length us, event | category | flops | bytes accessed | tf_op | source)
XLA Modules:
  0.0 588.5 jit_solution(1134561391602241981)
XLA Ops:
  10.3 1.5 copy.74
  11.9 1.5 copy.75
  14.1 1.7 copy.77.gate_in
  16.9 1.3 copy.76.column_ref
  18.5 0.9 constant_dynamic-slice_fusion.4
  20.1 1.3 fusion.4.normed_in
  22.6 110.6 %mixer_forward.1 = (bf16[512,1024]{1,0:T(8,128)(2,1)}, bf16[2048,1024]{1,0:T(8,128)(2,1)}, bf16[1024,896]{1,0:T(8,128)(2,1)}, bf16[1024,704]{1,0:T(8,128)(2,1)},...) custom-call(f32[34]{0:T(128)} %pad.8.retain_ref, ...), custom_call_target="tpu_custom_call" | custom-call | tf_op jit(solution)/shard_map/mixer_forward/pallas_call | solution.py:559
  133.2 67.1 %ffn.1 = (f32[512,1024]{1,0:T(8,128)}, f32[512,1024]{1,0:T(8,128)}, bf16[2048,256]{1,0:T(8,128)(2,1)}, bf16[2048,1024]{1,0:T(8,128)(2,1)}, bf16[1024,704]{1,0:T(...) custom-call(bf16[512,1024]{1,0:T(8,128)(2,1)} %tokens_ref.1, ...), custom_call_target="tpu_custom_call" | custom-call | tf_op jit(solution)/shard_map/ffn/pallas_call | solution.py:1154
  201.9 59.9 %mixer_backward.1 = (bf16[2048,896]{1,0:T(8,128)(2,1)}, f32[12,256]{1,0:T(8,128)}, f32[1,128]{1,0:T(1,128)}) custom-call(f32[34]{0:T(128)} %pad.8.retain_ref, s32[2048,1]{1,0:T(8,128)} %copy.76.column_ref, s32[1,2048]{1,0:T(1,128)} %row_ref.3, bf16[2048,256]{1,0:T(8,128)(2,1)} %get-tuple-element.48.grad_ref, bf16[2064,896]{1,0:T(8,128)(2,1)} %get-tuple-element.49.packed_ref, ...), custom_call_target="tpu_custom_call" | custom-call | tf_op jit(solution)/shard_map/mixer_backward/pallas_call | solution.py:826
  261.8 8.2 %convolution_convert_fusion = bf16[2048,1024]{1,0:T(8,128)(2,1)} fusion(bf16[2048,896]{1,0:T(8,128)(2,1)} %get-tuple-element.55, bf16[1024,896]{1,0:T(8,128)(2,1)S(1)} %copy-done.11), kind=kOutput, calls=%fused_computation.2 | convolution fusion | flops 3760193536 | bytes 9699328 | tf_op jit(solution)/shard_map/dot_general | solution.py:1203
  270.0 4.8 all-to-all-start.1
  275.1 9.1 %convolution_convert_fusion.1 = bf16[1024,896]{1,0:T(8,128)(2,1)} fusion(bf16[2048,1024]{1,0:T(8,128)(2,1)} %get-tuple-element.58, bf16[2048,896]{1,0:T(8,128)(2,1)} %get-tuple-element.55), kind=kOutput, calls=%fused_computation.17 | convolution fusion | flops 3759013888 | bytes 9699328 | tf_op jit(solution)/shard_map/dot_general | solution.py:1207
  284.2 39.0 %all-to-all-done.1 = bf16[4,512,1024]{2,1,0:T(8,128)(2,1)} async-done(((bf16[4,512,1024]{2,1,0:T(8,128)(2,1)}), bf16[4,512,1024]{2,1,0:T(8,128)(2,1)}, u32[]{:S(2)}, u32[]{:S(2)}) %all-to-all-start.1) | async-done | bytes 4194336 | tf_op jit(solution)/shard_map/all_to_all | solution.py:1332
  323.2 5.0 all-to-all-start
  329.1 52.4 %all-gather.1 = bf16[512,704]{1,0:T(8,128)(2,1)S(1)} all-gather(bf16[128,704]{1,0:T(8,128)(2,1)} %reduce-scatter.10.cloned.1.call-done), channel_id=3, replica_groups=mesh['seq'=4,'fsdp'=8] {'seq'}, dimensions={0}, use_global_device_ids=true | all-gather | bytes 901120 | tf_op jit(solution)/shard_map/all_gather | solution.py:1268
  382.4 1.5 copy.88
  383.9 8.9 %all-gather.2 = bf16[512,704]{1,0:T(8,128)(2,1)S(1)} all-gather(bf16[128,704]{1,0:T(8,128)(2,1)} %reduce-scatter.12.cloned.1.call-done), channel_id=4, replica_groups=mesh['seq'=4,'fsdp'=8] {'seq'}, dimensions={0}, use_global_device_ids=true | all-gather | bytes 901120 | tf_op jit(solution)/shard_map/all_gather | solution.py:1268
  393.7 1.5 copy.89
  395.3 11.6 %reduce-scatter.14.cloned.1.call-done = bf16[88,1024]{1,0:T(8,128)(2,1)} async-done(((bf16[704,1024]{1,0:T(8,128)(2,1)}), bf16[88,1024]{1,0:T(8,128)(2,1)}) %reduce-scatter.14.cloned.1.call-update) | async-done | bytes 180240 | tf_op jit(solution)/shard_map/reduce_scatter | solution.py:1344
  406.9 8.4 %all_gather.15 = bf16[352,1024]{1,0:T(8,128)(2,1)S(1)} all-gather(bf16[88,1024]{1,0:T(8,128)(2,1)} %reduce-scatter.14.cloned.1.call-done), channel_id=1, replica_groups=mesh['seq'=4,'fsdp'=8] {'seq'}, dimensions={0}, use_global_device_ids=true | all-gather | bytes 901120 | tf_op jit(solution)/shard_map/all_gather | solution.py:1268
  415.3 1.3 convert_element_type.49
  416.6 3.4 convert_reduce_fusion
  420.6 40.7 %all-reduce.2 = (f32[1024]{0:T(1024)}, f32[3,4,1024]{2,1,0:T(4,128)}, f32[128]{0:T(128)}, f32[1024]{0:T(1024)}) all-reduce(f32[1024]{0:T(1024)S(1)} %get-tuple-element.108, f32[3,4,1024]{2,1,0:T(4,128)S(1)} %constant_dynamic-update-slice_fusion, f32[128]{0:T(128)S(1)} %bitcast.63, ...), channel_id=1, replica_groups=mesh['seq'=4,'fsdp'=8] {'seq','fsdp'}, use_global_device_ids=true, to_apply=%region_7.8 | all-reduce | flops 14464 | bytes 115712 | tf_op jit(solution)/shard_map/psum | solution.py:1383
  461.4 3.6 convert_reduce_fusion.1
  465.0 1.3 add_convert_fusion
  466.9 1.9 fusion.8
  468.8 7.1 %reduce-scatter.6.cloned.1.call-done = bf16[128,896]{1,0:T(8,128)(2,1)} async-done(((bf16[1024,896]{1,0:T(8,128)(2,1)}), bf16[128,896]{1,0:T(8,128)(2,1)}) %reduce-scatter.6.cloned.1.call-update) | async-done | bytes 229392 | tf_op jit(solution)/shard_map/reduce_scatter | solution.py:1344
  475.9 9.5 %all-gather = bf16[512,896]{1,0:T(8,128)(2,1)S(1)} all-gather(bf16[128,896]{1,0:T(8,128)(2,1)} %reduce-scatter.6.cloned.1.call-done), channel_id=2, replica_groups=mesh['seq'=4,'fsdp'=8] {'seq'}, dimensions={0}, use_global_device_ids=true | all-gather | bytes 1146880 | tf_op jit(solution)/shard_map/all_gather | solution.py:1268
  485.7 0.9 copy.91
  488.3 58.1 %reduce-scatter.8.cloned.1.call-done = bf16[128,1024]{1,0:T(8,128)(2,1)} async-done(((bf16[1024,1024]{1,0:T(8,128)(2,1)}), bf16[128,1024]{1,0:T(8,128)(2,1)}) %reduce-scatter.8.cloned.1.call-update) | async-done | bytes 262160 | tf_op jit(solution)/shard_map/reduce_scatter | solution.py:1344
  547.1 32.5 %all-reduce.5.cloned.1.call-done = bf16[128,1024]{1,0:T(8,128)(2,1)} async-done(((bf16[128,1024]{1,0:T(8,128)(2,1)}), bf16[128,1024]{1,0:T(8,128)(2,1)}) %all-reduce.5.cloned.1.call-update) | async-done | bytes 262160 | tf_op jit(solution)/shard_map/psum | solution.py:1379
  579.6 1.8 convert_element_type.48
  (74 shorter events, 15.3 us)
Async XLA Ops:
  7.2 12.2 %copy-start = (bf16[352,1024]{1,0:T(8,128)(2,1)S(1)}, bf16[352,1024]{1,0:T(8,128)(2,1)}, u32[]{:S(2)}) copy-start(bf16[352,1024]{1,0:T(8,128)(2,1)} %param.28) | copy-start | bytes 2162692
  7.2 321.9 %reduce-scatter.10.cloned.1.call-start = ((), (), s32[]{:S(2)}) async-start(), calls=%async_computation.10 | async-start | bytes 1769472 | tf_op jit(solution)/shard_map/reduce_scatter | solution.py:1344
  10.3 6.3 %copy-start.2 = (bf16[512,1024]{1,0:T(8,128)(2,1)S(1)}, bf16[512,1024]{1,0:T(8,128)(2,1)}, u32[]{:S(2)}) copy-start(bf16[512,1024]{1,0:T(8,128)(2,1)} %tokens_ref.1) | copy-start | bytes 3145732
  11.9 5.1 copy-start.6
  13.3 4.9 copy-start.12
  13.4 6.7 %copy-start.7 = (f32[1024]{0:T(1024)S(1)}, f32[1024]{0:T(1024)}, u32[]{:S(2)}) copy-start(f32[1024]{0:T(1024)} %param.17) | copy-start | bytes 12292
  200.4 183.5 %reduce-scatter.12.cloned.1.call-start = ((), (), s32[]{:S(2)}) async-start(), calls=%async_computation.11 | async-start | bytes 1769472 | tf_op jit(solution)/shard_map/reduce_scatter | solution.py:1344
  201.1 205.7 %reduce-scatter.14.cloned.1.call-start = ((), (), s32[]{:S(2)}) async-start(), calls=%async_computation.12 | async-start | bytes 1622016 | tf_op jit(solution)/shard_map/reduce_scatter | solution.py:1344
  201.9 59.9 %copy-start.11 = (bf16[1024,896]{1,0:T(8,128)(2,1)S(1)}, bf16[1024,896]{1,0:T(8,128)(2,1)}, u32[]{:S(2)}) copy-start(bf16[1024,896]{1,0:T(8,128)(2,1)} %get-tuple-element.56) | copy-start | bytes 5505028
  270.0 53.3 %all-to-all-start.1 = ((bf16[4,512,1024]{2,1,0:T(8,128)(2,1)}), bf16[4,512,1024]{2,1,0:T(8,128)(2,1)}, u32[]{:S(2)}, u32[]{:S(2)}) async-start(bf16[4,512,1024]{2,1,0:T(8,128)(2,1)} %bitcast.47), calls=%async_computation.1 | async-start | bytes 8388608 | tf_op jit(solution)/shard_map/all_to_all | solution.py:1332
  274.8 201.1 %reduce-scatter.6.cloned.1.call-start = ((), (), s32[]{:S(2)}) async-start(), calls=%async_computation.7 | async-start | bytes 2064384 | tf_op jit(solution)/shard_map/reduce_scatter | solution.py:1344
  323.2 138.1 %all-to-all-start = ((bf16[4,512,1024]{2,1,0:T(8,128)(2,1)}), bf16[4,512,1024]{2,1,0:T(8,128)(2,1)}, u32[]{:S(2)}, u32[]{:S(2)}) async-start(bf16[4,512,1024]{2,1,0:T(8,128)(2,1)} %bitcast.46), calls=%async_computation | async-start | bytes 8388608 | tf_op jit(solution)/shard_map/all_to_all | solution.py:1332
  328.3 0.7 copy-start.8
  328.3 218.0 %reduce-scatter.8.cloned.1.call-start = ((), (), s32[]{:S(2)}) async-start(), calls=%async_computation.8 | async-start | bytes 2359296 | tf_op jit(solution)/shard_map/reduce_scatter | solution.py:1344
  328.9 250.7 %all-reduce.5.cloned.1.call-start = ((), (), s32[]{:S(2)}) async-start(), calls=%async_computation.9 | async-start | bytes 524288 | tf_op jit(solution)/shard_map/psum | solution.py:1379
  416.6 3.4 copy-start.3
  420.0 0.7 copy-start.9
  420.0 0.7 copy-start.10
  461.4 3.6 copy-start.4
  465.0 2.0 copy-start.5
  485.7 95.7 %copy-start.1 = (bf16[352,1024]{1,0:T(8,128)(2,1)S(1)}, bf16[352,1024]{1,0:T(8,128)(2,1)}, u32[]{:S(2)}) copy-start(bf16[352,1024]{1,0:T(8,128)(2,1)} %param.28) | copy-start | bytes 2162692
Sparse Core Ops, SparseCore 0:
  200.5 71.2 reduce-scatter.9
  275.7 63.7 reduce-scatter.11
  342.9 63.9 reduce-scatter.13
  410.2 65.7 reduce-scatter.5
  479.7 66.5 reduce-scatter.7
  548.6 30.9 all-reduce.4

commit v4 on v3

--- a/solution.py
+++ b/solution.py
@@ -276,9 +276,10 @@
     packed_ref,
     delta_ref,
     inverse_ref,
-    big_ref,
+    keep_big,
     update_ref,
     state_ref,
+    big_ref,
     mask_ref,
     fresh_ref,
     own_ref,
@@ -456,10 +457,10 @@
         for index, place in enumerate(places):
             inverse_ref[place] = inverses[index].astype(jnp.bfloat16)
             big_ref[place, 0:BT, :] = onward[index][:, :DK].astype(jnp.bfloat16)
-            big_ref[place, BT : 2 * BT, :] = solved[index][:, :DK].astype(jnp.bfloat16)
-            big_ref[place, 2 * BT : 3 * BT, :] = (
+            big_ref[place, BT : 2 * BT, :] = (
                 kept_values[index][3] - through[index][:, :DK]
             ).astype(jnp.bfloat16)
+            big_ref[place, 2 * BT : 3 * BT, :] = solved[index][:, :DK].astype(jnp.bfloat16)
             add_ref[place] = onward[index][:, DK:]
             fresh_ref[place] = solved[index][:, DK:]
             own_ref[place] = through[index][:, DK:]
@@ -478,8 +479,8 @@
             product = products[head]
             state_ref[place] = lows[head]
             following.append(states[head] * through - product[:BT] + add_ref[place])
-            update_ref[place] = (fresh_ref[place] - product[BT : 2 * BT]).astype(jnp.bfloat16)
-            delta = own_ref[place] + product[2 * BT :]
+            update_ref[place] = (fresh_ref[place] - product[2 * BT :]).astype(jnp.bfloat16)
+            delta = own_ref[place] + product[BT : 2 * BT]
             delta_ref[pl.ds(base, BT), head * DK : head * DK + DK] = delta
             inv = lax.rsqrt(jnp.mean(delta * delta, axis=1, keepdims=True) + EPS_NORM)
             ready_ref[pl.ds(base, BT), head * DK : head * DK + DK] = (
@@ -491,6 +492,10 @@
     lax.fori_loop(0, blocks, advance, (zero,) * heads)
 
     pieces[3].relay()
+    keep_parts = pltpu.make_async_copy(
+        big_ref.at[:, pl.ds(0, 2 * BT), :], keep_big, local_sems.at[11]
+    )
+    keep_parts.start()
 
     def hand_over(shift):
         target = (seq + shift) % n_seq
@@ -527,6 +532,7 @@
     swap.wait()
     keep_normed.wait()
     keep_mixer.wait()
+    keep_parts.wait()
     share_cot.finish()
     for piece in pieces[1:]:
         piece.finish()
@@ -570,13 +576,14 @@
             jax.ShapeDtypeStruct((HALO + tokens, width), low),
             jax.ShapeDtypeStruct((tokens, heads * DK), full),
             jax.ShapeDtypeStruct((count, BT, BT), low),
-            jax.ShapeDtypeStruct((count, 3 * BT, BT), low),
+            jax.ShapeDtypeStruct((count, 2 * BT, BT), low),
             jax.ShapeDtypeStruct((count, BT, BT), low),
             jax.ShapeDtypeStruct((count, BT, BT), low),
         ),
         in_specs=[spec(SMEM)] + [spec()] * 4 + [spec(ANY)] * 7,
-        out_specs=(spec(ANY),) * 8 + (spec(),) * 6,
+        out_specs=(spec(ANY),) * 8 + (spec(),) * 3 + (spec(ANY),) + (spec(),) * 2,
         scratch_shapes=[
+            pltpu.VMEM((count, 3 * BT, BT), low),
             pltpu.VMEM((7, BT, BT), full),
             pltpu.VMEM((count, BT, BT), full),
             pltpu.VMEM((count, BT, BT), full),
@@ -590,7 +597,7 @@
             pltpu.SemaphoreType.DMA((gathers,)),
             pltpu.SemaphoreType.DMA((shares,)),
             pltpu.SemaphoreType.DMA((shares,)),
-            pltpu.SemaphoreType.DMA((11,)),
+            pltpu.SemaphoreType.DMA((12,)),
         ],
         compiler_params=pltpu.CompilerParams(
             vmem_limit_bytes=60 << 20, collective_id=1, has_side_effects=True
@@ -599,13 +606,484 @@
     )(retain, column, row, taps, gain, normed, mixer, gate, up, down, out, cot)
 
 
+class Wire:
+    def __init__(self, send, recv):
+        self.send, self.recv, self.used = send, recv, 0
+
+    def copy(self, source, target, seq, fsdp):
+        index = self.used
+        self.used += 1
+        return pltpu.make_async_remote_copy(
+            src_ref=source,
+            dst_ref=target,
+            send_sem=self.send.at[index],
+            recv_sem=self.recv.at[index],
+            device_id=(seq, fsdp),
+            device_id_type=MESH,
+        )
+
+
+def ffn_copies(n_seq, parts):
+    chips = n_seq // 2
+    return parts * (2 + 4 * (chips - 1)) + parts * (n_seq - 1)
+
+
+def ffn_kernel(
+    n_seq,
+    n_fsdp,
+    tokens_ref,
+    mixed_ref,
+    out_ref,
+    gain_ref,
+    gate_in,
+    up_in,
+    down_in,
+    cot_in,
+    hidden_ref,
+    grad_hidden_ref,
+    heads_ref,
+    result_ref,
+    grad_gate_ref,
+    grad_up_ref,
+    grad_down_ref,
+    grad_out_ref,
+    grad_gain_ref,
+    gate_ref,
+    up_ref,
+    down_ref,
+    cot_ref,
+    second_ref,
+    second_t_ref,
+    active_t_ref,
+    lin_gate_ref,
+    lin_up_ref,
+    keep_ref,
+    give_ref,
+    from_mate_ref,
+    reduce_ref,
+    from_far_ref,
+    attn_ref,
+    mixed_grad_ref,
+    stage_ref,
+    send_sems,
+    recv_sems,
+    local_sems,
+):
+    own, model = tokens_ref.shape
+    group = own * n_seq
+    part = min(PB, own)
+    parts = own // part
+    chips = n_seq // 2
+    seq, fsdp = lax.axis_index("seq"), lax.axis_index("fsdp")
+    mate = seq + 1 - 2 * (seq % 2)
+    units = gate_ref.shape[1]
+    low = jnp.bfloat16
+
+    loads = [
+        pltpu.make_async_copy(source, target, local_sems.at[index])
+        for index, (source, target) in enumerate(
+            ((gate_in, gate_ref), (up_in, up_ref), (down_in, down_ref), (cot_in, cot_ref))
+        )
+    ]
+    for load in loads:
+        load.start()
+
+    wire = Wire(send_sems, recv_sems)
+
+    def far(step):
+        return (seq + n_seq - 2 * step) % n_seq
+
+    def rows(ref, shard, index):
+        return ref.at[pl.ds(aligned(shard * own + index * part, part), part)]
+
+    def local_rows(ref, index):
+        return ref.at[pl.ds(index * part, part)]
+
+    to_mate, across, passed, give_mate, give_far, reduced = {}, {}, {}, {}, {}, {}
+    for index in range(parts):
+        mine = rows(second_ref, seq, index)
+        to_mate[index] = wire.copy(mine, mine, mate, fsdp)
+        give_mate[index] = wire.copy(
+            local_rows(give_ref.at[0], index), local_rows(from_mate_ref.at[0], index), mate, fsdp
+        )
+        for step in range(1, chips):
+            across[step, index] = wire.copy(mine, mine, (seq + 2 * step) % n_seq, fsdp)
+            there = rows(second_ref, far(step), index)
+            passed[step, index] = wire.copy(there, there, mate, fsdp)
+            give_far[step, index] = wire.copy(
+                local_rows(give_ref.at[step], index),
+                local_rows(from_mate_ref.at[step], index),
+                mate,
+                fsdp,
+            )
+            reduced[step, index] = wire.copy(
+                local_rows(reduce_ref.at[step - 1], index),
+                local_rows(from_far_ref.at[step - 1], index),
+                far(step),
+                fsdp,
+            )
+
+    greet_near(n_seq)
+
+    for index in range(parts):
+        at = slice(index * part, index * part + part)
+        hidden = tokens_ref[at, :].astype(jnp.float32) + bdot(mixed_ref[at, :], out_ref[...])
+        hidden_ref[at, :] = hidden
+        inv = lax.rsqrt(jnp.mean(hidden * hidden, axis=1, keepdims=True) + EPS_NORM)
+        second_ref[pl.ds(aligned(seq * own + index * part, part), part), :] = (
+            hidden * inv * gain_ref[...]
+        ).astype(low)
+        for step in range(1, chips):
+            across[step, index].start()
+        to_mate[index].start()
+    for load in loads:
+        load.wait()
+
+    count = n_seq * parts
+
+    def block(number, carry):
+        near = number < 2 * parts
+        late = number - 2 * parts
+        step_at = late // (2 * parts) + 1
+        rest = late % (2 * parts)
+        far_at = (seq + 2 * n_seq - 2 * step_at) % n_seq
+        far_mate = far_at + 1 - 2 * (far_at % 2)
+        shard = jnp.where(
+            near,
+            jnp.where(number < parts, seq, mate),
+            jnp.where(rest % 2 == 0, far_mate, far_at),
+        )
+        index_at = jnp.where(near, number % parts, rest // 2)
+        base = aligned(shard * own + index_at * part, part)
+
+        for index in range(parts):
+
+            @pl.when(number == parts + index)
+            def _():
+                to_mate[index].wait_recv()
+
+            for step in range(1, chips):
+
+                @pl.when(number == 2 * parts * step + 2 * index)
+                def _():
+                    across[step, index].wait_recv()
+                    passed[step, index].start()
+                    passed[step, index].wait_recv()
+
+        second = second_ref[pl.ds(base, part), :]
+        second_t_ref[:, pl.ds(base, part)] = second.T
+        gate_lin = bdot(second, gate_ref[...])
+        up_lin = bdot(second, up_ref[...])
+        cot = cot_ref[pl.ds(base, part), :]
+        grad_active = bdot(cot, down_ref[...], NT)
+        gate_sig = sigmoid(gate_lin)
+        silu = gate_lin * gate_sig
+        active = (silu * up_lin).astype(low)
+        active_t_ref[:, pl.ds(base, part)] = active.T
+        grad_gate = (grad_active * up_lin * (gate_sig + silu * (1.0 - gate_sig))).astype(low)
+        grad_up = (grad_active * silu).astype(low)
+        lin_gate_ref[pl.ds(base, part), :] = grad_gate
+        lin_up_ref[pl.ds(base, part), :] = grad_up
+        grad_second = bdot(grad_gate, gate_ref[...], NT) + bdot(grad_up, up_ref[...], NT)
+        stage_ref[...] = grad_second
+        result_ref[pl.ds(base, part), :] = bdot(active, down_ref[...]).astype(low)
+
+        for index in range(parts):
+            at = slice(index * part, index * part + part)
+
+            @pl.when(number == index)
+            def _():
+                keep_ref[at, :] = stage_ref[...]
+
+            @pl.when(number == parts + index)
+            def _():
+                give_ref[0, at, :] = stage_ref[...].astype(low)
+                give_mate[index].start()
+
+            for step in range(1, chips):
+
+                @pl.when(number == 2 * parts * step + 2 * index)
+                def _():
+                    give_ref[step, at, :] = stage_ref[...].astype(low)
+                    give_far[step, index].start()
+
+                @pl.when(number == 2 * parts * step + 2 * index + 1)
+                def _():
+                    give_far[step, index].wait_recv()
+                    reduce_ref[step - 1, at, :] = (
+                        stage_ref[...] + from_mate_ref[step, at, :].astype(jnp.float32)
+                    ).astype(low)
+                    reduced[step, index].start()
+
+        return carry
+
+    lax.fori_loop(0, count, block, 0)
+
+    tile = 256
+
+    def down_tile(number, carry):
+        base = aligned(number * tile, tile)
+        grad_down_ref[:, pl.ds(base, tile)] = bdot(
+            active_t_ref[...], cot_ref[:, pl.ds(base, tile)]
+        ).astype(low)
+        return carry
+
+    lax.fori_loop(0, model // tile, down_tile, 0)
+
+    grad_gain_ref[...] = jnp.zeros(grad_gain_ref.shape, jnp.float32)
+    width = model // n_seq
+    handed = []
+    for index in range(parts):
+        at = slice(index * part, index * part + part)
+        give_mate[index].wait_recv()
+        total = keep_ref[at, :] + from_mate_ref[0, at, :].astype(jnp.float32)
+        for step in range(1, chips):
+            reduced[step, index].wait_recv()
+            total = total + from_far_ref[step - 1, at, :].astype(jnp.float32)
+        hidden = hidden_ref[at, :]
+        inv = lax.rsqrt(jnp.mean(hidden * hidden, axis=1, keepdims=True) + EPS_NORM)
+        unit = hidden * inv
+        grad_gain_ref[...] += jnp.sum(total * unit, axis=0, keepdims=True)
+        grad_unit = total * gain_ref[...]
+        grad_hidden = inv * (
+            grad_unit - unit * jnp.mean(grad_unit * unit, axis=1, keepdims=True)
+        ) + cot_ref[pl.ds(aligned(seq * own + index * part, part), part), :].astype(jnp.float32)
+        grad_hidden_ref[at, :] = grad_hidden
+        attn = grad_hidden.astype(low)
+        attn_ref[at, :] = attn
+        mixed_grad_ref[at, :] = bdot(attn, out_ref[...], NT).astype(low)
+        for shift in range(1, n_seq):
+            target = (seq + shift) % n_seq
+            copy = wire.copy(
+                mixed_grad_ref.at[at, pl.ds(aligned(target * width, width), width)],
+                rows(heads_ref, seq, index),
+                target,
+                fsdp,
+            )
+            copy.start()
+            handed.append(copy)
+        heads_ref[pl.ds(aligned(seq * own + index * part, part), part), :] = mixed_grad_ref[
+            at, pl.ds(aligned(seq * width, width), width)
+        ]
+
+    def wide_tile(number, carry):
+        base = aligned(number * tile, tile)
+        turned = second_t_ref[pl.ds(base, tile), :]
+        grad_gate_ref[pl.ds(base, tile), :] = bdot(turned, lin_gate_ref[...]).astype(low)
+        grad_up_ref[pl.ds(base, tile), :] = bdot(turned, lin_up_ref[...]).astype(low)
+        return carry
+
+    lax.fori_loop(0, model // tile, wide_tile, 0)
+    for base in range(0, model, tile):
+        grad_out_ref[base : base + tile, :] = bdot(
+            mixed_ref[:, base : base + tile], attn_ref[...], TN
+        ).astype(low)
+
+    for index in range(parts):
+        to_mate[index].wait_send()
+        give_mate[index].wait_send()
+        for step in range(1, chips):
+            across[step, index].wait_send()
+            passed[step, index].wait_send()
+            give_far[step, index].wait_send()
+            reduced[step, index].wait_send()
+    for copy in handed:
+        copy.wait()
+
+
+def greet_near(n_seq):
+    seq, fsdp = lax.axis_index("seq"), lax.axis_index("fsdp")
+    barrier = pltpu.get_barrier_semaphore()
+    for step in range(1, n_seq):
+        pl.semaphore_signal(
+            barrier, inc=1, device_id=((seq + step) % n_seq, fsdp), device_id_type=MESH
+        )
+    pl.semaphore_wait(barrier, n_seq - 1)
+
+
+def ffn_block(n_seq, n_fsdp, tokens, mixed, out, gain, gate, up, down, cot):
+    own, model = tokens.shape
+    group = own * n_seq
+    units = gate.shape[1]
+    chips = n_seq // 2
+    low, full = jnp.bfloat16, jnp.float32
+    part = min(PB, own)
+    copies = ffn_copies(n_seq, own // part)
+
+    def shape(dims, kind=low):
+        return jax.ShapeDtypeStruct(dims, kind)
+
+    return pl.pallas_call(
+        functools.partial(ffn_kernel, n_seq, n_fsdp),
+        out_shape=(
+            shape((own, model), full),
+            shape((own, model), full),
+            shape((group, model // n_seq)),
+            shape((group, model)),
+            shape((model, units)),
+            shape((model, units)),
+            shape((units, model)),
+            shape((model, model)),
+            shape((1, model), full),
+        ),
+        in_specs=[spec()] * 4 + [spec(ANY)] * 4,
+        out_specs=(spec(),) * 9,
+        scratch_shapes=[
+            pltpu.VMEM((model, units), low),
+            pltpu.VMEM((model, units), low),
+            pltpu.VMEM((units, model), low),
+            pltpu.VMEM((group, model), low),
+            pltpu.VMEM((group, model), low),
+            pltpu.VMEM((model, group), low),
+            pltpu.VMEM((units, group), low),
+            pltpu.VMEM((group, units), low),
+            pltpu.VMEM((group, units), low),
+            pltpu.VMEM((own, model), full),
+            pltpu.VMEM((chips, own, model), low),
+            pltpu.VMEM((chips, own, model), low),
+            pltpu.VMEM((chips - 1, own, model), low),
+            pltpu.VMEM((chips - 1, own, model), low),
+            pltpu.VMEM((own, model), low),
+            pltpu.VMEM((own, model), low),
+            pltpu.VMEM((part, model), full),
+            pltpu.SemaphoreType.DMA((copies,)),
+            pltpu.SemaphoreType.DMA((copies,)),
+            pltpu.SemaphoreType.DMA((4,)),
+        ],
+        compiler_params=pltpu.CompilerParams(
+            vmem_limit_bytes=63 << 20, collective_id=2, has_side_effects=True
+        ),
+        name="ffn",
+    )(tokens, mixed, out, gain, gate, up, down, cot)
+
+
+class Scatter:
+    outer = 4
+
+    @classmethod
+    def copies(cls, n_fsdp):
+        return cls.outer * (n_fsdp // cls.outer - 1) + cls.outer - 1
+
+    def __init__(self, n_fsdp, wire, block, own, first, second):
+        self.inner = n_fsdp // self.outer
+        me = lax.axis_index("fsdp")
+        seq = lax.axis_index("seq")
+        self.high, self.low = me // self.inner, me % self.inner
+        self.own, self.first, self.second = own, first, second
+        self.near, self.away = [], []
+        for hop in range(1, self.inner):
+            lower = (self.low + hop) % self.inner
+            for high in range(self.outer):
+                self.near.append(
+                    wire.copy(
+                        block(high * self.inner + lower),
+                        first.at[(hop - 1) * self.outer + high],
+                        seq,
+                        self.high * self.inner + lower,
+                    )
+                )
+        for step in range(1, self.outer):
+            higher = (self.high + step) % self.outer
+            self.away.append(
+                wire.copy(own(higher), second.at[step - 1], seq, higher * self.inner + self.low)
+            )
+
+    def start(self):
+        for copy in self.near:
+            copy.start()
+
+    def combine(self):
+        for copy in self.near:
+            copy.wait_recv()
+        for high in range(self.outer):
+            block = self.own(high)
+            total = block[...].astype(jnp.float32)
+            for hop in range(1, self.inner):
+                total = total + self.first[(hop - 1) * self.outer + high].astype(jnp.float32)
+            block[...] = total.astype(jnp.bfloat16)
+        for copy in self.away:
+            copy.start()
+
+    def total(self):
+        for copy in self.away:
+            copy.wait_recv()
+        total = self.own(self.high)[...].astype(jnp.float32)
+        for step in range(1, self.outer):
+            total = total + self.second[step - 1].astype(jnp.float32)
+        return total.astype(jnp.bfloat16)
+
+    def drain(self):
+        for copy in self.near + self.away:
+            copy.wait_send()
+
+
+CHUNK = 64
+
+
+class SeqSum:
+    def __init__(self, n_seq, wire, give, mine, from_mate, from_far):
+        self.chips = n_seq // 2
+        seq, fsdp = lax.axis_index("seq"), lax.axis_index("fsdp")
+        mate = seq + 1 - 2 * (seq % 2)
+        self.mine, self.from_mate, self.from_far = mine, from_mate, from_far
+        self.gives = [
+            wire.copy(give(step), from_mate.at[step], mate, fsdp) for step in range(self.chips)
+        ]
+        self.across = [
+            wire.copy(
+                mine(step),
+                from_far.at[step - 1],
+                (seq + n_seq - 2 * step) % n_seq,
+                fsdp,
+            )
+            for step in range(1, self.chips)
+        ]
+
+    def reduce(self, step):
+        self.gives[step].wait_recv()
+        mine = self.mine(step)
+
+        def add(number, carry):
+            at = pl.ds(aligned(number * CHUNK, CHUNK), CHUNK)
+            mine[at, :] = (
+                mine[at, :].astype(jnp.float32) + self.from_mate[step, at, :].astype(jnp.float32)
+            ).astype(jnp.bfloat16)
+            return carry
+
+        lax.fori_loop(0, mine.shape[0] // CHUNK, add, 0)
+        self.across[step - 1].start()
+
+    def arrive(self):
+        self.gives[0].wait_recv()
+        for copy in self.across:
+            copy.wait_recv()
+
+    def total(self, at):
+        total = self.mine(0)[at, :].astype(jnp.float32) + self.from_mate[0, at, :].astype(
+            jnp.float32
+        )
+        for step in range(1, self.chips):
+            total = total + self.from_far[step - 1, at, :].astype(jnp.float32)
+        return total
+
+    def drain(self):
+        for copy in self.gives + self.across:
+            copy.wait_send()
+
+
+def split_columns(width):
+    first = (width // DK + 1) // 2 * DK
+    return ((0, first), (first, width - first))
+
+
 def mixer_backward_kernel(
     heads,
+    n_seq,
+    n_fsdp,
     retain_ref,
     column_ref,
     row_ref,
     grad_ref,
-    packed_ref,
     taps_ref,
     gain_ref,
     delta_ref,
@@ -613,18 +1091,250 @@
     big_ref,
     update_ref,
     state_ref,
-    out_ref,
-    taps_out_ref,
-    gain_out_ref,
+    norm_gain_ref,
+    ffn_gain_ref,
+    packed_in,
+    normed_in,
+    weight_in,
+    tokens_in,
+    hidden_in,
+    grad_hidden_in,
+    result_in,
+    gate_in,
+    up_in,
+    down_in,
+    out_in,
+    result_out,
+    tokens_out,
+    gate_out,
+    up_out,
+    down_out,
+    out_out,
+    mixer_out,
+    small_out,
+    norm_out,
+    packed_ref,
     grad_delta_ref,
     add_ref,
     after_ref,
     conv_ref,
     grad_proj_ref,
+    arrived_ref,
+    weight_ref,
+    weight_grad_ref,
+    wide_ref,
+    tokens_ref,
+    result_ref,
+    result_mine,
+    result_mate,
+    result_far,
+    normed_mine,
+    normed_give,
+    normed_mate,
+    normed_far,
+    gate_own,
+    gate_first,
+    gate_second,
+    up_own,
+    up_first,
+    up_second,
+    down_own,
+    down_first,
+    down_second,
+    out_sum,
+    out_mate,
+    out_first,
+    out_second,
+    out_far,
+    mixer_first_a,
+    mixer_second_a,
+    mixer_first_b,
+    mixer_second_b,
+    gate_total,
+    up_total,
+    down_total,
+    out_total,
+    mixer_total,
+    small_ref,
+    small_all,
+    norm_ref,
+    norm_all,
+    send_sems,
+    recv_sems,
+    gather_send,
+    gather_recv,
+    share_send,
+    share_recv,
+    local_sems,
 ):
     tokens = grad_ref.shape[0]
     blocks = tokens // BT
     width = 3 * heads * DK
+    own = tokens // n_seq
+    model = tokens_ref.shape[1]
+    own_rows = gate_own.shape[1]
+    seq, fsdp = lax.axis_index("seq"), lax.axis_index("fsdp")
+    mate = seq + 1 - 2 * (seq % 2)
+    core = seq % 2
+    chip = seq // 2
+    chips = n_seq // 2
+    inner = n_fsdp // Scatter.outer
+    inner_low = fsdp % inner
+    low, full = jnp.bfloat16, jnp.float32
+
+    local = {}
+
+    def bring(name, source, target):
+        copy = pltpu.make_async_copy(source, target, local_sems.at[len(local)])
+        local[name] = copy
+        return copy
+
+    def far(step):
+        return (seq + n_seq - 2 * step) % n_seq
+
+    def far_mate(step):
+        there = far(step)
+        return there + 1 - 2 * (there % 2)
+
+    def shard(ref, index):
+        return ref.at[pl.ds(aligned(index * own, own), own)]
+
+    bring("packed", packed_in, packed_ref.at[:, pl.ds(0, packed_in.shape[1])]).start()
+    wire = Wire(send_sems, recv_sems)
+    result_sum = SeqSum(
+        n_seq,
+        wire,
+        lambda step: shard(result_in, mate if step == 0 else far_mate(step)),
+        lambda step: result_mine.at[step],
+        result_mate,
+        result_far,
+    )
+    normed_sum = SeqSum(
+        n_seq,
+        wire,
+        lambda step: normed_give.at[step],
+        lambda step: normed_mine.at[step],
+        normed_mate,
+        normed_far,
+    )
+    half = out_sum.shape[1]
+    out_rows = out_sum.shape[0] // n_fsdp
+    half_at = pl.ds(aligned(core * half, half), half)
+    out_give = wire.copy(
+        out_in.at[:, pl.ds(aligned((1 - core) * half, half), half)], out_mate, mate, fsdp
+    )
+
+    def rows_of(ref, size):
+        return lambda owner: ref.at[pl.ds(aligned(owner * size, size), size)]
+
+    def held(ref):
+        return lambda high: ref.at[high]
+
+    gate_sum = Scatter(
+        n_fsdp, wire, rows_of(gate_in, own_rows), held(gate_own), gate_first, gate_second
+    )
+    up_sum = Scatter(n_fsdp, wire, rows_of(up_in, own_rows), held(up_own), up_first, up_second)
+    down_sum = Scatter(
+        n_fsdp, wire, lambda owner: down_in.at[owner], held(down_own), down_first, down_second
+    )
+    out_scatter = Scatter(
+        n_fsdp,
+        wire,
+        rows_of(out_sum, out_rows),
+        lambda high: rows_of(out_sum, out_rows)(high * inner + inner_low),
+        out_first,
+        out_second,
+    )
+    spans = split_columns(width + DK)
+
+    def mixer_block(span):
+        return lambda owner: weight_grad_ref.at[
+            pl.ds(aligned(owner * own_rows, own_rows), own_rows), pl.ds(span[0], span[1])
+        ]
+
+    mixer_sums = [
+        Scatter(
+            n_fsdp,
+            wire,
+            mixer_block(span),
+            (lambda at: lambda high: at(high * inner + inner_low))(mixer_block(span)),
+            first,
+            second,
+        )
+        for span, first, second in (
+            (spans[0], mixer_first_a, mixer_second_a),
+            (spans[1], mixer_first_b, mixer_second_b),
+        )
+    ]
+    out_across = [
+        wire.copy(out_far.at[chip], out_far.at[chip], (seq + 2 * step) % n_seq, fsdp)
+        for step in range(1, chips)
+    ]
+    out_swap = wire.copy(out_total, out_out.at[:, half_at], mate, fsdp)
+
+    share_sems = (share_send, share_recv)
+    gather_sems = (gather_send, gather_recv)
+    per_share, per_gather = Share.copies(n_seq), Gather.copies(n_fsdp)
+
+    def share(index, source, ref):
+        return Share(
+            n_seq,
+            source,
+            lambda owner: ref.at[owner],
+            share_sems,
+            index * per_share,
+            local_sems.at[50 + index],
+        )
+
+    gate_share = share(0, gate_total, gate_out)
+    up_share = share(1, up_total, up_out)
+    down_share = share(2, down_total, down_out)
+    mixer_shares = [
+        Share(
+            n_seq,
+            mixer_total.at[:, pl.ds(span[0], span[1])],
+            (lambda place: lambda owner: mixer_out.at[owner, :, place])(pl.ds(span[0], span[1])),
+            share_sems,
+            (3 + index) * per_share,
+            local_sems.at[53 + index],
+        )
+        for index, span in enumerate(spans)
+    ]
+    small_share = share(5, small_ref, small_out)
+    norm_share = share(6, norm_ref, norm_out)
+    small_gather = Gather(
+        n_fsdp,
+        small_ref,
+        lambda owner: small_all.at[owner],
+        gather_sems,
+        0,
+        local_sems.at[57],
+    )
+    norm_gather = Gather(
+        n_fsdp,
+        norm_ref,
+        lambda owner: norm_all.at[owner],
+        gather_sems,
+        per_gather,
+        local_sems.at[58],
+    )
+
+    for high in range(Scatter.outer):
+        owner = high * inner + inner_low
+        bring(("gate", high), rows_of(gate_in, own_rows)(owner), gate_own.at[high]).start()
+        bring(("up", high), rows_of(up_in, own_rows)(owner), up_own.at[high]).start()
+        bring(("down", high), down_in.at[owner], down_own.at[high]).start()
+    bring("out", out_in.at[:, half_at], out_sum).start()
+    bring("result", shard(result_in, seq), result_mine.at[0]).start()
+    for step in range(1, chips):
+        bring(("result", step), shard(result_in, far(step)), result_mine.at[step]).start()
+    bring("hidden", hidden_in, wide_ref).start()
+
+    greet(n_seq, n_fsdp)
+    gate_sum.start()
+    for copy in result_sum.gives:
+        copy.start()
+    out_give.start()
 
     def head_norm(step, total):
         base = pl.multiple_of(step * PB, PB)
@@ -637,25 +1347,33 @@
             unit = delta * inv
             total = total + jnp.sum(grad * unit, axis=0, keepdims=True)
             grad_unit = grad * gain_ref[...]
-            low = (
+            shrunk = (
                 inv * (grad_unit - unit * jnp.mean(grad_unit * unit, axis=1, keepdims=True))
-            ).astype(jnp.bfloat16)
-            grad_delta_ref[pl.ds(base, PB), at] = low
+            ).astype(low)
+            grad_delta_ref[pl.ds(base, PB), at] = shrunk
             for sub in range(PB // BT):
                 place = head * blocks + step * (PB // BT) + sub
                 add_ref[place] = bdot(
-                    big_ref[place, 2 * BT : 3 * BT, :], low[sub * BT : sub * BT + BT], TN
-                )
+                    big_ref[place, BT : 2 * BT, :], shrunk[sub * BT : sub * BT + BT], TN
+                ).astype(low)
         return total
 
-    gain_out_ref[...] = lax.fori_loop(
-        0, tokens // PB, head_norm, jnp.zeros((1, DK), jnp.float32)
-    )
+    small_ref[...] = jnp.zeros(small_ref.shape, full)
+    small_ref[0:1, :] = ffn_gain_ref[...]
+    small_ref[1:2, 0:DK] = lax.fori_loop(0, tokens // PB, head_norm, jnp.zeros((1, DK), full))
+
+    for high in range(Scatter.outer):
+        local["gate", high].wait()
+    gate_sum.combine()
+    up_sum.start()
+    for step in range(1, chips):
+        local["result", step].wait()
+        result_sum.reduce(step)
 
     def retreat(step, grads):
         block = blocks - 1 - step
         through = retain_ref[2 * block] * retain_ref[2 * block + 1]
-        lows = [grad.astype(jnp.bfloat16) for grad in grads]
+        lows = [grad.astype(low) for grad in grads]
         following = []
         for head in range(heads):
             place = head * blocks + block
@@ -663,22 +1381,76 @@
             following.append(
                 grads[head] * through
                 - bdot(big_ref[place, 0:BT, :], lows[head], TN)
-                + add_ref[place]
+                + add_ref[place].astype(full)
             )
         return tuple(following)
 
-    zero = jnp.zeros((DK, DK), jnp.float32)
+    zero = jnp.zeros((DK, DK), full)
     lax.fori_loop(0, blocks, retreat, (zero,) * heads)
-
-    conv_ref[tokens : tokens + HALO, :] = jnp.zeros((HALO, width), jnp.float32)
-
-    def gradients(block, carry):
-        first, second = retain_ref[2 * block], retain_ref[2 * block + 1]
+    local["packed"].wait()
+
+    conv_ref[BT : BT + HALO, :] = jnp.zeros((HALO, width), full)
+
+    def up_stage():
+        for high in range(Scatter.outer):
+            local["up", high].wait()
+        up_sum.combine()
+        down_sum.start()
+        gate_total[...] = gate_sum.total()
+        gate_share.start()
+
+    def add_out():
+        local["out"].wait()
+        out_give.wait_recv()
+
+        def add(number, carry):
+            at = pl.ds(aligned(number * CHUNK, CHUNK), CHUNK)
+            out_sum[at, :] = (out_sum[at, :].astype(full) + out_mate[at, :].astype(full)).astype(
+                low
+            )
+            return carry
+
+        lax.fori_loop(0, out_sum.shape[0] // CHUNK, add, 0)
+
+    def down_stage():
+        for high in range(Scatter.outer):
+            local["down", high].wait()
+        down_sum.combine()
+        out_scatter.start()
+        gate_share.relay()
+        up_total[...] = up_sum.total()
+        up_share.start()
+
+    def result_stage():
+        local["hidden"].wait()
+        local["result"].wait()
+        result_sum.arrive()
+
+        def add(number, carry):
+            at = pl.ds(aligned(number * CHUNK, CHUNK), CHUNK)
+            result_ref[at, :] = (wide_ref[at, :] + result_sum.total(at)).astype(low)
+            return carry
+
+        lax.fori_loop(0, own // CHUNK, add, 0)
+
+    def gradients(step, carry):
+        for moment, stage in ((3, up_stage), (6, add_out), (10, down_stage), (13, result_stage)):
+
+            @pl.when(step == moment)
+            def _():
+                stage()
+
+        block = blocks - 1 - step
+        first, second, third = (
+            retain_ref[2 * block],
+            retain_ref[2 * block + 1],
+            retain_ref[2 * block + 2],
+        )
         base = pl.multiple_of(block * BT, BT)
-        masks = tap_masks(first, second, 1.0, BT)
+        masks = tap_masks(first, second, third, BT + HALO)
+        near_masks = [None] + [mask[:BT] for mask in masks[1:]]
         seen, kept = block_flags(first, second)
         rows, cols, cross = pair_mask(second)
-        _, _, _ = rows, cols, cross
         turned = jnp.where((rows < CH) & (cols >= CH), second, 1.0)
         lanes = iota((BT, BT), 1)
         strengths = sigmoid(
@@ -695,7 +1467,7 @@
                     taps_ref[kind * CONV + back : kind * CONV + back + 1, head * DK : head * DK + DK]
                     for back in range(CONV)
                 ]
-                conv = conv_of(window, taps, masks)
+                conv = conv_of(window, taps, near_masks)
                 gate = sigmoid(conv)
                 convs.append(conv)
                 gates.append(gate)
@@ -763,463 +1535,284 @@
             )
             for kind in range(3):
                 at = (kind * heads + head) * DK
-                conv_ref[pl.ds(base, BT), at : at + DK] = (
+                conv_ref[0:BT, at : at + DK] = (
                     scaled[kind] * gates[kind] * (1.0 + convs[kind] * (1.0 - gates[kind]))
                 )
         grad_proj_ref[pl.ds(base, BT), width : width + BT] = (
             grad_strengths * strengths * (1.0 - strengths)
         ).astype(jnp.bfloat16)
-        return carry
-
-    lax.fori_loop(0, blocks, gradients, 0)
-
-    taps_out_ref[...] = jnp.zeros(taps_out_ref.shape, jnp.float32)
-
-    def conv_back(block, carry):
-        first, second, third = (
-            retain_ref[2 * block],
-            retain_ref[2 * block + 1],
-            retain_ref[2 * block + 2],
-        )
-        base = pl.multiple_of(block * BT, BT)
-        masks = tap_masks(first, second, third, BT + HALO)
         for kind in range(3):
             for head in range(heads):
                 at = (kind * heads + head) * DK
-                grads = conv_ref[pl.ds(base, BT + HALO), at : at + DK]
+                span = slice(head * DK, head * DK + DK)
+                grads = conv_ref[:, at : at + DK]
                 window = packed_ref[pl.ds(base, HALO + BT), at : at + DK].astype(jnp.float32)
                 total = None
                 for back in range(CONV):
                     row = kind * CONV + back
-                    tap = taps_ref[row : row + 1, head * DK : head * DK + DK]
+                    tap = taps_ref[row : row + 1, span]
                     masked = grads if back == 0 else grads * masks[back]
                     shifted = (
                         masked if back == 0 else pltpu.roll(masked, BT + HALO - back, 0)
                     )[:BT]
                     total = shifted * tap if total is None else total + shifted * tap
                     past = (window if back == 0 else pltpu.roll(window, back, 0))[HALO:]
-                    taps_out_ref[row : row + 1, head * DK : head * DK + DK] += jnp.sum(
+                    small_ref[2 + row : 3 + row, span] += jnp.sum(
                         masked[:BT] * past, axis=0, keepdims=True
                     )
                 grad_proj_ref[pl.ds(base, BT), at : at + DK] = total.astype(jnp.bfloat16)
+        conv_ref[BT : BT + HALO, :] = conv_ref[0:HALO, :]
         return carry
 
-    lax.fori_loop(0, blocks, conv_back, 0)
-
-    def unpermute(step, carry):
-        base = pl.multiple_of(step * PB, PB)
-        out_ref[pl.ds(base, PB), :] = unpermute_rows(
-            row_ref[...], base, grad_proj_ref[...], tokens
-        ).astype(jnp.bfloat16)
-        return carry
-
-    lax.fori_loop(0, tokens // PB, unpermute, 0)
-
-
-def mixer_backward(retain, column, row, grad_mixed, taps, gain, saved):
-    packed, delta, inverse, big, update, state = saved
-    tokens = grad_mixed.shape[0]
+    lax.fori_loop(0, blocks, gradients, 0)
+
+    bring("keep_result", result_ref, result_out).start()
+    bring("normed", normed_in, packed_ref.at[pl.ds(0, tokens)]).start()
+    bring("weight", weight_in, weight_ref).start()
+    bring("grad_hidden", grad_hidden_in, wide_ref).start()
+    bring("tokens", tokens_in, tokens_ref).start()
+    out_scatter.combine()
+    small_gather.start()
+    up_share.relay()
+    down_total[...] = down_sum.total()
+    down_share.start()
+
+    def unpermute(index):
+        part = min(PB, own)
+
+        def step(number, carry):
+            base = aligned(index * own + number * part, part)
+            hot = jnp.where(row_ref[...] == iota((part, tokens), 0) + base, 1.0, 0.0).astype(low)
+            arrived_ref[pl.ds(base, part), :] = lax.dot_general(
+                hot, grad_proj_ref[...], NN, preferred_element_type=jnp.float32
+            ).astype(low)
+            return carry
+
+        lax.fori_loop(0, own // part, step, 0)
+
+    def push_back(index, target):
+        part = min(PB, own)
+
+        def step(number, carry):
+            base = aligned(index * own + number * part, part)
+            target[pl.ds(aligned(number * part, part), part), :] = bdot(
+                arrived_ref[pl.ds(base, part), :], weight_ref[...], NT
+            ).astype(low)
+            return carry
+
+        lax.fori_loop(0, own // part, step, 0)
+
+    waited = False
+    for step in range(1, chips):
+        unpermute(far_mate(step))
+        if not waited:
+            local["weight"].wait()
+            waited = True
+        push_back(far_mate(step), normed_give.at[step])
+        normed_sum.gives[step].start()
+        unpermute(far(step))
+        push_back(far(step), normed_mine.at[step])
+        normed_sum.reduce(step)
+    unpermute(mate)
+    unpermute(seq)
+    if not waited:
+        local["weight"].wait()
+    small_gather.relay()
+    local["normed"].wait()
+
+    def weight_grad(span):
+        def step(number, carry):
+            at = pl.ds(aligned(number * PB, PB), PB)
+            weight_grad_ref[at, pl.ds(span[0], span[1])] = bdot(
+                packed_ref[0:tokens, at], arrived_ref[:, pl.ds(span[0], span[1])], TN
+            ).astype(low)
+            return carry
+
+        lax.fori_loop(0, model // PB, step, 0)
+
+    weight_grad(spans[0])
+    mixer_sums[0].start()
+    weight_grad(spans[1])
+    mixer_sums[1].start()
+    push_back(mate, normed_give.at[0])
+    normed_sum.gives[0].start()
+    push_back(seq, normed_mine.at[0])
+
+    out_far[chip] = out_scatter.total()
+    for copy in out_across:
+        copy.start()
+    down_share.relay()
+    small_gather.finish()
+    total = small_all[0]
+    for owner in range(1, n_fsdp):
+        total = total + small_all[owner]
+    small_ref[...] = total
+    small_share.start()
+    mixer_sums[0].combine()
+    for copy in out_across:
+        copy.wait_recv()
+    total = out_far[0].astype(full)
+    for index in range(1, chips):
+        total = total + out_far[index].astype(full)
+    out_total[...] = total.astype(low)
+    out_swap.start()
+    bring("keep_out", out_total, out_out.at[:, half_at]).start()
+
+    local["grad_hidden"].wait()
+    local["tokens"].wait()
+    normed_sum.arrive()
+
+    def norm_back(number, total):
+        at = pl.ds(aligned(number * CHUNK, CHUNK), CHUNK)
+        values = tokens_ref[at, :].astype(full)
+        inv = lax.rsqrt(jnp.mean(values * values, axis=1, keepdims=True) + EPS_NORM)
+        unit = values * inv
+        grad = normed_sum.total(at)
+        grad_unit = grad * norm_gain_ref[...]
+        wide_ref[at, :] += inv * (
+            grad_unit - unit * jnp.mean(grad_unit * unit, axis=1, keepdims=True)
+        )
+        return total + jnp.sum(grad * unit, axis=0, keepdims=True)
+
+    norm_ref[...] = jnp.zeros(norm_ref.shape, full)
+    norm_ref[0:1, :] = lax.fori_loop(0, own // CHUNK, norm_back, jnp.zeros((1, model), full))
+    bring("keep_tokens", wide_ref, tokens_out).start()
+    norm_gather.start()
+    small_share.relay()
+    mixer_sums[1].combine()
+    norm_gather.relay()
+    mixer_total[:, spans[0][0] : spans[0][0] + spans[0][1]] = mixer_sums[0].total()
+    mixer_shares[0].start()
+    norm_gather.finish()
+    total = norm_all[0]
+    for owner in range(1, n_fsdp):
+        total = total + norm_all[owner]
+    norm_ref[...] = total
+    norm_share.start()
+    mixer_shares[0].relay()
+    norm_share.relay()
+    mixer_total[:, spans[1][0] : spans[1][0] + spans[1][1]] = mixer_sums[1].total()
+    mixer_shares[1].start()
+    mixer_shares[1].relay()
+    for each in [gate_share, up_share, down_share, small_share, norm_share] + mixer_shares:
+        each.finish()
+    for each in [gate_sum, up_sum, down_sum, out_scatter] + mixer_sums + [result_sum, normed_sum]:
+        each.drain()
+    for copy in out_across:
+        copy.wait_send()
+    out_give.wait_send()
+    out_swap.wait()
+    for name in ("keep_result", "keep_out", "keep_tokens"):
+        local[name].wait()
+
+
+def mixer_backward(n_seq, n_fsdp, small, saved, big):
+    (retain, column, row, grad_heads, taps, gain, norm_gain, ffn_gain) = small
+    packed, delta, inverse, parts, update, state = saved
+    normed, weight, own_tokens, hidden, grad_hidden, result, gate, up, down, out = big
+    tokens = grad_heads.shape[0]
     width = packed.shape[1]
     heads = taps.shape[1] // DK
     count = heads * (tokens // BT)
+    own, model = own_tokens.shape
+    units = gate.shape[1]
+    own_rows = gate.shape[0] // n_fsdp
+    slab = down.shape[1]
+    out_rows = out.shape[0] // n_fsdp
+    half = out.shape[1] // 2
+    chips = n_seq // 2
+    outer = Scatter.outer
+    near = outer * (n_fsdp // outer - 1)
     low, full = jnp.bfloat16, jnp.float32
-    return pl.pallas_call(
-        functools.partial(mixer_backward_kernel, heads),
-        out_shape=(
-            jax.ShapeDtypeStruct((tokens, width), low),
-            jax.ShapeDtypeStruct(taps.shape, full),
-            jax.ShapeDtypeStruct((1, DK), full),
-        ),
-        in_specs=[spec(SMEM)] + [spec()] * 11,
-        out_specs=(spec(),) * 3,
-        scratch_shapes=[
-            pltpu.VMEM((tokens, heads * DK), low),
-            pltpu.VMEM((count, BT, BT), full),
-            pltpu.VMEM((count, BT, BT), low),
-            pltpu.VMEM((tokens + HALO, 3 * heads * DK), full),
-            pltpu.VMEM((tokens, width), low),
-        ],
-        compiler_params=pltpu.CompilerParams(vmem_limit_bytes=56 << 20),
-        name="mixer_backward",
-    )(retain, column, row, grad_mixed, packed, taps, gain, delta, inverse, big, update, state)
-
-
-class Wire:
-    def __init__(self, send, recv):
-        self.send, self.recv, self.used = send, recv, 0
-
-    def copy(self, source, target, seq, fsdp):
-        index = self.used
-        self.used += 1
-        return pltpu.make_async_remote_copy(
-            src_ref=source,
-            dst_ref=target,
-            send_sem=self.send.at[index],
-            recv_sem=self.recv.at[index],
-            device_id=(seq, fsdp),
-            device_id_type=MESH,
-        )
-
-
-def ffn_copies(n_seq, parts):
-    chips = n_seq // 2
-    return parts * (2 + 4 * (chips - 1)) + parts * (n_seq - 1)
-
-
-def ffn_kernel(
-    n_seq,
-    n_fsdp,
-    tokens_ref,
-    mixed_ref,
-    out_ref,
-    gain_ref,
-    gate_in,
-    up_in,
-    down_in,
-    cot_in,
-    hidden_ref,
-    grad_hidden_ref,
-    heads_ref,
-    result_ref,
-    grad_gate_ref,
-    grad_up_ref,
-    grad_down_ref,
-    grad_out_ref,
-    grad_gain_ref,
-    gate_ref,
-    up_ref,
-    down_ref,
-    cot_ref,
-    second_ref,
-    second_t_ref,
-    active_t_ref,
-    lin_gate_ref,
-    lin_up_ref,
-    keep_ref,
-    give_ref,
-    from_mate_ref,
-    reduce_ref,
-    from_far_ref,
-    attn_ref,
-    mixed_grad_ref,
-    stage_ref,
-    send_sems,
-    recv_sems,
-    local_sems,
-):
-    own, model = tokens_ref.shape
-    group = own * n_seq
-    part = min(PB, own)
-    parts = own // part
-    chips = n_seq // 2
-    seq, fsdp = lax.axis_index("seq"), lax.axis_index("fsdp")
-    mate = seq + 1 - 2 * (seq % 2)
-    units = gate_ref.shape[1]
-    low = jnp.bfloat16
-
-    loads = [
-        pltpu.make_async_copy(source, target, local_sems.at[index])
-        for index, (source, target) in enumerate(
-            ((gate_in, gate_ref), (up_in, up_ref), (down_in, down_ref), (cot_in, cot_ref))
-        )
-    ]
-    for load in loads:
-        load.start()
-
-    wire = Wire(send_sems, recv_sems)
-
-    def far(step):
-        return (seq + n_seq - 2 * step) % n_seq
-
-    def rows(ref, shard, index):
-        return ref.at[pl.ds(aligned(shard * own + index * part, part), part)]
-
-    def local_rows(ref, index):
-        return ref.at[pl.ds(index * part, part)]
-
-    to_mate, across, passed, give_mate, give_far, reduced = {}, {}, {}, {}, {}, {}
-    for index in range(parts):
-        mine = rows(second_ref, seq, index)
-        to_mate[index] = wire.copy(mine, mine, mate, fsdp)
-        give_mate[index] = wire.copy(
-            local_rows(give_ref.at[0], index), local_rows(from_mate_ref.at[0], index), mate, fsdp
-        )
-        for step in range(1, chips):
-            across[step, index] = wire.copy(mine, mine, (seq + 2 * step) % n_seq, fsdp)
-            there = rows(second_ref, far(step), index)
-            passed[step, index] = wire.copy(there, there, mate, fsdp)
-            give_far[step, index] = wire.copy(
-                local_rows(give_ref.at[step], index),
-                local_rows(from_mate_ref.at[step], index),
-                mate,
-                fsdp,
-            )
-            reduced[step, index] = wire.copy(
-                local_rows(reduce_ref.at[step - 1], index),
-                local_rows(from_far_ref.at[step - 1], index),
-                far(step),
-                fsdp,
-            )
-
-    greet_near(n_seq)
-
-    for index in range(parts):
-        at = slice(index * part, index * part + part)
-        hidden = tokens_ref[at, :].astype(jnp.float32) + bdot(mixed_ref[at, :], out_ref[...])
-        hidden_ref[at, :] = hidden
-        inv = lax.rsqrt(jnp.mean(hidden * hidden, axis=1, keepdims=True) + EPS_NORM)
-        second_ref[pl.ds(aligned(seq * own + index * part, part), part), :] = (
-            hidden * inv * gain_ref[...]
-        ).astype(low)
-        for step in range(1, chips):
-            across[step, index].start()
-        to_mate[index].start()
-    for load in loads:
-        load.wait()
-
-    count = n_seq * parts
-
-    def block(number, carry):
-        near = number < 2 * parts
-        late = number - 2 * parts
-        step_at = late // (2 * parts) + 1
-        rest = late % (2 * parts)
-        far_at = (seq + 2 * n_seq - 2 * step_at) % n_seq
-        far_mate = far_at + 1 - 2 * (far_at % 2)
-        shard = jnp.where(
-            near,
-            jnp.where(number < parts, seq, mate),
-            jnp.where(rest % 2 == 0, far_mate, far_at),
-        )
-        index_at = jnp.where(near, number % parts, rest // 2)
-        base = aligned(shard * own + index_at * part, part)
-
-        for index in range(parts):
-
-            @pl.when(number == parts + index)
-            def _():
-                to_mate[index].wait_recv()
-
-            for step in range(1, chips):
-
-                @pl.when(number == 2 * parts * step + 2 * index)
-                def _():
-                    across[step, index].wait_recv()
-                    passed[step, index].start()
-                    passed[step, index].wait_recv()
-
-        second = second_ref[pl.ds(base, part), :]
-        second_t_ref[:, pl.ds(base, part)] = second.T
-        gate_lin = bdot(second, gate_ref[...])
-        up_lin = bdot(second, up_ref[...])
-        cot = cot_ref[pl.ds(base, part), :]
-        grad_active = bdot(cot, down_ref[...], NT)
-        gate_sig = sigmoid(gate_lin)
-        silu = gate_lin * gate_sig
-        active = (silu * up_lin).astype(low)
-        active_t_ref[:, pl.ds(base, part)] = active.T
-        grad_gate = (grad_active * up_lin * (gate_sig + silu * (1.0 - gate_sig))).astype(low)
-        grad_up = (grad_active * silu).astype(low)
-        lin_gate_ref[pl.ds(base, part), :] = grad_gate
-        lin_up_ref[pl.ds(base, part), :] = grad_up
-        grad_second = bdot(grad_gate, gate_ref[...], NT) + bdot(grad_up, up_ref[...], NT)
-        stage_ref[...] = grad_second
-        result_ref[pl.ds(base, part), :] = bdot(active, down_ref[...]).astype(low)
-
-        for index in range(parts):
-            at = slice(index * part, index * part + part)
-
-            @pl.when(number == index)
-            def _():
-                keep_ref[at, :] = stage_ref[...]
-
-            @pl.when(number == parts + index)
-            def _():
-                give_ref[0, at, :] = stage_ref[...].astype(low)
-                give_mate[index].start()
-
-            for step in range(1, chips):
-
-                @pl.when(number == 2 * parts * step + 2 * index)
-                def _():
-                    give_ref[step, at, :] = stage_ref[...].astype(low)
-                    give_far[step, index].start()
-
-                @pl.when(number == 2 * parts * step + 2 * index + 1)
-                def _():
-                    give_far[step, index].wait_recv()
-                    reduce_ref[step - 1, at, :] = (
-                        stage_ref[...] + from_mate_ref[step, at, :].astype(jnp.float32)
-                    ).astype(low)
-                    reduced[step, index].start()
-
-        return carry
-
-    lax.fori_loop(0, count, block, 0)
-
-    tile = 256
-
-    def down_tile(number, carry):
-        base = aligned(number * tile, tile)
-        grad_down_ref[:, pl.ds(base, tile)] = bdot(
-            active_t_ref[...], cot_ref[:, pl.ds(base, tile)]
-        ).astype(low)
-        return carry
-
-    lax.fori_loop(0, model // tile, down_tile, 0)
-
-    grad_gain_ref[...] = jnp.zeros(grad_gain_ref.shape, jnp.float32)
-    width = model // n_seq
-    handed = []
-    for index in range(parts):
-        at = slice(index * part, index * part + part)
-        give_mate[index].wait_recv()
-        total = keep_ref[at, :] + from_mate_ref[0, at, :].astype(jnp.float32)
-        for step in range(1, chips):
-            reduced[step, index].wait_recv()
-            total = total + from_far_ref[step - 1, at, :].astype(jnp.float32)
-        hidden = hidden_ref[at, :]
-        inv = lax.rsqrt(jnp.mean(hidden * hidden, axis=1, keepdims=True) + EPS_NORM)
-        unit = hidden * inv
-        grad_gain_ref[...] += jnp.sum(total * unit, axis=0, keepdims=True)
-        grad_unit = total * gain_ref[...]
-        grad_hidden = inv * (
-            grad_unit - unit * jnp.mean(grad_unit * unit, axis=1, keepdims=True)
-        ) + cot_ref[pl.ds(aligned(seq * own + index * part, part), part), :].astype(jnp.float32)
-        grad_hidden_ref[at, :] = grad_hidden
-        attn = grad_hidden.astype(low)
-        attn_ref[at, :] = attn
-        mixed_grad_ref[at, :] = bdot(attn, out_ref[...], NT).astype(low)
-        for shift in range(1, n_seq):
-            target = (seq + shift) % n_seq
-            copy = wire.copy(
-                mixed_grad_ref.at[at, pl.ds(aligned(target * width, width), width)],
-                rows(heads_ref, seq, index),
-                target,
-                fsdp,
-            )
-            copy.start()
-            handed.append(copy)
-        heads_ref[pl.ds(aligned(seq * own + index * part, part), part), :] = mixed_grad_ref[
-            at, pl.ds(aligned(seq * width, width), width)
-        ]
-
-    def wide_tile(number, carry):
-        base = aligned(number * tile, tile)
-        turned = second_t_ref[pl.ds(base, tile), :]
-        grad_gate_ref[pl.ds(base, tile), :] = bdot(turned, lin_gate_ref[...]).astype(low)
-        grad_up_ref[pl.ds(base, tile), :] = bdot(turned, lin_up_ref[...]).astype(low)
-        return carry
-
-    lax.fori_loop(0, model // tile, wide_tile, 0)
-    for base in range(0, model, tile):
-        grad_out_ref[base : base + tile, :] = bdot(
-            mixed_ref[:, base : base + tile], attn_ref[...], TN
-        ).astype(low)
-
-    for index in range(parts):
-        to_mate[index].wait_send()
-        give_mate[index].wait_send()
-        for step in range(1, chips):
-            across[step, index].wait_send()
-            passed[step, index].wait_send()
-            give_far[step, index].wait_send()
-            reduced[step, index].wait_send()
-    for copy in handed:
-        copy.wait()
-
-
-def greet_near(n_seq):
-    seq, fsdp = lax.axis_index("seq"), lax.axis_index("fsdp")
-    barrier = pltpu.get_barrier_semaphore()
-    for step in range(1, n_seq):
-        pl.semaphore_signal(
-            barrier, inc=1, device_id=((seq + step) % n_seq, fsdp), device_id_type=MESH
-        )
-    pl.semaphore_wait(barrier, n_seq - 1)
-
-
-def ffn_block(n_seq, n_fsdp, tokens, mixed, out, gain, gate, up, down, cot):
-    own, model = tokens.shape
-    group = own * n_seq
-    units = gate.shape[1]
-    chips = n_seq // 2
-    low, full = jnp.bfloat16, jnp.float32
-    part = min(PB, own)
-    copies = ffn_copies(n_seq, own // part)
+    spans = split_columns(width)
+    copies = 6 * Scatter.copies(n_fsdp) + 2 * (2 * chips - 1) + 2 + chips - 1
+    shares, gathers = 7 * Share.copies(n_seq), 2 * Gather.copies(n_fsdp)
 
     def shape(dims, kind=low):
         return jax.ShapeDtypeStruct(dims, kind)
 
+    def sum_buffers(rows, cols):
+        return [pltpu.VMEM((near, rows, cols), low), pltpu.VMEM((outer - 1, rows, cols), low)]
+
+    def block_buffers(rows, cols):
+        return [pltpu.VMEM((outer, rows, cols), low)] + sum_buffers(rows, cols)
+
     return pl.pallas_call(
-        functools.partial(ffn_kernel, n_seq, n_fsdp),
+        functools.partial(mixer_backward_kernel, heads, n_seq, n_fsdp),
         out_shape=(
+            shape((own, model)),
             shape((own, model), full),
-            shape((own, model), full),
-            shape((group, model // n_seq)),
-            shape((group, model)),
-            shape((model, units)),
-            shape((model, units)),
-            shape((units, model)),
-            shape((model, model)),
-            shape((1, model), full),
+            shape((n_seq, own_rows, units)),
+            shape((n_seq, own_rows, units)),
+            shape((n_seq, slab, model)),
+            shape((out_rows, 2 * half)),
+            shape((n_seq, own_rows, width)),
+            shape((n_seq, 16, model), full),
+            shape((n_seq, 8, model), full),
         ),
-        in_specs=[spec()] * 4 + [spec(ANY)] * 4,
-        out_specs=(spec(),) * 9,
+        in_specs=[spec(SMEM)] + [spec()] * 12 + [spec(ANY)] * 11,
+        out_specs=(spec(ANY),) * 9,
         scratch_shapes=[
-            pltpu.VMEM((model, units), low),
-            pltpu.VMEM((model, units), low),
-            pltpu.VMEM((units, model), low),
-            pltpu.VMEM((group, model), low),
-            pltpu.VMEM((group, model), low),
-            pltpu.VMEM((model, group), low),
-            pltpu.VMEM((units, group), low),
-            pltpu.VMEM((group, units), low),
-            pltpu.VMEM((group, units), low),
+            pltpu.VMEM((HALO + tokens, max(width, model)), low),
+            pltpu.VMEM((tokens, heads * DK), low),
+            pltpu.VMEM((count, BT, BT), low),
+            pltpu.VMEM((count, BT, BT), low),
+            pltpu.VMEM((BT + HALO, 3 * heads * DK), full),
+            pltpu.VMEM((tokens, width), low),
+            pltpu.VMEM((tokens, width), low),
+            pltpu.VMEM((model, width), low),
+            pltpu.VMEM((model, width), low),
             pltpu.VMEM((own, model), full),
+            pltpu.VMEM((own, model), low),
+            pltpu.VMEM((own, model), low),
             pltpu.VMEM((chips, own, model), low),
             pltpu.VMEM((chips, own, model), low),
             pltpu.VMEM((chips - 1, own, model), low),
+            pltpu.VMEM((chips, own, model), low),
+            pltpu.VMEM((chips, own, model), low),
+            pltpu.VMEM((chips, own, model), low),
             pltpu.VMEM((chips - 1, own, model), low),
-            pltpu.VMEM((own, model), low),
-            pltpu.VMEM((own, model), low),
-            pltpu.VMEM((part, model), full),
+            *block_buffers(own_rows, units),
+            *block_buffers(own_rows, units),
+            *block_buffers(slab, model),
+            pltpu.VMEM((out.shape[0], half), low),
+            pltpu.VMEM((out.shape[0], half), low),
+            *sum_buffers(out_rows, half),
+            pltpu.VMEM((chips, out_rows, half), low),
+            *sum_buffers(own_rows, spans[0][1]),
+            *sum_buffers(own_rows, spans[1][1]),
+            pltpu.VMEM((own_rows, units), low),
+            pltpu.VMEM((own_rows, units), low),
+            pltpu.VMEM((slab, model), low),
+            pltpu.VMEM((out_rows, half), low),
+            pltpu.VMEM((own_rows, width), low),
+            pltpu.VMEM((16, model), full),
+            pltpu.VMEM((n_fsdp, 16, model), full),
+            pltpu.VMEM((8, model), full),
+            pltpu.VMEM((n_fsdp, 8, model), full),
             pltpu.SemaphoreType.DMA((copies,)),
             pltpu.SemaphoreType.DMA((copies,)),
-            pltpu.SemaphoreType.DMA((4,)),
+            pltpu.SemaphoreType.DMA((gathers,)),
+            pltpu.SemaphoreType.DMA((gathers,)),
+            pltpu.SemaphoreType.DMA((shares,)),
+            pltpu.SemaphoreType.DMA((shares,)),
+            pltpu.SemaphoreType.DMA((60,)),
         ],
         compiler_params=pltpu.CompilerParams(
-            vmem_limit_bytes=63 << 20, collective_id=2, has_side_effects=True
+            vmem_limit_bytes=63 << 20, collective_id=3, has_side_effects=True
         ),
-        name="ffn",
-    )(tokens, mixed, out, gain, gate, up, down, cot)
-
-
-def matmul(first, second):
-    return lax.dot_general(first, second, NN, preferred_element_type=jnp.float32)
-
-
-def times_transposed(first, second):
-    return lax.dot_general(first, second, NT, preferred_element_type=jnp.float32)
-
-
-def contract_rows(first, second):
-    return lax.dot_general(first, second, TN, preferred_element_type=jnp.float32)
+        name="mixer_backward",
+    )(
+        retain, column, row, grad_heads, taps, gain, delta, inverse, parts, update, state,
+        norm_gain, ffn_gain, packed, normed, weight, own_tokens, hidden, grad_hidden, result,
+        gate, up, down, out,
+    )
 
 
 def rms_forward(values, gain):
     inv_rms = lax.rsqrt(jnp.mean(values * values, axis=-1, keepdims=True) + EPS_NORM)
     unit_rows = values * inv_rms
     return (unit_rows * gain, unit_rows, inv_rms)
-
-
-def rms_backward(grad_out, unit_rows, inv_rms, gain):
-    grad_gain = jnp.sum(grad_out * unit_rows, axis=0)
-    grad_unit = grad_out * gain
-    grad_in = inv_rms * (
-        grad_unit - unit_rows * jnp.mean(grad_unit * unit_rows, axis=-1, keepdims=True)
-    )
-    return (grad_in, grad_gain)
 
 
 def retains(lengths, tokens):
@@ -1264,9 +1857,6 @@
     units = slab * n_fsdp
     own_rows = w_query.shape[0]
 
-    def gather(array, axis_name, axis=0):
-        return lax.all_gather(array, axis_name, axis=axis, tiled=True)
-
     def pick_units(array):
         split = array.reshape(array.shape[0], n_fsdp, n_seq, slab)
         return lax.dynamic_index_in_dim(split, place, 2, keepdims=False).reshape(-1, units)
@@ -1326,37 +1916,36 @@
         full_down,
         cot_all,
     )
-    grad_ffn_gain = grad_ffn_gain[0]
-
-    def spread(partial):
-        pieces = lax.all_to_all(
-            partial.astype(jnp.bfloat16).reshape(n_seq, -1, model),
-            "seq",
-            split_axis=0,
-            concat_axis=0,
-            tiled=True,
-        )
-        return jnp.sum(pieces.astype(jnp.float32), axis=0)
-
-    result = (hidden + spread(result_part)).astype(jnp.bfloat16)
-
-    def scatter(array):
-        return lax.psum_scatter(
-            array.astype(jnp.bfloat16), "fsdp", scatter_dimension=0, tiled=True
-        )
-
-    part_gate, part_up, part_down, part_out = (
-        scatter(array) for array in (wide_gate, wide_up, wide_down, wide_out)
-    )
-    grad_proj, grad_taps, grad_gain = mixer_backward(
-        retain, column, row, grad_heads, taps, gain, saved
-    )
-    grad_normed = spread(times_transposed(grad_proj, w_mixer))
-    part_mixer = scatter(contract_rows(normed, grad_proj))
-    grad_inputs, grad_norm_gain = rms_backward(grad_normed, unit_one, inv_one, norm_gain)
-    grad_inputs = grad_inputs + grad_hidden
-
-    all_mixer = gather(part_mixer[None], "seq").astype(jnp.float32)
+    result, grad_inputs, part_gate, part_up, part_down, sum_out, part_mixer, small, norm_sum = (
+        mixer_backward(
+            n_seq,
+            n_fsdp,
+            (
+                retain,
+                column,
+                row,
+                grad_heads,
+                taps,
+                gain,
+                norm_gain.reshape(1, model),
+                grad_ffn_gain,
+            ),
+            saved,
+            (
+                normed,
+                w_mixer,
+                tokens,
+                hidden,
+                grad_hidden,
+                result_part,
+                wide_gate,
+                wide_up,
+                wide_down.reshape(n_fsdp, slab, model),
+                wide_out,
+            ),
+        )
+    )
+    all_mixer = part_mixer.astype(jnp.float32)
 
     def mixer_columns(start, size):
         return (
@@ -1366,22 +1955,24 @@
     sum_q, sum_k, sum_v = (mixer_columns(kind * width, width) for kind in range(3))
     sum_b = mixer_columns(3 * width, heads)
 
-    def all_units(part):
-        pieces = gather(part[None], "seq").astype(jnp.float32)
+    def all_units(pieces):
         return (
-            pieces.reshape(n_seq, own_rows, n_fsdp, slab)
+            pieces.astype(jnp.float32)
+            .reshape(n_seq, own_rows, n_fsdp, slab)
             .transpose(1, 2, 0, 3)
             .reshape(own_rows, hidden_units)
         )
 
     sum_gate, sum_up = all_units(part_gate), all_units(part_up)
-    sum_down = gather(part_down, "seq").astype(jnp.float32)
-    sum_out = lax.psum(part_out, "seq").astype(jnp.float32)
-    conv_full = lax.dynamic_update_slice_in_dim(
-        jnp.zeros_like(conv_taps), grad_taps.reshape(3, CONV, width), place * width, 2
-    )
-    norm_total, ffn_total, head_total, conv_total = lax.psum(
-        (grad_norm_gain, grad_ffn_gain, grad_gain[0], conv_full), ("seq", "fsdp")
+    sum_down = part_down.astype(jnp.float32).reshape(n_seq * slab, model)
+    sum_out = sum_out.astype(jnp.float32)
+    norm_total = jnp.sum(norm_sum[:, 0], axis=0)
+    ffn_total = jnp.sum(small[:, 0], axis=0)
+    head_total = jnp.sum(small[:, 1, :DK], axis=0)
+    conv_total = (
+        small[:, 2 : 2 + 3 * CONV, :width]
+        .transpose(1, 0, 2)
+        .reshape(3, CONV, n_seq * width)
     )
     return (
         result,

time: 591 us -> 370 us (0.63)
  waiting for transfers between devices: 150 us -> 0 us
  blocking collectives: 120 us -> 0 us
  Pallas kernels: 238 us -> 329 us
  matrix products: 17.3 us -> 0 us
  between operations: 14.7 us -> 0.82 us
  starting transfers between devices: 10.3 us -> 0 us
    pallas_call x1, Pallas kernels: 59.9 us -> 153 us  [mixer_backward(): pl.pallas_call(functools.partial(mixer_backward_kernel, heads, n_seq, n_f...]
    all_gather x4 -> x0, blocking collectives: 79.3 us -> none  [gather(): return lax.all_gather(array, axis_name, axis=axis, tiled=True)]
    reduce_scatter x5 -> x0, waiting for transfers between devices: 76.8 us -> none  [scatter(): lax.psum_scatter(array.astype(jnp.bfloat16), 'fsdp', scatter_dimension=0,...]
    psum x1 -> x0, blocking collectives: 40.7 us -> none  [local(): lax.psum((grad_norm_gain, grad_ffn_gain, grad_gain[0], conv_full), ('seq'...]
    all_to_all x2 -> x0, waiting for transfers between devices: 39 us -> none  [spread(): lax.all_to_all(partial.astype(jnp.bfloat16).reshape(n_seq, -1, model), 's...]
    psum x1 -> x0, waiting for transfers between devices: 32.5 us -> none  [local(): sum_out = lax.psum(part_out, 'seq').astype(jnp.float32)]
    dot_general x2 -> x0, matrix products: 17.3 us -> none  [the longest x1 9.14 us: contract_rows(): lax.dot_general(first, second, TN, preferred_element_type=jnp.float32)]
    all_to_all x2 -> x0, starting transfers between devices: 9.86 us -> none  [spread(): lax.all_to_all(partial.astype(jnp.bfloat16).reshape(n_seq, -1, model), 's...]
  transfers between devices with their start and end apart: 8 -> 0, of which waited for: 5 -> 0; matrix products, arithmetic and copies ran while one was open for 6% -> 0% of each run, Pallas kernels for 10% -> 0%
where the time goes in v4:
time: 370 us; the launch traced here: 369 us
  Pallas kernels  329 us (89%)
  local copies, waits for them, and re-layouts  25.8 us (7%)
  other arithmetic  12.9 us (3%)
    pallas_call x1, Pallas kernels, mixer_backward(): pl.pallas_call(functools.partial(mixer_backward_kernel, heads, n_seq, n_f...  153 us
    pallas_call x1, Pallas kernels, mixer_forward(): pl.pallas_call(functools.partial(mixer_forward_kernel, heads, n_seq, n_fs...  109 us
    pallas_call x1, Pallas kernels, ffn_block(): pl.pallas_call(functools.partial(ffn_kernel, n_seq, n_fsdp), out_shape=(s...  67.3 us
    unnamed x26, local copies, waits for them, and re-layouts  11.7 us

profile of v4, /device:TPU:0, one launch (start us, length us, event | category | flops | bytes accessed | tf_op | source)
XLA Modules:
  0.0 369.0 jit_solution(5535463809424794767)
XLA Ops:
  0.7 0.8 constant_dynamic-slice_fusion.3
  1.5 0.8 select_reduce_fusion
  2.9 1.5 fusion
  4.4 0.7 constant_dynamic-slice_fusion.7
  5.9 0.8 constant_dynamic-slice_fusion.6
  6.7 0.9 constant_dynamic-slice_fusion.4
  7.6 0.7 fusion.4.mixer_in
  8.3 0.7 constant_dynamic-slice_fusion.down_in
  9.3 1.5 copy.58
  10.9 0.8 copy.60.gate_in
  11.7 0.8 copy.61.up_in
  12.5 1.3 fusion.2.normed_in
  13.8 1.3 copy.62.column_ref
  15.1 109.5 %mixer_forward.1 = (bf16[512,1024]{1,0:T(8,128)(2,1)}, bf16[2048,1024]{1,0:T(8,128)(2,1)}, bf16[1024,896]{1,0:T(8,128)(2,1)}, bf16[1024,704]{1,0:T(8,128)(2,1)},...) custom-call(f32[34]{0:T(128)} %pad.8.retain_ref, ...), custom_call_target="tpu_custom_call" | custom-call | tf_op jit(solution)/shard_map/mixer_forward/pallas_call | solution.py:565
  124.6 67.3 %ffn.1 = (f32[512,1024]{1,0:T(8,128)}, f32[512,1024]{1,0:T(8,128)}, bf16[2048,256]{1,0:T(8,128)(2,1)}, bf16[2048,1024]{1,0:T(8,128)(2,1)}, bf16[1024,704]{1,0:T(...) custom-call(bf16[512,1024]{1,0:T(8,128)(2,1)} %tokens_in.1, ...), custom_call_target="tpu_custom_call" | custom-call | tf_op jit(solution)/shard_map/ffn/pallas_call | solution.py:916
  191.9 152.7 %mixer_backward.1 = (bf16[512,1024]{1,0:T(8,128)(2,1)}, f32[512,1024]{1,0:T(8,128)}, bf16[4,128,704]{2,1,0:T(8,128)(2,1)}, bf16[4,128,704]{2,1,0:T(8,128)(2,1)},...) custom-call(f32[34]{0:T(128)} %pad.8.retain_ref, ...), custom_call_target="tpu_custom_call" | custom-call | tf_op jit(solution)/shard_map/mixer_backward/pallas_call | solution.py:1740
  344.6 1.2 slice_reduce_fusion.2
  345.9 1.5 slice_reduce_fusion.1
  347.4 1.5 slice_reduce_fusion
  348.9 0.8 slice_bitcast_fusion.4
  350.4 1.8 convert_element_type.26
  352.2 1.4 copy.68
  353.7 1.5 copy.75
  355.3 1.4 copy.70
  356.8 1.5 copy.76
  358.4 2.4 bitcast_convert_fusion
  361.0 0.7 copy.66
  361.9 1.0 copy.74
  363.1 1.0 copy.73
  364.3 1.0 copy.72
  365.3 2.3 copy.80
  367.7 1.3 copy.81
  (35 shorter events, 3.6 us)
Async XLA Ops:
  0.6 7.6 %copy-start = (bf16[352,1024]{1,0:T(8,128)(2,1)S(1)}, bf16[352,1024]{1,0:T(8,128)(2,1)}, u32[]{:S(2)}) copy-start(bf16[352,1024]{1,0:T(8,128)(2,1)} %param.28) | copy-start | bytes 2162692
  0.7 8.3 %copy-start.5 = (bf16[128,2816]{1,0:T(8,128)(2,1)S(1)}, bf16[128,2816]{1,0:T(8,128)(2,1)}, u32[]{:S(2)}) copy-start(bf16[128,2816]{1,0:T(8,128)(2,1)} %param.26) | copy-start | bytes 2162692
  9.0 3.5 copy-start.2
  9.0 3.5 copy-start.7
  10.8 3.0 copy-start.6
  356.8 3.9 %copy-start.4 = (bf16[4,128,896]{2,1,0:T(8,128)(2,1)S(1)}, bf16[4,128,896]{2,1,0:T(8,128)(2,1)}, u32[]{:S(2)}) copy-start(bf16[4,128,896]{2,1,0:T(8,128)(2,1)} %get-tuple-element.72) | copy-start | bytes 2752516
  364.1 3.5 copy-start.3
  365.3 3.7 copy-start.1
